TPU v7x, 32 devices: a whole 2x2x4 slice. The times are simulated.
32 devices in a mesh: tm: 8 (over z, y), chan: 4 (over x, core).
Axes of the slice: x: 2, y: 2, z: 4, core: 2. Of those that a mesh axis runs over, the one named last changes fastest.
Arguments:
- series_value: bfloat16 [4096, 1024], P('tm', 'chan'), may hold values from -6 to 6
- series_gate: bfloat16 [4096, 1024], P('tm', 'chan'), may hold values from -6 to 6
- long_filter: bfloat16 [4096, 1024], P('tm', 'chan'), may hold values from -2 to 2
- step_table: float32 [200, 1024], P(None, 'chan'), may hold values from -3 to 3
- diffusion_step: int32 [1], replicated, may hold values from 0 to 199
- mask_embed: float32 [1024], P('chan'), may hold values from -3 to 3
- block_flags: int32 [64], P('tm'), may hold values 0 or 1
- skip_gain: float32 [1024], P('chan'), may hold values from 0.5 to 1.5
- norm_gain: float32 [1024], replicated, may hold values from 0.5 to 2
- w_gate: bfloat16 [1024, 2048], P(None, 'chan'), may hold values from -0.1875 to 0.1875
- w_up: bfloat16 [1024, 2048], P(None, 'chan'), may hold values from -0.1875 to 0.1875
- w_down: bfloat16 [2048, 1024], P('chan'), may hold values from -0.125 to 0.125
Outputs:
- layer_out: bfloat16 [4096, 1024], P('tm', 'chan')
All inputs are finite; a program needn't handle non-finite values. No bound on the sum of `block_flags` on one device may be relied on, other than what follows from the above.
Results may differ from a plain program's by a relative error of at most 0.014.
Values may be sent and summed in bfloat16 or wider, within the bound.
No kernel may reach another device: no remote copies, remote signals or barrier semaphores. Data moves between devices by JAX's collectives and lax.ppermute only.
A program may use at most 128 MiB of HBM per device.

v0:
```python
import math

import jax
import jax.numpy as jnp
import numpy as np
from jax import lax
from jax.experimental import pallas as pl
from jax.experimental.pallas import tpu as pltpu
from jax.sharding import PartitionSpec as P

FLAGBLK = 64
bf16 = jnp.bfloat16
f32 = jnp.float32


def split_table(table):
    high = table.astype(bf16)
    low = (table - high.astype(np.float64)).astype(bf16)
    return high, low


def block_tables(block):
    freq = np.concatenate([np.arange(0, block, 2), np.arange(1, block, 2)])
    time = np.arange(block)
    turn = np.pi * ((2 * freq[None, :] + 1) * time[:, None] % (4 * block)) / (2 * block)
    forward = np.concatenate([np.cos(turn), -np.sin(turn)], axis=1)
    turn = np.pi * ((2 * freq[:, None] + 1) * (block + time[None, :]) % (4 * block)) / (2 * block)
    inverse = np.concatenate([np.cos(turn), -np.sin(turn)], axis=0) / block
    return split_table(forward) + split_table(inverse)


def dot(left, right):
    return jnp.dot(left, right, preferred_element_type=f32)


def prepare_kernel(step_ref, flags_ref, value_ref, filter_ref, table_ref, mask_ref, out_ref):
    embed = table_ref[pl.ds(step_ref[0], 1), :]
    mask = mask_ref[...]
    parts = []
    for at in range(value_ref.shape[0] // FLAGBLK):
        rows = value_ref[at * FLAGBLK : (at + 1) * FLAGBLK, :].astype(f32)
        parts.append((rows + embed + flags_ref[at].astype(f32) * mask).astype(bf16))
    inputs = jnp.concatenate(parts, axis=0)
    shape = (out_ref.shape[0], out_ref.shape[2], out_ref.shape[3])
    out_ref[:, 0] = inputs.T.reshape(shape)
    out_ref[:, 1] = filter_ref[...].T.reshape(shape)


def convolve_kernel(
    both_ref, fh_ref, fl_ref, gh_ref, gl_ref, skip_ref, out_ref, x_ref, h_ref, z_ref
):
    tm, _, chans, rows = both_ref.shape
    block = rows // 2
    half = block // 2
    nb = 2 * tm
    for which, dst in ((0, x_ref), (1, h_ref)):
        for part in range(2):
            data = both_ref[:, which, :, part * block : (part + 1) * block]
            data = data.reshape(tm * chans, block)
            spec = dot(data, fh_ref[...]) + dot(data, fl_ref[...])
            dst[:, part] = spec.reshape(tm, chans, 2 * block)

    def read(ref, at, sub, lanes):
        return ref[at // 2, at % 2, sub, lanes]

    def windows(at, sub, odd):
        re = slice(odd * half, (odd + 1) * half)
        im = slice(block + odd * half, block + (odd + 1) * half)
        return re, im

    def tile(step, carry):
        sub = pl.ds(pl.multiple_of(step * 8, 8), 8)
        for odd in range(2):
            for low in range(0, half, 128):
                width = min(128, half)
                re = slice(odd * half + low, odd * half + low + width)
                im = slice(block + odd * half + low, block + odd * half + low + width)
                if nb <= 16:
                    hr, hi = [], []
                    for d in range(nb):
                        cur_re, cur_im = read(h_ref, d, sub, re), read(h_ref, d, sub, im)
                        if d == 0:
                            wr, wi = (-cur_im, cur_re) if odd else (cur_im, -cur_re)
                        elif odd:
                            wr, wi = prev_re - cur_im, prev_im + cur_re
                        else:
                            wr, wi = prev_re + cur_im, prev_im - cur_re
                        prev_re, prev_im = cur_re, cur_im
                        hr.append(wr)
                        hi.append(wi)
                    for a in range(nb):
                        zr, zi = None, None
                        for d in range(a + 1):
                            xr, xi = read(x_ref, a - d, sub, re), read(x_ref, a - d, sub, im)
                            tr = xr * hr[d] - xi * hi[d]
                            ti = xr * hi[d] + xi * hr[d]
                            zr, zi = (tr, ti) if zr is None else (zr + tr, zi + ti)
                        z_ref[a // 2, a % 2, sub, re] = zr
                        z_ref[a // 2, a % 2, sub, im] = zi
                else:

                    def out_block(a, carry):
                        def pair(d, acc):
                            before = jnp.maximum(d - 1, 0)
                            keep = (d > 0).astype(f32)
                            pr = keep * read(h_ref, before, sub, re)
                            pi = keep * read(h_ref, before, sub, im)
                            cr, ci = read(h_ref, d, sub, re), read(h_ref, d, sub, im)
                            wr, wi = (pr - ci, pi + cr) if odd else (pr + ci, pi - cr)
                            xr, xi = read(x_ref, a - d, sub, re), read(x_ref, a - d, sub, im)
                            return (
                                acc[0] + xr * wr - xi * wi,
                                acc[1] + xr * wi + xi * wr,
                            )

                        zero = jnp.zeros((8, width), f32)
                        zr, zi = lax.fori_loop(0, a + 1, pair, (zero, zero))
                        z_ref[a // 2, a % 2, sub, re] = zr
                        z_ref[a // 2, a % 2, sub, im] = zi
                        return carry

                    lax.fori_loop(0, nb, out_block, 0)
        return carry

    lax.fori_loop(0, chans // 8, tile, 0)
    skip = skip_ref[...]
    for part in range(2):
        spec = z_ref[:, part].reshape(tm * chans, 2 * block)
        high = spec.astype(bf16)
        low = (spec - high.astype(f32)).astype(bf16)
        conv = dot(high, gh_ref[...]) + dot(low, gh_ref[...]) + dot(high, gl_ref[...])
        inputs = both_ref[:, 0, :, part * block : (part + 1) * block].astype(f32)
        total = (conv.reshape(tm, chans, block) + skip[None] * inputs).astype(bf16)
        out_ref[:, 0, part] = total
        out_ref[:, 1, part] = total


def feed_forward_kernel(
    chan_ref,
    conv_ref,
    gate0_ref,
    gate1_ref,
    gate2_ref,
    gate3_ref,
    gain_ref,
    wg0_ref,
    wu0_ref,
    wd0_ref,
    wg1_ref,
    wu1_ref,
    wd1_ref,
    out0_ref,
    out1_ref,
    out2_ref,
    out3_ref,
    mixed_ref,
    normed_ref,
):
    here = chan_ref[0]
    rows, width = gate0_ref.shape
    total = gain_ref.shape[0] * width
    square = jnp.zeros((rows, 1), f32)
    for j, gate_ref in enumerate((gate0_ref, gate1_ref, gate2_ref, gate3_ref)):
        conv = conv_ref[here ^ j].T.astype(f32)
        mixed = (gate_ref[...].astype(f32) * conv).astype(bf16)
        mixed_ref[j] = mixed
        wide = mixed.astype(f32)
        square = square + jnp.sum(wide * wide, axis=-1, keepdims=True)
    scale = lax.rsqrt(square / total + 1e-06)
    for j in range(4):
        at = here ^ j
        normed = (mixed_ref[j].astype(f32) * scale * gain_ref[at]).astype(bf16)
        normed_ref[:, pl.ds(pl.multiple_of(at * width, width), width)] = normed
    normed = normed_ref[...]
    hidden = []
    for wg_ref, wu_ref in ((wg0_ref, wu0_ref), (wg1_ref, wu1_ref)):
        gate = dot(normed, wg_ref[...])
        up = dot(normed, wu_ref[...])
        hidden.append((gate / (1.0 + jnp.exp(-gate)) * up).astype(bf16))
    for j, out_ref in ((2, out2_ref), (3, out3_ref), (1, out1_ref), (0, out0_ref)):
        cols = pl.ds(pl.multiple_of((here ^ j) * width, width), width)
        part = dot(hidden[0], wd0_ref[:, cols]) + dot(hidden[1], wd1_ref[:, cols])
        if j < 2:
            part = part + mixed_ref[j].astype(f32)
        out_ref[...] = part.astype(bf16)


VMEM = pltpu.MemorySpace.VMEM
SMEM = pltpu.MemorySpace.SMEM


def whole(space=VMEM):
    return pl.BlockSpec(memory_space=space)


def params(mib):
    return pltpu.CompilerParams(vmem_limit_bytes=mib << 20)


def shards(
    series_value,
    series_gate,
    long_filter,
    step_table,
    diffusion_step,
    mask_embed,
    block_flags,
    skip_gain,
    norm_gain,
    w_gate,
    w_up,
    w_down,
):
    tm = lax.axis_size("tm")
    chan = lax.axis_size("chan")
    here = lax.axis_index("chan")
    rows, width = series_value.shape
    own = width // tm
    block = rows // 2
    core = here % 2

    def swap(values, bits):
        return lax.ppermute(values, "chan", [(at, at ^ bits) for at in range(chan)])

    direct = own % 16 == 0
    made = pl.pallas_call(
        prepare_kernel,
        out_shape=jax.ShapeDtypeStruct(
            (tm, 2, own, rows) if direct else (1, 2, width, rows), bf16
        ),
        in_specs=[whole(SMEM), whole(SMEM)] + [whole()] * 4,
        out_specs=whole(),
        compiler_params=params(32),
        name="prepare",
    )(
        diffusion_step,
        block_flags,
        series_value,
        long_filter,
        step_table,
        mask_embed.reshape(1, width),
    )
    if not direct:
        made = made.reshape(2, tm, own, rows).transpose(1, 0, 2, 3)
    both = lax.all_to_all(made, "tm", split_axis=0, concat_axis=0, tiled=True)

    gate_own = lax.dynamic_slice_in_dim(series_gate, core * block, block, 0)
    gate_other = lax.dynamic_slice_in_dim(series_gate, (1 - core) * block, block, 0)
    gates = (gate_own, swap(gate_other, 1), swap(gate_own, 2), swap(gate_other, 3))
    wg1, wu1, wd1 = swap(w_gate, 1), swap(w_up, 1), swap(w_down, 1)

    skip = lax.dynamic_slice_in_dim(skip_gain, lax.axis_index("tm") * own, own, 0)
    skip = skip.reshape(own, 1)
    held = own
    if not direct:
        held = -(-own // 16) * 16
        both = jnp.pad(both, ((0, 0), (0, 0), (0, held - own), (0, 0)))
        skip = jnp.pad(skip, ((0, held - own), (0, 0)))
    tables = [jnp.asarray(table) for table in block_tables(block)]
    conv = pl.pallas_call(
        convolve_kernel,
        out_shape=jax.ShapeDtypeStruct((tm, 2, 2, held, block), bf16),
        in_specs=[whole()] * 6,
        out_specs=whole(),
        scratch_shapes=[pltpu.VMEM((tm, 2, held, 2 * block), f32)] * 3,
        compiler_params=params(48),
        name="convolve",
    )(both, *tables, skip)
    if not direct:
        conv = conv[:, :, :, :own]
    conv = lax.all_to_all(
        conv.reshape(tm * chan, own, block), ("tm", "chan"), split_axis=0, concat_axis=0, tiled=True
    )
    conv = conv.reshape(tm, chan, own, block).transpose(1, 0, 2, 3).reshape(chan, width, block)

    outs = pl.pallas_call(
        feed_forward_kernel,
        out_shape=[jax.ShapeDtypeStruct((block, width), bf16)] * 4,
        in_specs=[whole(SMEM)] + [whole()] * 12,
        out_specs=[whole()] * 4,
        scratch_shapes=[
            pltpu.VMEM((4, block, width), bf16),
            pltpu.VMEM((block, 4 * width), bf16),
        ],
        compiler_params=params(48),
        name="feed_forward",
    )(
        here.reshape(1).astype(jnp.int32),
        conv,
        *gates,
        norm_gain.reshape(chan, 1, width),
        w_gate,
        w_up,
        w_down,
        wg1,
        wu1,
        wd1,
    )
    same = outs[0].astype(f32) + swap(outs[2], 2).astype(f32)
    other = swap(outs[1], 1).astype(f32) + swap(outs[3], 3).astype(f32)
    first = jnp.where(core == 0, same, other).astype(bf16)
    second = jnp.where(core == 0, other, same).astype(bf16)
    return jnp.concatenate([first, second], axis=0)


def solution(mesh):
    placed = (
        P("tm", "chan"),
        P("tm", "chan"),
        P("tm", "chan"),
        P(None, "chan"),
        P(),
        P("chan"),
        P("tm"),
        P("chan"),
        P(),
        P(None, "chan"),
        P(None, "chan"),
        P("chan", None),
    )
    return jax.shard_map(
        shards, mesh=mesh, in_specs=placed, out_specs=P("tm", "chan"), check_vma=False
    )
```

profile of v0, /device:TPU:0, one launch (start us, length us, event | category | flops | bytes accessed | tf_op | source)
XLA Modules:
  0.0 70.5 jit_solution(1454792443253704107)
XLA Ops:
  0.0 0.0 copy-start
  0.7 0.7 copy-done.13
  1.3 0.0 copy-done.14
  1.4 0.9 %copy-done.4 = bf16[512,256]{1,0:T(8,128)(2,1)S(1)} copy-done((bf16[512,256]{1,0:T(8,128)(2,1)S(1)}, bf16[512,256]{1,0:T(8,128)(2,1)}, u32[]{:S(2)}) %copy-start.4) | copy-done | bytes 262168
  2.3 0.9 %copy-done.5 = bf16[512,256]{1,0:T(8,128)(2,1)S(1)} copy-done((bf16[512,256]{1,0:T(8,128)(2,1)S(1)}, bf16[512,256]{1,0:T(8,128)(2,1)}, u32[]{:S(2)}) %copy-start.5) | copy-done | bytes 262168
  3.3 0.9 %copy-done.10 = f32[200,256]{1,0:T(8,128)S(1)} copy-done((f32[200,256]{1,0:T(8,128)S(1)}, f32[200,256]{1,0:T(8,128)}, u32[]{:S(2)}) %copy-start.10) | copy-done | bytes 204824
  4.2 1.6 %prepare.1 = bf16[8,2,32,512]{3,2,1,0:T(8,128)(2,1)} custom-call(s32[1]{0:T(128)S(6)} %copy.20.step_ref, s32[8]{0:T(128)S(1)} %copy-done.14, bf16[512,256]{1,0:T(8,128)(2,1)S(1)} %copy-done.4, bf16[512,256]{1,0:T(8,128)(2,1)S(1)} %copy-done.5, f32[200,256]{1,0:T(8,128)S(1)} %copy-done.10, f32[1,256]{1,0:T(1,128)S(1)} %bitcast.12), custom_call_target="tpu_custom_call" | custom-call | tf_op jit(solution)/shard_map/prepare/pallas_call | solution.py:226
  5.7 7.3 %all-to-all-start = ((bf16[8,2,32,512]{3,2,1,0:T(8,128)(2,1)}), bf16[8,2,32,512]{3,2,1,0:T(8,128)(2,1)S(1)}, u32[]{:S(2)}, u32[]{:S(2)}) async-start(bf16[8,2,32,512]{3,2,1,0:T(8,128)(2,1)} %prepare.1), calls=%async_computation | async-start | bytes 1048576 | tf_op jit(solution)/shard_map/all_to_all | solution.py:245
  13.0 0.0 copy-done.1
  13.0 0.1 collective-permute-start.3
  13.1 0.5 collective-permute-start.4
  13.6 0.1 collective-permute-start.5
  13.7 0.0 copy-done
  13.7 0.1 dynamic-slice_bitcast_fusion
  13.8 0.1 copy.18.skip_ref
  13.9 13.6 %all-to-all-done.both_ref = bf16[8,2,32,512]{3,2,1,0:T(8,128)(2,1)S(1)} async-done(((bf16[8,2,32,512]{3,2,1,0:T(8,128)(2,1)}), bf16[8,2,32,512]{3,2,1,0:T(8,128)(2,1)S(1)}, u32[]{:S(2)}, u32[]{:S(2)}) %all-to-all-start) | async-done | bytes 524320 | tf_op jit(solution)/shard_map/all_to_all | solution.py:245
  27.5 0.9 %copy-done.6 = bf16[512,256]{1,0:T(8,128)(2,1)S(1)} copy-done((bf16[512,256]{1,0:T(8,128)(2,1)S(1)}, bf16[512,256]{1,0:T(8,128)(2,1)}, u32[]{:S(2)}) %copy-start.6) | copy-done | bytes 262168
  28.5 0.9 %copy-done.7 = bf16[512,256]{1,0:T(8,128)(2,1)S(1)} copy-done((bf16[512,256]{1,0:T(8,128)(2,1)S(1)}, bf16[512,256]{1,0:T(8,128)(2,1)}, u32[]{:S(2)}) %copy-start.7) | copy-done | bytes 262168
  29.4 0.9 %copy-done.8 = bf16[256,512]{1,0:T(8,128)(2,1)S(1)} copy-done((bf16[256,512]{1,0:T(8,128)(2,1)S(1)}, bf16[256,512]{1,0:T(8,128)(2,1)}, u32[]{:S(2)}) %copy-start.8) | copy-done | bytes 262168
  30.4 0.9 %copy-done.9 = bf16[256,512]{1,0:T(8,128)(2,1)S(1)} copy-done((bf16[256,512]{1,0:T(8,128)(2,1)S(1)}, bf16[256,512]{1,0:T(8,128)(2,1)}, u32[]{:S(2)}) %copy-start.9) | copy-done | bytes 262168
  31.3 3.4 %convolve.1 = bf16[8,2,2,32,256]{4,3,2,1,0:T(8,128)(2,1)} custom-call(bf16[8,2,32,512]{3,2,1,0:T(8,128)(2,1)S(1)} %all-to-all-done.both_ref, bf16[256,512]{1,0:T(8,128)(2,1)S(1)} %copy-done.9, bf16[256,512]{1,0:T(8,128)(2,1)S(1)} %copy-done.8, bf16[512,256]{1,0:T(8,128)(2,1)S(1)} %copy-done.7, bf16[512,256]{1,0:T(8,128)(2,1)S(1)} %copy-done.6, ...), custom_call_target="tpu_custom_call" | custom-call | tf_op jit(solution)/shard_map/convolve/pallas_call | solution.py:260
  34.7 3.8 %all-to-all-start.1 = ((bf16[32,32,256]{2,1,0:T(8,128)(2,1)}), bf16[32,32,256]{2,1,0:T(8,128)(2,1)}, u32[]{:S(2)}, u32[]{:S(2)}) async-start(bf16[32,32,256]{2,1,0:T(8,128)(2,1)} %bitcast.3), calls=%async_computation.1 | async-start | bytes 1048576 | tf_op jit(solution)/shard_map/all_to_all | solution.py:271
  38.5 0.0 copy-start.3
  38.5 0.7 constant_dynamic-slice_fusion
  39.2 1.4 %collective-permute-start.2 = (bf16[256,256]{1,0:T(8,128)(2,1)}, bf16[256,256]{1,0:T(8,128)(2,1)S(1)}, u32[]{:S(2)}, u32[]{:S(2)}) collective-permute-start(bf16[256,256]{1,0:T(8,128)(2,1)} %get-tuple-element.15), channel_id=1, source_target_pairs={{0,3},{1,2},{2,1},{3,0},{4,7},{5,6},{6,5},{7,4},{8,11},{9,10},{10,... | collective-permute-start | bytes 393224 | tf_op jit(solution)/shard_map/ppermute | solution.py:223
  40.6 0.4 collective-permute-start
  41.0 7.0 %collective-permute-done.2.gate3_ref = bf16[256,256]{1,0:T(8,128)(2,1)S(1)} collective-permute-done((bf16[256,256]{1,0:T(8,128)(2,1)}, bf16[256,256]{1,0:T(8,128)(2,1)S(1)}, u32[]{:S(2)}, u32[]{:S(2)}) %collective-permute-start.2) | collective-permute-done | bytes 131104 | tf_op jit(solution)/shard_map/ppermute | solution.py:223
  48.0 0.9 %collective-permute-start.1 = (bf16[256,256]{1,0:T(8,128)(2,1)S(1)}, bf16[256,256]{1,0:T(8,128)(2,1)}, u32[]{:S(2)}, u32[]{:S(2)}) collective-permute-start(bf16[256,256]{1,0:T(8,128)(2,1)S(1)} %get-tuple-element.16.gate0_ref), channel_id=1, source_target_pairs={{0,2},{1,3},{2,0},{3,1},{4,6},{5,7},{6,4},{7,5},{8,10},{9,11},{10,... | collective-permute-start | bytes 393224 | tf_op jit(solution)/shard_map/ppermute | solution.py:223
  48.9 5.1 %all-to-all-done.1 = bf16[32,32,256]{2,1,0:T(8,128)(2,1)} async-done(((bf16[32,32,256]{2,1,0:T(8,128)(2,1)}), bf16[32,32,256]{2,1,0:T(8,128)(2,1)}, u32[]{:S(2)}, u32[]{:S(2)}) %all-to-all-start.1) | async-done | bytes 524320 | tf_op jit(solution)/shard_map/all_to_all | solution.py:271
  54.0 1.1 %copy.19 = bf16[4,8,32,256]{3,2,1,0:T(8,128)(2,1)S(1)} copy(bf16[4,8,32,256]{3,2,0,1:T(8,128)(2,1)} %bitcast.5) | data formatting | bytes 1048576 | tf_op jit(solution)/shard_map/transpose | solution.py:274
  55.1 0.0 copy-start.12
  55.1 0.0 collective-permute-done.gate1_ref
  55.1 0.0 collective-permute-done.1.gate2_ref
  55.1 0.0 collective-permute-done.3.wg1_ref
  55.1 0.0 collective-permute-done.4.wu1_ref
  55.2 0.0 collective-permute-done.5.wd1_ref
  55.2 0.0 copy-done.3
  55.2 0.6 copy-done.12
  55.8 5.0 %feed_forward.1 = (bf16[256,256]{1,0:T(8,128)(2,1)S(1)}, bf16[256,256]{1,0:T(8,128)(2,1)}, bf16[256,256]{1,0:T(8,128)(2,1)}, bf16[256,256]{1,0:T(8,128)(2,1)}) custom-call(s32[1]{0:T(128)} %bitcast.chan_ref, bf16[4,256,256]{2,1,0:T(8,128)(2,1)S(1)} %bitcast.10, bf16[256,256]{1,0:T(8,128)(2,1)S(1)} %get-tuple-element.16.gate0_ref, ...), custom_call_target="tpu_custom_call" | custom-call | tf_op jit(solution)/shard_map/feed_forward/pallas_call | solution.py:276
  60.8 0.6 copy-done.11
  61.5 0.9 %collective-permute-start.6 = (bf16[256,256]{1,0:T(8,128)(2,1)}, bf16[256,256]{1,0:T(8,128)(2,1)S(1)}, u32[]{:S(2)}, u32[]{:S(2)}) collective-permute-start(bf16[256,256]{1,0:T(8,128)(2,1)} %get-tuple-element.10), channel_id=1, source_target_pairs={{0,2},{1,3},{2,0},{3,1},{4,6},{5,7},{6,4},{7,5},{8,10},{9,11},{10,... | collective-permute-start | bytes 393224 | tf_op jit(solution)/shard_map/ppermute | solution.py:223
  62.4 0.1 collective-permute-start.7
  62.5 1.1 %collective-permute-start.8 = (bf16[256,256]{1,0:T(8,128)(2,1)}, bf16[256,256]{1,0:T(8,128)(2,1)S(1)}, u32[]{:S(2)}, u32[]{:S(2)}) collective-permute-start(bf16[256,256]{1,0:T(8,128)(2,1)} %get-tuple-element.12), channel_id=1, source_target_pairs={{0,3},{1,2},{2,1},{3,0},{4,7},{5,6},{6,5},{7,4},{8,11},{9,10},{10,... | collective-permute-start | bytes 393224 | tf_op jit(solution)/shard_map/ppermute | solution.py:223
  63.6 4.4 %collective-permute-done.6 = bf16[256,256]{1,0:T(8,128)(2,1)S(1)} collective-permute-done((bf16[256,256]{1,0:T(8,128)(2,1)}, bf16[256,256]{1,0:T(8,128)(2,1)S(1)}, u32[]{:S(2)}, u32[]{:S(2)}) %collective-permute-start.6) | collective-permute-done | bytes 131104 | tf_op jit(solution)/shard_map/ppermute | solution.py:223
  68.1 0.0 collective-permute-done.7
  68.1 0.8 %collective-permute-done.8 = bf16[256,256]{1,0:T(8,128)(2,1)S(1)} collective-permute-done((bf16[256,256]{1,0:T(8,128)(2,1)}, bf16[256,256]{1,0:T(8,128)(2,1)S(1)}, u32[]{:S(2)}, u32[]{:S(2)}) %collective-permute-start.8) | collective-permute-done | bytes 131104 | tf_op jit(solution)/shard_map/ppermute | solution.py:223
  68.8 1.0 %select_convert_fusion.1 = (bf16[256,256]{1,0:T(8,128)(2,1)S(1)}, bf16[256,256]{1,0:T(8,128)(2,1)S(1)}) fusion(bf16[256,256]{1,0:T(8,128)(2,1)S(1)} %collective-permute-done.6, bf16[256,256]{1,0:T(8,128)(2,1)} %copy-done.11, bf16[256,256]{1,0:T(8,128)(2,1)S(1)} %collective-permute-done.8, bf16[256,256]{1,0:T(8,128)(2,1)S(1)} %collective-permute-done.7, pred[]{:T(512)S(6)} %eq.6), kind=kLoop, calls=%fused_computation.2 | loop fusion | flops 655360 | bytes 786433 | tf_op jit(solution)/shard_map/convert_element_type | solution.py:301
  69.8 0.7 %pad_maximum_fusion = bf16[512,256]{1,0:T(8,128)(2,1)} fusion(bf16[256,256]{1,0:T(8,128)(2,1)S(1)} %get-tuple-element.14, bf16[256,256]{1,0:T(8,128)(2,1)S(1)} %get-tuple-element.13), kind=kLoop, calls=%fused_computation | loop fusion | flops 524288 | bytes 524288 | tf_op jit(solution)/shard_map/concatenate | solution.py:303
  (15 shorter events, 0.0 us)
Async XLA Ops:
  0.0 13.7 %copy-start = (f32[256]{0:T(256)S(1)}, f32[256]{0:T(256)}, u32[]{:S(2)}) copy-start(f32[256]{0:T(256)} %param.23) | copy-start | bytes 3076
  0.7 0.7 copy-start.13
  0.7 0.7 copy-start.14
  1.4 1.0 %copy-start.4 = (bf16[512,256]{1,0:T(8,128)(2,1)S(1)}, bf16[512,256]{1,0:T(8,128)(2,1)}, u32[]{:S(2)}) copy-start(bf16[512,256]{1,0:T(8,128)(2,1)} %value_ref.1) | copy-start | bytes 786436
  2.3 0.9 %copy-start.5 = (bf16[512,256]{1,0:T(8,128)(2,1)S(1)}, bf16[512,256]{1,0:T(8,128)(2,1)}, u32[]{:S(2)}) copy-start(bf16[512,256]{1,0:T(8,128)(2,1)} %filter_ref.1) | copy-start | bytes 786436
  3.3 0.9 %copy-start.10 = (f32[200,256]{1,0:T(8,128)S(1)}, f32[200,256]{1,0:T(8,128)}, u32[]{:S(2)}) copy-start(f32[200,256]{1,0:T(8,128)} %table_ref.1) | copy-start | bytes 614404
  4.2 8.8 %copy-start.1 = (bf16[1024,512]{1,0:T(8,128)(2,1)S(1)}, bf16[1024,512]{1,0:T(8,128)(2,1)}, u32[]{:S(2)}) copy-start(bf16[1024,512]{1,0:T(8,128)(2,1)} %wg0_ref.1) | copy-start | bytes 3145732
  4.2 8.9 %copy-start.2 = (bf16[1024,512]{1,0:T(8,128)(2,1)S(1)}, bf16[1024,512]{1,0:T(8,128)(2,1)}, u32[]{:S(2)}) copy-start(bf16[1024,512]{1,0:T(8,128)(2,1)} %wu0_ref.1) | copy-start | bytes 3145732
  5.7 21.8 %all-to-all-start = ((bf16[8,2,32,512]{3,2,1,0:T(8,128)(2,1)}), bf16[8,2,32,512]{3,2,1,0:T(8,128)(2,1)S(1)}, u32[]{:S(2)}, u32[]{:S(2)}) async-start(bf16[8,2,32,512]{3,2,1,0:T(8,128)(2,1)} %prepare.1), calls=%async_computation | async-start | bytes 1048576 | tf_op jit(solution)/shard_map/all_to_all | solution.py:245
  13.0 42.1 %collective-permute-start.3 = (bf16[1024,512]{1,0:T(8,128)(2,1)S(1)}, bf16[1024,512]{1,0:T(8,128)(2,1)}, u32[]{:S(2)}, u32[]{:S(2)}) collective-permute-start(bf16[1024,512]{1,0:T(8,128)(2,1)S(1)} %copy-done.1), channel_id=1, source_target_pairs={{0,1},{1,0},{2,3},{3,2},{4,5},{5,4},{6,7},{7,6},{8,9},{9,8},{10,11... | collective-permute-start | bytes 3145736 | tf_op jit(solution)/shard_map/ppermute | solution.py:223
  13.1 42.0 %collective-permute-start.4 = (bf16[1024,512]{1,0:T(8,128)(2,1)S(1)}, bf16[1024,512]{1,0:T(8,128)(2,1)}, u32[]{:S(2)}, u32[]{:S(2)}) collective-permute-start(bf16[1024,512]{1,0:T(8,128)(2,1)S(1)} %copy-done.2), channel_id=1, source_target_pairs={{0,1},{1,0},{2,3},{3,2},{4,5},{5,4},{6,7},{7,6},{8,9},{9,8},{10,11... | collective-permute-start | bytes 3145736 | tf_op jit(solution)/shard_map/ppermute | solution.py:223
  13.6 41.6 %collective-permute-start.5 = (bf16[512,1024]{1,0:T(8,128)(2,1)}, bf16[512,1024]{1,0:T(8,128)(2,1)}, u32[]{:S(2)}, u32[]{:S(2)}) collective-permute-start(bf16[512,1024]{1,0:T(8,128)(2,1)} %wd0_ref.1), channel_id=1, source_target_pairs={{0,1},{1,0},{2,3},{3,2},{4,5},{5,4},{6,7},{7,6},{8,9},{9,8},{10,11... | collective-permute-start | bytes 3145736 | tf_op jit(solution)/shard_map/ppermute | solution.py:223
  27.5 1.0 %copy-start.6 = (bf16[512,256]{1,0:T(8,128)(2,1)S(1)}, bf16[512,256]{1,0:T(8,128)(2,1)}, u32[]{:S(2)}) copy-start(bf16[512,256]{1,0:T(8,128)(2,1)} %constant.41.clone.gl_ref) | copy-start | bytes 786436
  28.5 0.9 %copy-start.7 = (bf16[512,256]{1,0:T(8,128)(2,1)S(1)}, bf16[512,256]{1,0:T(8,128)(2,1)}, u32[]{:S(2)}) copy-start(bf16[512,256]{1,0:T(8,128)(2,1)} %constant.40.clone.gh_ref) | copy-start | bytes 786436
  29.4 0.9 %copy-start.8 = (bf16[256,512]{1,0:T(8,128)(2,1)S(1)}, bf16[256,512]{1,0:T(8,128)(2,1)}, u32[]{:S(2)}) copy-start(bf16[256,512]{1,0:T(8,128)(2,1)} %constant.39.clone.fl_ref) | copy-start | bytes 786436
  30.4 0.9 %copy-start.9 = (bf16[256,512]{1,0:T(8,128)(2,1)S(1)}, bf16[256,512]{1,0:T(8,128)(2,1)}, u32[]{:S(2)}) copy-start(bf16[256,512]{1,0:T(8,128)(2,1)} %constant.38.clone.fh_ref) | copy-start | bytes 786436
  34.7 3.8 %copy-start.15 = (bf16[512,256]{1,0:T(8,128)(2,1)S(1)}, bf16[512,256]{1,0:T(8,128)(2,1)}, u32[]{:S(2)}) copy-start(bf16[512,256]{1,0:T(8,128)(2,1)} %param.17) | copy-start | bytes 786436
  34.7 19.3 %all-to-all-start.1 = ((bf16[32,32,256]{2,1,0:T(8,128)(2,1)}), bf16[32,32,256]{2,1,0:T(8,128)(2,1)}, u32[]{:S(2)}, u32[]{:S(2)}) async-start(bf16[32,32,256]{2,1,0:T(8,128)(2,1)} %bitcast.3), calls=%async_computation.1 | async-start | bytes 1048576 | tf_op jit(solution)/shard_map/all_to_all | solution.py:271
  38.5 16.7 %copy-start.3 = (bf16[512,1024]{1,0:T(8,128)(2,1)S(1)}, bf16[512,1024]{1,0:T(8,128)(2,1)}, u32[]{:S(2)}) copy-start(bf16[512,1024]{1,0:T(8,128)(2,1)} %wd0_ref.1) | copy-start | bytes 3145732
  39.2 8.8 %collective-permute-start.2 = (bf16[256,256]{1,0:T(8,128)(2,1)}, bf16[256,256]{1,0:T(8,128)(2,1)S(1)}, u32[]{:S(2)}, u32[]{:S(2)}) collective-permute-start(bf16[256,256]{1,0:T(8,128)(2,1)} %get-tuple-element.15), channel_id=1, source_target_pairs={{0,3},{1,2},{2,1},{3,0},{4,7},{5,6},{6,5},{7,4},{8,11},{9,10},{10,... | collective-permute-start | bytes 393224 | tf_op jit(solution)/shard_map/ppermute | solution.py:223
  40.6 14.5 %collective-permute-start = (bf16[256,256]{1,0:T(8,128)(2,1)}, bf16[256,256]{1,0:T(8,128)(2,1)S(1)}, u32[]{:S(2)}, u32[]{:S(2)}) collective-permute-start(bf16[256,256]{1,0:T(8,128)(2,1)} %get-tuple-element.15), channel_id=1, source_target_pairs={{0,1},{1,0},{2,3},{3,2},{4,5},{5,4},{6,7},{7,6},{8,9},{9,8},{10,11... | collective-permute-start | bytes 393224 | tf_op jit(solution)/shard_map/ppermute | solution.py:223
  48.0 7.2 %collective-permute-start.1 = (bf16[256,256]{1,0:T(8,128)(2,1)S(1)}, bf16[256,256]{1,0:T(8,128)(2,1)}, u32[]{:S(2)}, u32[]{:S(2)}) collective-permute-start(bf16[256,256]{1,0:T(8,128)(2,1)S(1)} %get-tuple-element.16.gate0_ref), channel_id=1, source_target_pairs={{0,2},{1,3},{2,0},{3,1},{4,6},{5,7},{6,4},{7,5},{8,10},{9,11},{10,... | collective-permute-start | bytes 393224 | tf_op jit(solution)/shard_map/ppermute | solution.py:223
  55.1 0.7 copy-start.12
  60.8 0.7 copy-start.11
  61.5 6.6 %collective-permute-start.6 = (bf16[256,256]{1,0:T(8,128)(2,1)}, bf16[256,256]{1,0:T(8,128)(2,1)S(1)}, u32[]{:S(2)}, u32[]{:S(2)}) collective-permute-start(bf16[256,256]{1,0:T(8,128)(2,1)} %get-tuple-element.10), channel_id=1, source_target_pairs={{0,2},{1,3},{2,0},{3,1},{4,6},{5,7},{6,4},{7,5},{8,10},{9,11},{10,... | collective-permute-start | bytes 393224 | tf_op jit(solution)/shard_map/ppermute | solution.py:223
  62.4 5.7 %collective-permute-start.7 = (bf16[256,256]{1,0:T(8,128)(2,1)}, bf16[256,256]{1,0:T(8,128)(2,1)S(1)}, u32[]{:S(2)}, u32[]{:S(2)}) collective-permute-start(bf16[256,256]{1,0:T(8,128)(2,1)} %get-tuple-element.11), channel_id=1, source_target_pairs={{0,1},{1,0},{2,3},{3,2},{4,5},{5,4},{6,7},{7,6},{8,9},{9,8},{10,11... | collective-permute-start | bytes 393224 | tf_op jit(solution)/shard_map/ppermute | solution.py:223
  62.5 6.3 %collective-permute-start.8 = (bf16[256,256]{1,0:T(8,128)(2,1)}, bf16[256,256]{1,0:T(8,128)(2,1)S(1)}, u32[]{:S(2)}, u32[]{:S(2)}) collective-permute-start(bf16[256,256]{1,0:T(8,128)(2,1)} %get-tuple-element.12), channel_id=1, source_target_pairs={{0,3},{1,2},{2,1},{3,0},{4,7},{5,6},{6,5},{7,4},{8,11},{9,10},{10,... | collective-permute-start | bytes 393224 | tf_op jit(solution)/shard_map/ppermute | solution.py:223
where the time goes:
time: 71.4 us; the launch traced here: 70.5 us
  waiting for transfers between devices  31 us (43%)
  starting transfers between devices  16.6 us (23%)
  local copies, waits for them, and re-layouts  10.5 us (15%)
  Pallas kernels  9.94 us (14%)
  other arithmetic  1.71 us (2%)
  between operations  0.83 us (1%)
    all_to_all x1, waiting for transfers between devices, shards(): both = lax.all_to_all(made, 'tm', split_axis=0, concat_axis=0, tiled=True)  13.6 us
    ppermute x9, waiting for transfers between devices, swap(): return lax.ppermute(values, 'chan', [(at, at ^ bits) for at in range(chan)])  12.2 us
    unnamed x32, local copies, waits for them, and re-layouts  8.59 us
    all_to_all x1, starting transfers between devices, shards(): both = lax.all_to_all(made, 'tm', split_axis=0, concat_axis=0, tiled=True)  7.28 us
    ppermute x9, starting transfers between devices, swap(): return lax.ppermute(values, 'chan', [(at, at ^ bits) for at in range(chan)])  5.51 us
    all_to_all x1, waiting for transfers between devices, shards(): lax.all_to_all(conv.reshape(tm * chan, own, block), ('tm', 'chan'), split...  5.15 us
    pallas_call x1, Pallas kernels, shards(): pl.pallas_call(feed_forward_kernel, out_shape=[jax.ShapeDtypeStruct((bloc...  5.03 us
    all_to_all x1, starting transfers between devices, shards(): lax.all_to_all(conv.reshape(tm * chan, own, block), ('tm', 'chan'), split...  3.78 us
  transfers between devices with their start and end apart: 11, of which 5 were waited for; matrix products, arithmetic and copies ran while one was open for 3% of the time, Pallas kernels for 5%

commit v1 on v0

--- a/solution.py
+++ b/solution.py
@@ -1,4 +1,4 @@
-import math
+import functools
 
 import jax
 import jax.numpy as jnp
@@ -33,26 +33,92 @@
     return jnp.dot(left, right, preferred_element_type=f32)
 
 
-def prepare_kernel(step_ref, flags_ref, value_ref, filter_ref, table_ref, mask_ref, out_ref):
+def start_loads(pairs, sems):
+    loads = [
+        pltpu.make_async_copy(src, dst, sems.at[at]) for at, (src, dst) in enumerate(pairs)
+    ]
+    for load in loads:
+        load.start()
+    return loads
+
+
+def prepare_kernel(
+    step_ref,
+    flags_hbm,
+    value_hbm,
+    filter_hbm,
+    table_hbm,
+    mask_hbm,
+    out_hbm,
+    flags_ref,
+    value_ref,
+    filter_ref,
+    table_ref,
+    mask_ref,
+    out_ref,
+    sems,
+    out_sems,
+):
+    loads = start_loads(
+        (
+            (filter_hbm, filter_ref),
+            (value_hbm, value_ref),
+            (flags_hbm, flags_ref),
+            (table_hbm, table_ref),
+            (mask_hbm, mask_ref),
+        ),
+        sems,
+    )
+    rows, width = value_ref.shape
+    groups = out_ref.shape[0]
+    lanes = 128
+    stores = []
+
+    def store(which, low, values):
+        share = groups * lanes // width
+        first = groups * low // width
+        part = out_ref.at[pl.ds(first, share), which]
+        part[...] = values.T.reshape(part.shape)
+        copy = pltpu.make_async_copy(
+            part, out_hbm.at[pl.ds(first, share), which], out_sems.at[len(stores)]
+        )
+        copy.start()
+        stores.append(copy)
+
+    steps = width // lanes if groups * lanes % width == 0 else 1
+    lanes = width // steps
+    loads[0].wait()
+    for low in range(0, width, lanes):
+        store(1, low, filter_ref[:, low : low + lanes])
+    for load in loads[1:]:
+        load.wait()
     embed = table_ref[pl.ds(step_ref[0], 1), :]
     mask = mask_ref[...]
-    parts = []
-    for at in range(value_ref.shape[0] // FLAGBLK):
-        rows = value_ref[at * FLAGBLK : (at + 1) * FLAGBLK, :].astype(f32)
-        parts.append((rows + embed + flags_ref[at].astype(f32) * mask).astype(bf16))
-    inputs = jnp.concatenate(parts, axis=0)
-    shape = (out_ref.shape[0], out_ref.shape[2], out_ref.shape[3])
-    out_ref[:, 0] = inputs.T.reshape(shape)
-    out_ref[:, 1] = filter_ref[...].T.reshape(shape)
+    for low in range(0, width, lanes):
+        here = slice(low, low + lanes)
+        parts = []
+        for at in range(rows // FLAGBLK):
+            values = value_ref[at * FLAGBLK : (at + 1) * FLAGBLK, here].astype(f32)
+            flag = flags_ref[at].astype(f32)
+            parts.append((values + embed[:, here] + flag * mask[:, here]).astype(bf16))
+        store(0, low, jnp.concatenate(parts, axis=0))
+    for copy in stores:
+        copy.wait()
 
 
 def convolve_kernel(
-    both_ref, fh_ref, fl_ref, gh_ref, gl_ref, skip_ref, out_ref, x_ref, h_ref, z_ref
+    both_ref, fh_hbm, fl_hbm, gh_hbm, gl_hbm, skip_ref, out_ref,
+    x_ref, h_ref, z_ref, fh_ref, fl_ref, gh_ref, gl_ref, sems
 ):
+    loads = start_loads(
+        ((fh_hbm, fh_ref), (fl_hbm, fl_ref), (gh_hbm, gh_ref), (gl_hbm, gl_ref)), sems
+    )
     tm, _, chans, rows = both_ref.shape
     block = rows // 2
     half = block // 2
     nb = 2 * tm
+    loads[0].wait()
+    loads[1].wait()
     for which, dst in ((0, x_ref), (1, h_ref)):
         for part in range(2):
             data = both_ref[:, which, :, part * block : (part + 1) * block]
@@ -123,6 +189,8 @@
         return carry
 
     lax.fori_loop(0, chans // 8, tile, 0)
+    loads[2].wait()
+    loads[3].wait()
     skip = skip_ref[...]
     for part in range(2):
         spec = z_ref[:, part].reshape(tm * chans, 2 * block)
@@ -142,30 +210,53 @@
     gate1_ref,
     gate2_ref,
     gate3_ref,
+    gain_hbm,
+    wg0_hbm,
+    wu0_hbm,
+    wg1_hbm,
+    wu1_hbm,
+    wd0_hbm,
+    wd1_hbm,
+    out0_ref,
+    out1_hbm,
+    out2_hbm,
+    out3_hbm,
+    mixed_ref,
+    normed_ref,
+    part_ref,
     gain_ref,
     wg0_ref,
     wu0_ref,
-    wd0_ref,
     wg1_ref,
     wu1_ref,
+    wd0_ref,
     wd1_ref,
-    out0_ref,
-    out1_ref,
-    out2_ref,
-    out3_ref,
-    mixed_ref,
-    normed_ref,
+    sems,
+    load_sems,
 ):
+    loads = start_loads(
+        (
+            (gain_hbm, gain_ref),
+            (wg0_hbm, wg0_ref),
+            (wu0_hbm, wu0_ref),
+            (wg1_hbm, wg1_ref),
+            (wu1_hbm, wu1_ref),
+            (wd0_hbm, wd0_ref),
+            (wd1_hbm, wd1_ref),
+        ),
+        load_sems,
+    )
     here = chan_ref[0]
     rows, width = gate0_ref.shape
     total = gain_ref.shape[0] * width
     square = jnp.zeros((rows, 1), f32)
     for j, gate_ref in enumerate((gate0_ref, gate1_ref, gate2_ref, gate3_ref)):
-        conv = conv_ref[here ^ j].T.astype(f32)
+        conv = conv_ref[:, here ^ j].reshape(width, rows).T.astype(f32)
         mixed = (gate_ref[...].astype(f32) * conv).astype(bf16)
         mixed_ref[j] = mixed
         wide = mixed.astype(f32)
         square = square + jnp.sum(wide * wide, axis=-1, keepdims=True)
+    loads[0].wait()
     scale = lax.rsqrt(square / total + 1e-06)
     for j in range(4):
         at = here ^ j
@@ -173,24 +264,50 @@
         normed_ref[:, pl.ds(pl.multiple_of(at * width, width), width)] = normed
     normed = normed_ref[...]
     hidden = []
-    for wg_ref, wu_ref in ((wg0_ref, wu0_ref), (wg1_ref, wu1_ref)):
+    for at, (wg_ref, wu_ref) in enumerate(((wg0_ref, wu0_ref), (wg1_ref, wu1_ref))):
+        loads[1 + 2 * at].wait()
+        loads[2 + 2 * at].wait()
         gate = dot(normed, wg_ref[...])
         up = dot(normed, wu_ref[...])
         hidden.append((gate / (1.0 + jnp.exp(-gate)) * up).astype(bf16))
-    for j, out_ref in ((2, out2_ref), (3, out3_ref), (1, out1_ref), (0, out0_ref)):
+    loads[5].wait()
+    loads[6].wait()
+    sends = []
+    for j, out_hbm in ((2, out2_hbm), (3, out3_hbm), (1, out1_hbm), (0, None)):
         cols = pl.ds(pl.multiple_of((here ^ j) * width, width), width)
         part = dot(hidden[0], wd0_ref[:, cols]) + dot(hidden[1], wd1_ref[:, cols])
         if j < 2:
             part = part + mixed_ref[j].astype(f32)
-        out_ref[...] = part.astype(bf16)
+        if out_hbm is None:
+            out0_ref[...] = part.astype(bf16)
+        else:
+            part_ref[j - 1] = part.astype(bf16)
+            send = pltpu.make_async_copy(part_ref.at[j - 1], out_hbm, sems.at[j - 1])
+            send.start()
+            sends.append(send)
+    for send in sends:
+        send.wait()
+
+
+def finish_kernel(core_ref, own_ref, side_ref, core1_ref, side1_ref, out_ref):
+    block = own_ref.shape[0]
+    same = pl.ds(pl.multiple_of(core_ref[0] * block, block), block)
+    other = pl.ds(pl.multiple_of((1 - core_ref[0]) * block, block), block)
+    out_ref[same, :] = (own_ref[...].astype(f32) + side_ref[...].astype(f32)).astype(bf16)
+    out_ref[other, :] = (core1_ref[...].astype(f32) + side1_ref[...].astype(f32)).astype(bf16)
 
 
 VMEM = pltpu.MemorySpace.VMEM
 SMEM = pltpu.MemorySpace.SMEM
+HBM = pltpu.MemorySpace.HBM
 
 
 def whole(space=VMEM):
     return pl.BlockSpec(memory_space=space)
+
+
+def stay(array):
+    return pltpu.with_memory_space_constraint(array, HBM)
 
 
 def params(mib):
@@ -223,22 +340,28 @@
         return lax.ppermute(values, "chan", [(at, at ^ bits) for at in range(chan)])
 
     direct = own % 16 == 0
+    shape = (tm, 2, own, rows) if direct else (1, 2, width, rows)
     made = pl.pallas_call(
         prepare_kernel,
-        out_shape=jax.ShapeDtypeStruct(
-            (tm, 2, own, rows) if direct else (1, 2, width, rows), bf16
-        ),
-        in_specs=[whole(SMEM), whole(SMEM)] + [whole()] * 4,
-        out_specs=whole(),
+        out_shape=jax.ShapeDtypeStruct(shape, bf16),
+        in_specs=[whole(SMEM)] + [whole(HBM)] * 5,
+        out_specs=whole(HBM),
+        scratch_shapes=[
+            pltpu.SMEM(block_flags.shape, jnp.int32),
+            pltpu.VMEM(series_value.shape, bf16),
+            pltpu.VMEM(long_filter.shape, bf16),
+            pltpu.VMEM(step_table.shape, f32),
+            pltpu.VMEM((1, width), f32),
+            pltpu.VMEM(shape, bf16),
+            pltpu.SemaphoreType.DMA((5,)),
+            pltpu.SemaphoreType.DMA((2 * max(1, width // 128),)),
+        ],
         compiler_params=params(32),
         name="prepare",
     )(
         diffusion_step,
-        block_flags,
-        series_value,
-        long_filter,
-        step_table,
-        mask_embed.reshape(1, width),
+        *map(stay, (block_flags, series_value, long_filter, step_table)),
+        stay(mask_embed.reshape(1, width)),
     )
     if not direct:
         made = made.reshape(2, tm, own, rows).transpose(1, 0, 2, 3)
@@ -256,13 +379,16 @@
         held = -(-own // 16) * 16
         both = jnp.pad(both, ((0, 0), (0, 0), (0, held - own), (0, 0)))
         skip = jnp.pad(skip, ((0, held - own), (0, 0)))
-    tables = [jnp.asarray(table) for table in block_tables(block)]
+    both, gates = lax.optimization_barrier((both, gates))
+    tables = [stay(jnp.asarray(table)) for table in block_tables(block)]
     conv = pl.pallas_call(
         convolve_kernel,
         out_shape=jax.ShapeDtypeStruct((tm, 2, 2, held, block), bf16),
-        in_specs=[whole()] * 6,
+        in_specs=[whole()] + [whole(HBM)] * 4 + [whole()],
         out_specs=whole(),
-        scratch_shapes=[pltpu.VMEM((tm, 2, held, 2 * block), f32)] * 3,
+        scratch_shapes=[pltpu.VMEM((tm, 2, held, 2 * block), f32)] * 3
+        + [pltpu.VMEM(table.shape, bf16) for table in tables]
+        + [pltpu.SemaphoreType.DMA((4,))],
         compiler_params=params(48),
         name="convolve",
     )(both, *tables, skip)
@@ -271,36 +397,47 @@
     conv = lax.all_to_all(
         conv.reshape(tm * chan, own, block), ("tm", "chan"), split_axis=0, concat_axis=0, tiled=True
     )
-    conv = conv.reshape(tm, chan, own, block).transpose(1, 0, 2, 3).reshape(chan, width, block)
-
+    conv = conv.reshape(tm, chan, own, block)
+    if not direct:
+        conv = conv.transpose(1, 0, 2, 3).reshape(1, chan, width, block)
+
+    gain = norm_gain.reshape(chan, 1, width)
     outs = pl.pallas_call(
         feed_forward_kernel,
         out_shape=[jax.ShapeDtypeStruct((block, width), bf16)] * 4,
-        in_specs=[whole(SMEM)] + [whole()] * 12,
-        out_specs=[whole()] * 4,
+        in_specs=[whole(SMEM)] + [whole()] * 5 + [whole(HBM)] * 7,
+        out_specs=[whole()] + [whole(HBM)] * 3,
         scratch_shapes=[
             pltpu.VMEM((4, block, width), bf16),
             pltpu.VMEM((block, 4 * width), bf16),
+            pltpu.VMEM((3, block, width), bf16),
+            pltpu.VMEM(gain.shape, f32),
+            pltpu.VMEM(w_gate.shape, bf16),
+            pltpu.VMEM(w_up.shape, bf16),
+            pltpu.VMEM(w_gate.shape, bf16),
+            pltpu.VMEM(w_up.shape, bf16),
+            pltpu.VMEM(w_down.shape, bf16),
+            pltpu.VMEM(w_down.shape, bf16),
+            pltpu.SemaphoreType.DMA((3,)),
+            pltpu.SemaphoreType.DMA((7,)),
         ],
         compiler_params=params(48),
         name="feed_forward",
+    )(here.reshape(1).astype(jnp.int32), conv, *gates, *map(stay, (gain, w_gate, w_up, wg1, wu1, w_down, wd1)))
+    return pl.pallas_call(
+        finish_kernel,
+        out_shape=jax.ShapeDtypeStruct((rows, width), bf16),
+        in_specs=[whole(SMEM)] + [whole()] * 4,
+        out_specs=whole(),
+        compiler_params=params(8),
+        name="finish",
     )(
-        here.reshape(1).astype(jnp.int32),
-        conv,
-        *gates,
-        norm_gain.reshape(chan, 1, width),
-        w_gate,
-        w_up,
-        w_down,
-        wg1,
-        wu1,
-        wd1,
-    )
-    same = outs[0].astype(f32) + swap(outs[2], 2).astype(f32)
-    other = swap(outs[1], 1).astype(f32) + swap(outs[3], 3).astype(f32)
-    first = jnp.where(core == 0, same, other).astype(bf16)
-    second = jnp.where(core == 0, other, same).astype(bf16)
-    return jnp.concatenate([first, second], axis=0)
+        core.reshape(1).astype(jnp.int32),
+        outs[0],
+        swap(outs[2], 2),
+        swap(outs[1], 1),
+        swap(outs[3], 3),
+    )
 
 
 def solution(mesh):

time: 71.4 us -> 62.5 us (0.88)
  local copies, waits for them, and re-layouts: 10.5 us -> 0.21 us
  Pallas kernels: 9.94 us -> 12.7 us
  other arithmetic: 1.71 us -> 0 us
  waiting for transfers between devices: 31 us -> 31.8 us
    all_to_all x1, waiting for transfers between devices: 5.15 us -> 15.5 us  [shards(): lax.all_to_all(conv.reshape(tm * chan, own, block), ('tm', 'chan'), split...]
    unnamed x32 -> x8, local copies, waits for them, and re-layouts: 8.59 us -> 0.02 us
    all_to_all x1, waiting for transfers between devices: 13.6 us -> 5.78 us  [shards(): both = lax.all_to_all(made, 'tm', split_axis=0, concat_axis=0, tiled=True)]
    ppermute x9, waiting for transfers between devices: 12.2 us -> 10.5 us  [swap(): return lax.ppermute(values, 'chan', [(at, at ^ bits) for at in range(chan)])]
    pallas_call x1 -> x2, Pallas kernels: 1.55 us -> 2.86 us  [the longest x1 2.09 us: shards(): pl.pallas_call(prepare_kernel, out_shape=jax.ShapeDtypeStruct(shape, bf16...]
    transpose x1 -> x0, local copies, waits for them, and re-layouts: 1.08 us -> none  [shards(): conv.reshape(tm, chan, own, block).transpose(1, 0, 2, 3)]
    pallas_call x1, Pallas kernels: 3.37 us -> 4.41 us  [shards(): pl.pallas_call(convolve_kernel, out_shape=jax.ShapeDtypeStruct((tm, 2, 2,...]
    convert_element_type x1 -> x0, other arithmetic: 0.98 us -> none  [shards(): first = jnp.where(core == 0, same, other).astype(bf16)]
  transfers between devices with their start and end apart: 11 -> 11, of which waited for: 5 -> 6; matrix products, arithmetic and copies ran while one was open for 3% -> 0% of each run, Pallas kernels for 5% -> 7%
where the time goes in v1:
time: 62.5 us; the launch traced here: 61.7 us
  waiting for transfers between devices  31.8 us (51%)
  starting transfers between devices  16.2 us (26%)
  Pallas kernels  12.7 us (20%)
  between operations  0.77 us (1%)
    all_to_all x1, waiting for transfers between devices, shards(): lax.all_to_all(conv.reshape(tm * chan, own, block), ('tm', 'chan'), split...  15.5 us
    ppermute x9, waiting for transfers between devices, swap(): return lax.ppermute(values, 'chan', [(at, at ^ bits) for at in range(chan)])  10.5 us
    all_to_all x1, starting transfers between devices, shards(): both = lax.all_to_all(made, 'tm', split_axis=0, concat_axis=0, tiled=True)  7.42 us
    all_to_all x1, waiting for transfers between devices, shards(): both = lax.all_to_all(made, 'tm', split_axis=0, concat_axis=0, tiled=True)  5.78 us
    pallas_call x1, Pallas kernels, shards(): pl.pallas_call(feed_forward_kernel, out_shape=[jax.ShapeDtypeStruct((bloc...  5.47 us
    ppermute x9, starting transfers between devices, swap(): return lax.ppermute(values, 'chan', [(at, at ^ bits) for at in range(chan)])  5.13 us
    pallas_call x1, Pallas kernels, shards(): pl.pallas_call(convolve_kernel, out_shape=jax.ShapeDtypeStruct((tm, 2, 2,...  4.41 us
    all_to_all x1, starting transfers between devices, shards(): lax.all_to_all(conv.reshape(tm * chan, own, block), ('tm', 'chan'), split...  3.66 us
  transfers between devices with their start and end apart: 11, of which 6 were waited for; matrix products, arithmetic and copies ran while one was open for 0% of the time, Pallas kernels for 7%

profile of v1, /device:TPU:0, one launch (start us, length us, event | category | flops | bytes accessed | tf_op | source)
XLA Modules:
  0.0 61.7 jit_solution(11718359632176561657)
XLA Ops:
  0.0 0.0 copy-start
  0.7 0.0 copy-start.3
  0.7 0.0 copy-start.2
  0.7 2.1 %prepare.1 = bf16[8,2,32,512]{3,2,1,0:T(8,128)(2,1)} custom-call(s32[1]{0:T(128)S(6)} %copy.18.step_ref, s32[8]{0:T(128)} %flags_hbm.1, bf16[512,256]{1,0:T(8,128)(2,1)} %value_hbm.1, bf16[512,256]{1,0:T(8,128)(2,1)} %filter_hbm.1, f32[200,256]{1,0:T(8,128)} %table_hbm.1, f32[1,256]{1,0:T(1,128)} %bitcast.10), custom_call_target="tpu_custom_call" | custom-call | tf_op jit(solution)/shard_map/prepare/pallas_call | solution.py:344
  2.8 0.0 copy-start.1
  2.8 7.4 %all-to-all-start = ((bf16[8,2,32,512]{3,2,1,0:T(8,128)(2,1)}), bf16[8,2,32,512]{3,2,1,0:T(8,128)(2,1)S(1)}, u32[]{:S(2)}, u32[]{:S(2)}) async-start(bf16[8,2,32,512]{3,2,1,0:T(8,128)(2,1)} %prepare.1), calls=%async_computation | async-start | bytes 1048576 | tf_op jit(solution)/shard_map/all_to_all | solution.py:368
  10.2 0.0 copy-done.3
  10.3 0.7 %collective-permute-start.2 = (bf16[256,256]{1,0:T(8,128)(2,1)S(1)}, bf16[256,256]{1,0:T(8,128)(2,1)S(1)}, u32[]{:S(2)}, u32[]{:S(2)}) collective-permute-start(bf16[256,256]{1,0:T(8,128)(2,1)S(1)} %get-tuple-element.23), channel_id=1, source_target_pairs={{0,3},{1,2},{2,1},{3,0},{4,7},{5,6},{6,5},{7,4},{8,11},{9,10},{10,... | collective-permute-start | bytes 393224 | tf_op jit(solution)/shard_map/ppermute | solution.py:340
  11.0 1.0 %collective-permute-start = (bf16[256,256]{1,0:T(8,128)(2,1)S(1)}, bf16[256,256]{1,0:T(8,128)(2,1)S(1)}, u32[]{:S(2)}, u32[]{:S(2)}) collective-permute-start(bf16[256,256]{1,0:T(8,128)(2,1)S(1)} %get-tuple-element.23), channel_id=1, source_target_pairs={{0,1},{1,0},{2,3},{3,2},{4,5},{5,4},{6,7},{7,6},{8,9},{9,8},{10,11... | collective-permute-start | bytes 393224 | tf_op jit(solution)/shard_map/ppermute | solution.py:340
  11.9 0.5 collective-permute-start.1
  12.5 0.0 copy-done.1
  12.5 0.0 collective-permute-start.3
  12.5 0.0 copy-done.2
  12.5 0.5 collective-permute-start.4
  13.0 3.1 %collective-permute-done.2.gate3_ref = bf16[256,256]{1,0:T(8,128)(2,1)S(1)} collective-permute-done((bf16[256,256]{1,0:T(8,128)(2,1)S(1)}, bf16[256,256]{1,0:T(8,128)(2,1)S(1)}, u32[]{:S(2)}, u32[]{:S(2)}) %collective-permute-start.2) | collective-permute-done | bytes 131104 | tf_op jit(solution)/shard_map/ppermute | solution.py:340
  16.1 0.2 collective-permute-start.5
  16.3 0.0 copy-done
  16.3 0.1 dynamic-slice_bitcast_fusion
  16.4 0.1 copy.17.skip_ref
  16.5 0.0 collective-permute-done.gate1_ref
  16.5 2.5 %collective-permute-done.1.gate2_ref = bf16[256,256]{1,0:T(8,128)(2,1)S(1)} collective-permute-done((bf16[256,256]{1,0:T(8,128)(2,1)S(1)}, bf16[256,256]{1,0:T(8,128)(2,1)S(1)}, u32[]{:S(2)}, u32[]{:S(2)}) %collective-permute-start.1) | collective-permute-done | bytes 131104 | tf_op jit(solution)/shard_map/ppermute | solution.py:340
  18.9 5.8 %all-to-all-done.both_ref = bf16[8,2,32,512]{3,2,1,0:T(8,128)(2,1)S(1)} async-done(((bf16[8,2,32,512]{3,2,1,0:T(8,128)(2,1)}), bf16[8,2,32,512]{3,2,1,0:T(8,128)(2,1)S(1)}, u32[]{:S(2)}, u32[]{:S(2)}) %all-to-all-start) | async-done | bytes 524320 | tf_op jit(solution)/shard_map/all_to_all | solution.py:368
  24.7 4.4 %convolve.1 = bf16[8,2,2,32,256]{4,3,2,1,0:T(8,128)(2,1)} custom-call(bf16[8,2,32,512]{3,2,1,0:T(8,128)(2,1)S(1)} %all-to-all-done.both_ref, bf16[256,512]{1,0:T(8,128)(2,1)} %constant.38.clone.fh_hbm, bf16[256,512]{1,0:T(8,128)(2,1)} %constant.39.clone.fl_hbm, bf16[512,256]{1,0:T(8,128)(2,1)} %constant.40.clone.gh_hbm, ...), custom_call_target="tpu_custom_call" | custom-call | tf_op jit(solution)/shard_map/convolve/pallas_call | solution.py:384
  29.1 3.7 %all-to-all-start.1 = ((bf16[32,32,256]{2,1,0:T(8,128)(2,1)}), bf16[32,32,256]{2,1,0:T(8,128)(2,1)S(1)}, u32[]{:S(2)}, u32[]{:S(2)}) async-start(bf16[32,32,256]{2,1,0:T(8,128)(2,1)} %bitcast.4), calls=%async_computation.1 | async-start | bytes 1048576 | tf_op jit(solution)/shard_map/all_to_all | solution.py:397
  32.8 0.0 collective-permute-done.3.wg1_hbm
  32.8 0.0 collective-permute-done.4.wu1_hbm
  32.8 0.0 collective-permute-done.5.wd1_hbm
  32.8 15.5 %all-to-all-done.1 = bf16[32,32,256]{2,1,0:T(8,128)(2,1)S(1)} async-done(((bf16[32,32,256]{2,1,0:T(8,128)(2,1)}), bf16[32,32,256]{2,1,0:T(8,128)(2,1)S(1)}, u32[]{:S(2)}, u32[]{:S(2)}) %all-to-all-start.1) | async-done | bytes 524320 | tf_op jit(solution)/shard_map/all_to_all | solution.py:397
  48.3 5.5 %feed_forward.1 = (bf16[256,256]{1,0:T(8,128)(2,1)S(1)}, bf16[256,256]{1,0:T(8,128)(2,1)S(1)}, bf16[256,256]{1,0:T(8,128)(2,1)S(1)}, bf16[256,256]{1,0:T(8,128)(2,1)S(1)}) custom-call(s32[1]{0:T(128)} %bitcast.1.chan_ref, bf16[8,4,32,256]{3,2,1,0:T(8,128)(2,1)S(1)} %bitcast.8, bf16[256,256]{1,0:T(8,128)(2,1)S(1)} %get-tuple-element.15.gate0_ref, ...), custom_call_target="tpu_custom_call" | custom-call | tf_op jit(solution)/shard_map/feed_forward/pallas_call | solution.py:405
  53.8 1.0 %collective-permute-start.6 = (bf16[256,256]{1,0:T(8,128)(2,1)S(1)}, bf16[256,256]{1,0:T(8,128)(2,1)S(1)}, u32[]{:S(2)}, u32[]{:S(2)}) collective-permute-start(bf16[256,256]{1,0:T(8,128)(2,1)S(1)} %get-tuple-element.20), channel_id=1, source_target_pairs={{0,2},{1,3},{2,0},{3,1},{4,6},{5,7},{6,4},{7,5},{8,10},{9,11},{10,... | collective-permute-start | bytes 393224 | tf_op jit(solution)/shard_map/ppermute | solution.py:340
  54.8 0.1 collective-permute-start.7
  55.0 1.1 %collective-permute-start.8 = (bf16[256,256]{1,0:T(8,128)(2,1)S(1)}, bf16[256,256]{1,0:T(8,128)(2,1)S(1)}, u32[]{:S(2)}, u32[]{:S(2)}) collective-permute-start(bf16[256,256]{1,0:T(8,128)(2,1)S(1)} %get-tuple-element.22), channel_id=1, source_target_pairs={{0,3},{1,2},{2,1},{3,0},{4,7},{5,6},{6,5},{7,4},{8,11},{9,10},{10,... | collective-permute-start | bytes 393224 | tf_op jit(solution)/shard_map/ppermute | solution.py:340
  56.0 4.2 %collective-permute-done.6.side_ref = bf16[256,256]{1,0:T(8,128)(2,1)S(1)} collective-permute-done((bf16[256,256]{1,0:T(8,128)(2,1)S(1)}, bf16[256,256]{1,0:T(8,128)(2,1)S(1)}, u32[]{:S(2)}, u32[]{:S(2)}) %collective-permute-start.6) | collective-permute-done | bytes 131104 | tf_op jit(solution)/shard_map/ppermute | solution.py:340
  60.3 0.0 collective-permute-done.7.core1_ref
  60.3 0.7 %collective-permute-done.8.side1_ref = bf16[256,256]{1,0:T(8,128)(2,1)S(1)} collective-permute-done((bf16[256,256]{1,0:T(8,128)(2,1)S(1)}, bf16[256,256]{1,0:T(8,128)(2,1)S(1)}, u32[]{:S(2)}, u32[]{:S(2)}) %collective-permute-start.8) | collective-permute-done | bytes 131104 | tf_op jit(solution)/shard_map/ppermute | solution.py:340
  61.0 0.8 %finish.1 = bf16[512,256]{1,0:T(8,128)(2,1)} custom-call(s32[1]{0:T(128)} %bitcast.core_ref, bf16[256,256]{1,0:T(8,128)(2,1)S(1)} %get-tuple-element.19.own_ref, bf16[256,256]{1,0:T(8,128)(2,1)S(1)} %collective-permute-done.6.side_ref, bf16[256,256]{1,0:T(8,128)(2,1)S(1)} %collective-permute-done.7.core1_ref, ...), custom_call_target="tpu_custom_call" | custom-call | tf_op jit(solution)/shard_map/finish/pallas_call | solution.py:427
  (1 shorter events, 0.0 us)
Async XLA Ops:
  0.0 16.3 %copy-start = (f32[256]{0:T(256)S(1)}, f32[256]{0:T(256)}, u32[]{:S(2)}) copy-start(f32[256]{0:T(256)} %param.23) | copy-start | bytes 3076
  0.7 9.6 %copy-start.3 = (bf16[512,256]{1,0:T(8,128)(2,1)S(1)}, bf16[512,256]{1,0:T(8,128)(2,1)}, u32[]{:S(2)}) copy-start(bf16[512,256]{1,0:T(8,128)(2,1)} %param.17) | copy-start | bytes 786436
  0.7 11.8 %copy-start.2 = (bf16[1024,512]{1,0:T(8,128)(2,1)S(1)}, bf16[1024,512]{1,0:T(8,128)(2,1)}, u32[]{:S(2)}) copy-start(bf16[1024,512]{1,0:T(8,128)(2,1)} %wu0_hbm.1) | copy-start | bytes 3145732
  2.8 9.7 %copy-start.1 = (bf16[1024,512]{1,0:T(8,128)(2,1)S(1)}, bf16[1024,512]{1,0:T(8,128)(2,1)}, u32[]{:S(2)}) copy-start(bf16[1024,512]{1,0:T(8,128)(2,1)} %wg0_hbm.1) | copy-start | bytes 3145732
  2.8 21.9 %all-to-all-start = ((bf16[8,2,32,512]{3,2,1,0:T(8,128)(2,1)}), bf16[8,2,32,512]{3,2,1,0:T(8,128)(2,1)S(1)}, u32[]{:S(2)}, u32[]{:S(2)}) async-start(bf16[8,2,32,512]{3,2,1,0:T(8,128)(2,1)} %prepare.1), calls=%async_computation | async-start | bytes 1048576 | tf_op jit(solution)/shard_map/all_to_all | solution.py:368
  10.3 5.8 %collective-permute-start.2 = (bf16[256,256]{1,0:T(8,128)(2,1)S(1)}, bf16[256,256]{1,0:T(8,128)(2,1)S(1)}, u32[]{:S(2)}, u32[]{:S(2)}) collective-permute-start(bf16[256,256]{1,0:T(8,128)(2,1)S(1)} %get-tuple-element.23), channel_id=1, source_target_pairs={{0,3},{1,2},{2,1},{3,0},{4,7},{5,6},{6,5},{7,4},{8,11},{9,10},{10,... | collective-permute-start | bytes 393224 | tf_op jit(solution)/shard_map/ppermute | solution.py:340
  11.0 5.5 %collective-permute-start = (bf16[256,256]{1,0:T(8,128)(2,1)S(1)}, bf16[256,256]{1,0:T(8,128)(2,1)S(1)}, u32[]{:S(2)}, u32[]{:S(2)}) collective-permute-start(bf16[256,256]{1,0:T(8,128)(2,1)S(1)} %get-tuple-element.23), channel_id=1, source_target_pairs={{0,1},{1,0},{2,3},{3,2},{4,5},{5,4},{6,7},{7,6},{8,9},{9,8},{10,11... | collective-permute-start | bytes 393224 | tf_op jit(solution)/shard_map/ppermute | solution.py:340
  11.9 7.0 %collective-permute-start.1 = (bf16[256,256]{1,0:T(8,128)(2,1)S(1)}, bf16[256,256]{1,0:T(8,128)(2,1)S(1)}, u32[]{:S(2)}, u32[]{:S(2)}) collective-permute-start(bf16[256,256]{1,0:T(8,128)(2,1)S(1)} %get-tuple-element.15.gate0_ref), channel_id=1, source_target_pairs={{0,2},{1,3},{2,0},{3,1},{4,6},{5,7},{6,4},{7,5},{8,10},{9,11},{10,... | collective-permute-start | bytes 393224 | tf_op jit(solution)/shard_map/ppermute | solution.py:340
  12.5 20.3 %collective-permute-start.3 = (bf16[1024,512]{1,0:T(8,128)(2,1)S(1)}, bf16[1024,512]{1,0:T(8,128)(2,1)}, u32[]{:S(2)}, u32[]{:S(2)}) collective-permute-start(bf16[1024,512]{1,0:T(8,128)(2,1)S(1)} %copy-done.1), channel_id=1, source_target_pairs={{0,1},{1,0},{2,3},{3,2},{4,5},{5,4},{6,7},{7,6},{8,9},{9,8},{10,11... | collective-permute-start | bytes 3145736 | tf_op jit(solution)/shard_map/ppermute | solution.py:340
  12.5 20.3 %collective-permute-start.4 = (bf16[1024,512]{1,0:T(8,128)(2,1)S(1)}, bf16[1024,512]{1,0:T(8,128)(2,1)}, u32[]{:S(2)}, u32[]{:S(2)}) collective-permute-start(bf16[1024,512]{1,0:T(8,128)(2,1)S(1)} %copy-done.2), channel_id=1, source_target_pairs={{0,1},{1,0},{2,3},{3,2},{4,5},{5,4},{6,7},{7,6},{8,9},{9,8},{10,11... | collective-permute-start | bytes 3145736 | tf_op jit(solution)/shard_map/ppermute | solution.py:340
  16.1 16.7 %collective-permute-start.5 = (bf16[512,1024]{1,0:T(8,128)(2,1)}, bf16[512,1024]{1,0:T(8,128)(2,1)}, u32[]{:S(2)}, u32[]{:S(2)}) collective-permute-start(bf16[512,1024]{1,0:T(8,128)(2,1)} %wd0_hbm.1), channel_id=1, source_target_pairs={{0,1},{1,0},{2,3},{3,2},{4,5},{5,4},{6,7},{7,6},{8,9},{9,8},{10,11... | collective-permute-start | bytes 3145736 | tf_op jit(solution)/shard_map/ppermute | solution.py:340
  29.1 19.2 %all-to-all-start.1 = ((bf16[32,32,256]{2,1,0:T(8,128)(2,1)}), bf16[32,32,256]{2,1,0:T(8,128)(2,1)S(1)}, u32[]{:S(2)}, u32[]{:S(2)}) async-start(bf16[32,32,256]{2,1,0:T(8,128)(2,1)} %bitcast.4), calls=%async_computation.1 | async-start | bytes 1048576 | tf_op jit(solution)/shard_map/all_to_all | solution.py:397
  53.8 6.4 %collective-permute-start.6 = (bf16[256,256]{1,0:T(8,128)(2,1)S(1)}, bf16[256,256]{1,0:T(8,128)(2,1)S(1)}, u32[]{:S(2)}, u32[]{:S(2)}) collective-permute-start(bf16[256,256]{1,0:T(8,128)(2,1)S(1)} %get-tuple-element.20), channel_id=1, source_target_pairs={{0,2},{1,3},{2,0},{3,1},{4,6},{5,7},{6,4},{7,5},{8,10},{9,11},{10,... | collective-permute-start | bytes 393224 | tf_op jit(solution)/shard_map/ppermute | solution.py:340
  54.8 5.5 %collective-permute-start.7 = (bf16[256,256]{1,0:T(8,128)(2,1)S(1)}, bf16[256,256]{1,0:T(8,128)(2,1)S(1)}, u32[]{:S(2)}, u32[]{:S(2)}) collective-permute-start(bf16[256,256]{1,0:T(8,128)(2,1)S(1)} %get-tuple-element.21), channel_id=1, source_target_pairs={{0,1},{1,0},{2,3},{3,2},{4,5},{5,4},{6,7},{7,6},{8,9},{9,8},{10,11... | collective-permute-start | bytes 393224 | tf_op jit(solution)/shard_map/ppermute | solution.py:340
  55.0 6.0 %collective-permute-start.8 = (bf16[256,256]{1,0:T(8,128)(2,1)S(1)}, bf16[256,256]{1,0:T(8,128)(2,1)S(1)}, u32[]{:S(2)}, u32[]{:S(2)}) collective-permute-start(bf16[256,256]{1,0:T(8,128)(2,1)S(1)} %get-tuple-element.22), channel_id=1, source_target_pairs={{0,3},{1,2},{2,1},{3,0},{4,7},{5,6},{6,5},{7,4},{8,11},{9,10},{10,... | collective-permute-start | bytes 393224 | tf_op jit(solution)/shard_map/ppermute | solution.py:340

commit v2 on v1

v2 whole, which is shorter than its diff:
```python
import functools

import jax
import jax.numpy as jnp
import numpy as np
from jax import lax
from jax.experimental import pallas as pl
from jax.experimental.pallas import tpu as pltpu
from jax.sharding import PartitionSpec as P

FLAGBLK = 64
bf16 = jnp.bfloat16
f32 = jnp.float32


def split_table(table):
    high = table.astype(bf16)
    low = (table - high.astype(np.float64)).astype(bf16)
    return high, low


def block_tables(block):
    freq = np.concatenate([np.arange(0, block, 2), np.arange(1, block, 2)])
    time = np.arange(block)
    turn = np.pi * ((2 * freq[None, :] + 1) * time[:, None] % (4 * block)) / (2 * block)
    forward = np.concatenate([np.cos(turn), -np.sin(turn)], axis=1)
    turn = np.pi * ((2 * freq[:, None] + 1) * (block + time[None, :]) % (4 * block)) / (2 * block)
    inverse = np.concatenate([np.cos(turn), -np.sin(turn)], axis=0) / block
    return split_table(forward) + split_table(inverse)


def dot(left, right):
    return jnp.dot(left, right, preferred_element_type=f32)


def start_loads(pairs, sems):
    loads = [
        pltpu.make_async_copy(src, dst, sems.at[at]) for at, (src, dst) in enumerate(pairs)
    ]
    for load in loads:
        load.start()
    return loads


def prepare_kernel(
    step_ref,
    flags_hbm,
    value_hbm,
    filter_hbm,
    table_hbm,
    mask_hbm,
    out_hbm,
    flags_ref,
    value_ref,
    filter_ref,
    table_ref,
    mask_ref,
    out_ref,
    sems,
    out_sems,
):
    loads = start_loads(
        (
            (filter_hbm, filter_ref),
            (value_hbm, value_ref),
            (flags_hbm, flags_ref),
            (table_hbm, table_ref),
            (mask_hbm, mask_ref),
        ),
        sems,
    )
    rows, width = value_ref.shape
    groups = out_ref.shape[0]
    lanes = 128
    stores = []

    def store(which, low, values):
        share = groups * lanes // width
        first = groups * low // width
        part = out_ref.at[pl.ds(first, share), which]
        part[...] = values.T.reshape(part.shape)
        copy = pltpu.make_async_copy(
            part, out_hbm.at[pl.ds(first, share), which], out_sems.at[len(stores)]
        )
        copy.start()
        stores.append(copy)

    steps = width // lanes if groups * lanes % width == 0 else 1
    lanes = width // steps
    loads[0].wait()
    for low in range(0, width, lanes):
        store(1, low, filter_ref[:, low : low + lanes])
    for load in loads[1:]:
        load.wait()
    embed = table_ref[pl.ds(step_ref[0], 1), :]
    mask = mask_ref[...]
    for low in range(0, width, lanes):
        here = slice(low, low + lanes)
        parts = []
        for at in range(rows // FLAGBLK):
            values = value_ref[at * FLAGBLK : (at + 1) * FLAGBLK, here].astype(f32)
            flag = flags_ref[at].astype(f32)
            parts.append((values + embed[:, here] + flag * mask[:, here]).astype(bf16))
        store(0, low, jnp.concatenate(parts, axis=0))
    for copy in stores:
        copy.wait()


def convolve_kernel(
    both_ref,
    fh_hbm,
    fl_hbm,
    gh_hbm,
    gl_hbm,
    skip_ref,
    out_hbm,
    x_ref,
    h_ref,
    z_ref,
    fh_ref,
    fl_ref,
    gh_ref,
    gl_ref,
    out_ref,
    sems,
    out_sems,
):
    loads = start_loads(
        ((fh_hbm, fh_ref), (fl_hbm, fl_ref), (gh_hbm, gh_ref), (gl_hbm, gl_ref)), sems
    )
    tm, _, chans, rows = both_ref.shape
    block = rows // 2
    half = block // 2
    nb = 2 * tm
    loads[0].wait()
    loads[1].wait()
    for which, dst in ((0, x_ref), (1, h_ref)):
        for part in range(2):
            data = both_ref[:, which, :, part * block : (part + 1) * block]
            data = data.reshape(tm * chans, block)
            spec = dot(data, fh_ref[...]) + dot(data, fl_ref[...])
            dst[:, part] = spec.reshape(tm, chans, 2 * block)

    def read(ref, at, sub, lanes):
        return ref[at // 2, at % 2, sub, lanes]

    def window(prev_re, prev_im, cur_re, cur_im, odd):
        if odd:
            return prev_re - cur_im, prev_im + cur_re
        return prev_re + cur_im, prev_im - cur_re

    def tile(step, carry):
        sub = pl.ds(pl.multiple_of(step * 8, 8), 8)
        width = min(128, half)
        for odd in range(2):
            for low in range(odd * half, (odd + 1) * half, width):
                re = slice(low, low + width)
                im = slice(block + low, block + low + width)
                zero = jnp.zeros((8, width), f32)

                def put(a, acc):
                    z_ref[a // 2, a % 2, sub, re] = acc[0] - acc[1]
                    z_ref[a // 2, a % 2, sub, im] = acc[2] - acc[0] - acc[1]

                def load(at):
                    xr, xi = read(x_ref, at, sub, re), read(x_ref, at, sub, im)
                    return xr, xi, xr + xi

                if nb <= 16:
                    taps = []
                    prev = (zero, zero)
                    for d in range(nb):
                        cur = read(h_ref, d, sub, re), read(h_ref, d, sub, im)
                        wr, wi = window(*prev, *cur, odd)
                        taps.append((wr, wi, wr + wi))
                        prev = cur
                    values = [load(at) for at in range(nb)]
                    for a in range(nb):
                        acc = None
                        for d in range(a + 1):
                            terms = [v * t for v, t in zip(values[a - d], taps[d])]
                            acc = terms if acc is None else [p + q for p, q in zip(acc, terms)]
                        put(a, acc)
                else:

                    def out_block(a, carry):
                        def pair(d, acc):
                            before = jnp.maximum(d - 1, 0)
                            keep = (d > 0).astype(f32)
                            wr, wi = window(
                                keep * read(h_ref, before, sub, re),
                                keep * read(h_ref, before, sub, im),
                                read(h_ref, d, sub, re),
                                read(h_ref, d, sub, im),
                                odd,
                            )
                            terms = zip(acc, load(a - d), (wr, wi, wr + wi))
                            return tuple(p + v * t for p, v, t in terms)

                        put(a, lax.fori_loop(0, a + 1, pair, (zero, zero, zero)))
                        return carry

                    lax.fori_loop(0, nb, out_block, 0)
        return carry

    lax.fori_loop(0, chans // 8, tile, 0)
    loads[2].wait()
    loads[3].wait()
    skip = skip_ref[...]
    stores = []
    for part in range(2):
        spec = z_ref[:, part].reshape(tm * chans, 2 * block)
        high = spec.astype(bf16)
        low = (spec - high.astype(f32)).astype(bf16)
        conv = dot(high, gh_ref[...]) + dot(low, gh_ref[...]) + dot(high, gl_ref[...])
        inputs = both_ref[:, 0, :, part * block : (part + 1) * block].astype(f32)
        out_ref[:, part] = (conv.reshape(tm, chans, block) + skip[None] * inputs).astype(bf16)
        store = pltpu.make_async_copy(
            out_ref.at[:, part], out_hbm.at[:, part], out_sems.at[part]
        )
        store.start()
        stores.append(store)
    for store in stores:
        store.wait()


def mix(conv_ref, gate_refs, place_ref, mixed_ref, ready_ref, gain_ref, square):
    chip, core = place_ref
    rows, width = gate_refs[0].shape
    for j, gate_ref in enumerate(gate_refs):
        at = core ^ j
        conv = conv_ref[:, at].reshape(width, rows).T.astype(f32)
        mixed = (gate_ref[...].astype(f32) * conv).astype(bf16)
        if mixed_ref is not None:
            mixed_ref[j] = mixed
        wide = mixed.astype(f32)
        square = square + jnp.sum(wide * wide, axis=-1, keepdims=True)
        lanes = pl.ds(pl.multiple_of(at * width, width), width)
        ready_ref[:, lanes] = (wide * gain_ref[2 * chip + at]).astype(bf16)
    return square


def feed_first_kernel(
    place_ref,
    conv_ref,
    gate0_ref,
    gate1_ref,
    gain_hbm,
    wg0_hbm,
    wu0_hbm,
    wg1_hbm,
    wu1_hbm,
    wd0_hbm,
    wd1_hbm,
    mixed_ref,
    square_ref,
    gain_ref,
    sums_ref,
    rest_ref,
    down_ref,
    ready_ref,
    now_ref,
    sems,
):
    chip, core = place_ref[0], place_ref[1]
    depth = now_ref.shape[1]
    hidden = wd0_hbm.shape[0]
    here = pl.ds(pl.multiple_of(chip * depth, depth), depth)
    there = pl.ds(pl.multiple_of((1 - chip) * depth, depth), depth)
    weights = (wg0_hbm, wu0_hbm, wg1_hbm, wu1_hbm)
    loads = start_loads(
        [(gain_hbm, gain_ref)]
        + [(weight.at[here], now_ref.at[at]) for at, weight in enumerate(weights)]
        + [(weight.at[there], rest_ref.at[at]) for at, weight in enumerate(weights)]
        + [
            (weight, down_ref.at[pl.ds(at * hidden, hidden)])
            for at, weight in enumerate((wd0_hbm, wd1_hbm))
        ],
        sems,
    )
    rows = gate0_ref.shape[0]
    loads[0].wait()
    square_ref[...] = mix(
        conv_ref,
        (gate0_ref, gate1_ref),
        (chip, core),
        mixed_ref,
        ready_ref,
        gain_ref,
        jnp.zeros((rows, 1), f32),
    )
    ready = ready_ref[...]
    for at in range(4):
        loads[1 + at].wait()
        sums_ref[at] = dot(ready, now_ref[at])
    for load in loads[5:]:
        load.wait()


def feed_second_kernel(
    place_ref,
    conv_ref,
    gate2_ref,
    gate3_ref,
    mixed_ref,
    square_ref,
    gain_ref,
    sums_ref,
    rest_ref,
    down_ref,
    out0_ref,
    out1_ref,
    out2_ref,
    out3_ref,
    ready_ref,
):
    chip, core = place_ref[0], place_ref[1]
    rows, width = gate2_ref.shape
    square = mix(
        conv_ref,
        (gate2_ref, gate3_ref),
        (1 - chip, core),
        None,
        ready_ref,
        gain_ref,
        square_ref[...],
    )
    scale = lax.rsqrt(square / (gain_ref.shape[0] * width) + 1e-06)
    ready = ready_ref[...]
    parts = []
    for at in range(2):
        gate = scale * (sums_ref[2 * at] + dot(ready, rest_ref[2 * at]))
        up = scale * (sums_ref[2 * at + 1] + dot(ready, rest_ref[2 * at + 1]))
        parts.append((gate / (1.0 + jnp.exp(-gate)) * up).astype(bf16))
    hidden = jnp.concatenate(parts, axis=1)
    for j, out_ref in ((2, out2_ref), (3, out3_ref), (1, out1_ref), (0, out0_ref)):
        at = (2 * chip + core) ^ j
        part = dot(hidden, down_ref[:, pl.ds(pl.multiple_of(at * width, width), width)])
        if j < 2:
            part = part + mixed_ref[j].astype(f32)
        out_ref[...] = part.astype(bf16)


def finish_kernel(place_ref, own_ref, side_ref, core1_ref, side1_ref, out_ref):
    block = own_ref.shape[0]
    same = pl.ds(pl.multiple_of(place_ref[1] * block, block), block)
    other = pl.ds(pl.multiple_of((1 - place_ref[1]) * block, block), block)
    out_ref[same, :] = (own_ref[...].astype(f32) + side_ref[...].astype(f32)).astype(bf16)
    out_ref[other, :] = (core1_ref[...].astype(f32) + side1_ref[...].astype(f32)).astype(bf16)


VMEM = pltpu.MemorySpace.VMEM
SMEM = pltpu.MemorySpace.SMEM
HBM = pltpu.MemorySpace.HBM


def whole(space=VMEM):
    return pl.BlockSpec(memory_space=space)


def stay(array):
    return pltpu.with_memory_space_constraint(array, HBM)


def params(mib):
    return pltpu.CompilerParams(vmem_limit_bytes=mib << 20)


def shards(
    series_value,
    series_gate,
    long_filter,
    step_table,
    diffusion_step,
    mask_embed,
    block_flags,
    skip_gain,
    norm_gain,
    w_gate,
    w_up,
    w_down,
):
    tm = lax.axis_size("tm")
    chip, core = lax.axis_index("x"), lax.axis_index("core")
    place = jnp.stack([chip, core]).astype(jnp.int32)
    rows, width = series_value.shape
    own = width // tm
    block = rows // 2
    depth = 2 * width

    def swap(values, bits):
        return lax.ppermute(values, ("x", "core"), [(at, at ^ bits) for at in range(4)])

    direct = own % 16 == 0
    shape = (tm, 2, own, rows) if direct else (1, 2, width, rows)
    made = pl.pallas_call(
        prepare_kernel,
        out_shape=jax.ShapeDtypeStruct(shape, bf16),
        in_specs=[whole(SMEM)] + [whole(HBM)] * 5,
        out_specs=whole(HBM),
        scratch_shapes=[
            pltpu.SMEM(block_flags.shape, jnp.int32),
            pltpu.VMEM(series_value.shape, bf16),
            pltpu.VMEM(long_filter.shape, bf16),
            pltpu.VMEM(step_table.shape, f32),
            pltpu.VMEM((1, width), f32),
            pltpu.VMEM(shape, bf16),
            pltpu.SemaphoreType.DMA((5,)),
            pltpu.SemaphoreType.DMA((2 * max(1, width // 128),)),
        ],
        compiler_params=params(32),
        name="prepare",
    )(
        diffusion_step,
        *map(stay, (block_flags, series_value, long_filter, step_table)),
        stay(mask_embed.reshape(1, width)),
    )
    if not direct:
        made = made.reshape(2, tm, own, rows).transpose(1, 0, 2, 3)
    both = lax.all_to_all(made, "tm", split_axis=0, concat_axis=0, tiled=True)

    gate_own = lax.dynamic_slice_in_dim(series_gate, core * block, block, 0)
    gate_other = lax.dynamic_slice_in_dim(series_gate, (1 - core) * block, block, 0)
    gates = (gate_own, swap(gate_other, 1), swap(gate_own, 2), swap(gate_other, 3))
    wg1, wu1, wd1 = swap(w_gate, 1), swap(w_up, 1), swap(w_down, 1)

    skip = lax.dynamic_slice_in_dim(skip_gain, lax.axis_index("tm") * own, own, 0)
    skip = skip.reshape(own, 1)
    held = own
    if not direct:
        held = -(-own // 16) * 16
        both = jnp.pad(both, ((0, 0), (0, 0), (0, held - own), (0, 0)))
        skip = jnp.pad(skip, ((0, held - own), (0, 0)))
    both, gates = lax.optimization_barrier((both, gates))
    tables = [stay(jnp.asarray(table)) for table in block_tables(block)]
    conv = pl.pallas_call(
        convolve_kernel,
        out_shape=jax.ShapeDtypeStruct((tm, 2, held, block), bf16),
        in_specs=[whole()] + [whole(HBM)] * 4 + [whole()],
        out_specs=whole(HBM),
        scratch_shapes=[pltpu.VMEM((tm, 2, held, 2 * block), f32)] * 3
        + [pltpu.VMEM(table.shape, bf16) for table in tables]
        + [pltpu.VMEM((tm, 2, held, block), bf16)]
        + [pltpu.SemaphoreType.DMA((4,)), pltpu.SemaphoreType.DMA((2,))],
        compiler_params=params(24),
        name="convolve",
    )(both, *tables, skip)
    if not direct:
        conv = conv[:, :, :own]

    conv = lax.all_to_all(
        conv.reshape(tm * 2, own, block), ("tm", "core"), split_axis=0, concat_axis=0, tiled=True
    )
    other = swap(conv, 2)

    def view(values):
        values = values.reshape(tm, 2, own, block)
        if not direct:
            values = values.transpose(1, 0, 2, 3).reshape(1, 2, width, block)
        return values

    gain = norm_gain.reshape(4, 1, width)
    held = [
        ((2, block, width), bf16),
        ((block, 1), f32),
        ((4, 1, width), f32),
        ((4, block, w_gate.shape[1]), f32),
        ((4, depth, w_gate.shape[1]), bf16),
        ((2 * w_down.shape[0], w_down.shape[1]), bf16),
    ]
    kept = pl.pallas_call(
        feed_first_kernel,
        out_shape=[jax.ShapeDtypeStruct(*spec) for spec in held],
        in_specs=[whole(SMEM)] + [whole()] * 3 + [whole(HBM)] * 7,
        out_specs=[whole()] * 6,
        scratch_shapes=[
            pltpu.VMEM((block, depth), bf16),
            pltpu.VMEM((4, depth, w_gate.shape[1]), bf16),
            pltpu.SemaphoreType.DMA((11,)),
        ],
        compiler_params=params(24),
        name="feed_first",
    )(place, view(conv), *gates[:2], *map(stay, (gain, w_gate, w_up, wg1, wu1, w_down, wd1)))
    outs = pl.pallas_call(
        feed_second_kernel,
        out_shape=[jax.ShapeDtypeStruct((block, width), bf16)] * 4,
        in_specs=[whole(SMEM)] + [whole()] * 9,
        out_specs=[whole()] * 4,
        scratch_shapes=[pltpu.VMEM((block, depth), bf16)],
        compiler_params=params(24),
        name="feed_second",
    )(place, view(other), *gates[2:], *kept)
    return pl.pallas_call(
        finish_kernel,
        out_shape=jax.ShapeDtypeStruct((rows, width), bf16),
        in_specs=[whole(SMEM)] + [whole()] * 4,
        out_specs=whole(),
        compiler_params=params(8),
        name="finish",
    )(place, outs[0], swap(outs[2], 2), swap(outs[1], 1), swap(outs[3], 3))


def solution(mesh):
    axes = mesh.devices.reshape(mesh.shape["tm"], mesh.shape["chan"] // 2, 2)
    mesh = jax.sharding.Mesh(axes, ("tm", "x", "core"))
    chan = ("x", "core")
    placed = (
        P("tm", chan),
        P("tm", chan),
        P("tm", chan),
        P(None, chan),
        P(),
        P(chan),
        P("tm"),
        P(chan),
        P(),
        P(None, chan),
        P(None, chan),
        P(chan, None),
    )
    return jax.shard_map(
        shards, mesh=mesh, in_specs=placed, out_specs=P("tm", chan), check_vma=False
    )
```

time: 62.5 us -> 61.5 us (0.984)
  waiting for transfers between devices: 31.8 us -> 17.6 us
  blocking collectives: 0 us -> 13.6 us
  starting transfers between devices: 16.2 us -> 14.9 us
  local copies, waits for them, and re-layouts: 0.21 us -> 1.16 us
    all_to_all x1 -> x0, waiting for transfers between devices: 15.5 us -> none  [shards(): lax.all_to_all(conv.reshape(tm * chan, own, block), ('tm', 'chan'), split...]
    all_to_all x0 -> x1, blocking collectives: none -> 13.6 us  [shards(): lax.all_to_all(conv.reshape(tm * 2, own, block), ('tm', 'core'), split_ax...]
    ppermute x9 -> x10, waiting for transfers between devices: 10.5 us -> 14.5 us  [swap(): lax.ppermute(values, ('x', 'core'), [(at, at ^ bits) for at in range(4)])]
    all_to_all x1 -> x0, starting transfers between devices: 3.66 us -> none  [shards(): lax.all_to_all(conv.reshape(tm * chan, own, block), ('tm', 'chan'), split...]
    all_to_all x1, waiting for transfers between devices: 5.78 us -> 3.09 us  [shards(): both = lax.all_to_all(made, 'tm', split_axis=0, concat_axis=0, tiled=True)]
    ppermute x9 -> x10, starting transfers between devices: 5.13 us -> 7.56 us  [swap(): lax.ppermute(values, ('x', 'core'), [(at, at ^ bits) for at in range(4)])]
    dynamic_slice x1, local copies, waits for them, and re-layouts: 0.03 us -> 0.98 us  [shards(): lax.dynamic_slice_in_dim(series_gate, (1 - core) * block, block, 0)]
    pallas_call x2 -> x3, Pallas kernels: 9.88 us -> 9.8 us  [the longest x1 4.04 us: shards(): pl.pallas_call(convolve_kernel, out_shape=jax.ShapeDtypeStruct((tm, 2, he...]
  transfers between devices with their start and end apart: 11 -> 11, of which waited for: 6 -> 7; matrix products, arithmetic and copies ran while one was open for 0% -> 2% of each run, Pallas kernels for 7% -> 12%
where the time goes in v2:
time: 61.5 us; the launch traced here: 61.2 us
  waiting for transfers between devices  17.6 us (29%)
  starting transfers between devices  14.9 us (24%)
  blocking collectives  13.6 us (22%)
  Pallas kernels  13.1 us (21%)
  local copies, waits for them, and re-layouts  1.16 us (2%)
  between operations  0.87 us (1%)
    ppermute x10, waiting for transfers between devices, swap(): lax.ppermute(values, ('x', 'core'), [(at, at ^ bits) for at in range(4)])  14.5 us
    all_to_all x1, blocking collectives, shards(): lax.all_to_all(conv.reshape(tm * 2, own, block), ('tm', 'core'), split_ax...  13.6 us
    ppermute x10, starting transfers between devices, swap(): lax.ppermute(values, ('x', 'core'), [(at, at ^ bits) for at in range(4)])  7.56 us
    all_to_all x1, starting transfers between devices, shards(): both = lax.all_to_all(made, 'tm', split_axis=0, concat_axis=0, tiled=True)  7.29 us
    pallas_call x1, Pallas kernels, shards(): pl.pallas_call(convolve_kernel, out_shape=jax.ShapeDtypeStruct((tm, 2, he...  4.04 us
    pallas_call x1, Pallas kernels, shards(): pl.pallas_call(feed_first_kernel, out_shape=[jax.ShapeDtypeStruct(*spec)...  3.47 us
    all_to_all x1, waiting for transfers between devices, shards(): both = lax.all_to_all(made, 'tm', split_axis=0, concat_axis=0, tiled=True)  3.09 us
    pallas_call x1, Pallas kernels, shards(): pl.pallas_call(feed_second_kernel, out_shape=[jax.ShapeDtypeStruct((block...  2.3 us
  transfers between devices with their start and end apart: 11, of which 7 were waited for; matrix products, arithmetic and copies ran while one was open for 2% of the time, Pallas kernels for 12%

profile of v2, /device:TPU:0, one launch (start us, length us, event | category | flops | bytes accessed | tf_op | source)
XLA Modules:
  0.0 61.2 jit_solution(7192477280081550535)
XLA Ops:
  0.0 0.0 copy-start
  0.0 0.0 copy-start.1
  0.0 0.0 copy-start.2
  0.8 2.0 %prepare.1 = bf16[8,2,32,512]{3,2,1,0:T(8,128)(2,1)} custom-call(s32[1]{0:T(128)S(6)} %copy.18.step_ref, s32[8]{0:T(128)} %flags_hbm.1, bf16[512,256]{1,0:T(8,128)(2,1)} %value_hbm.1, bf16[512,256]{1,0:T(8,128)(2,1)} %filter_hbm.1, f32[200,256]{1,0:T(8,128)} %table_hbm.1, f32[1,256]{1,0:T(1,128)} %bitcast.13), custom_call_target="tpu_custom_call" | custom-call | tf_op jit(solution)/shard_map/prepare/pallas_call | solution.py:396
  2.8 7.3 %all-to-all-start = ((bf16[8,2,32,512]{3,2,1,0:T(8,128)(2,1)}), bf16[8,2,32,512]{3,2,1,0:T(8,128)(2,1)S(1)}, u32[]{:S(2)}, u32[]{:S(2)}) async-start(bf16[8,2,32,512]{3,2,1,0:T(8,128)(2,1)} %prepare.1), calls=%async_computation | async-start | bytes 1048576 | tf_op jit(solution)/shard_map/all_to_all | solution.py:420
  10.1 0.0 copy-done.1
  10.1 0.1 collective-permute-start.4
  10.2 0.0 copy-done.2
  10.2 0.5 collective-permute-start.5
  10.7 0.1 collective-permute-start.6
  10.8 1.0 %constant_dynamic-slice_fusion = (bf16[256,256]{1,0:T(8,128)(2,1)S(1)}, bf16[256,256]{1,0:T(8,128)(2,1)S(1)}) fusion(bf16[512,256]{1,0:T(8,128)(2,1)} %param.17, s32[]{:T(128)S(6)} %select_n.10, s32[]{:T(128)S(6)} %select_n.9), kind=kLoop, calls=%fused_computation.2 | loop fusion | bytes 524296 | tf_op jit(solution)/shard_map/dynamic_slice | solution.py:423
  11.7 0.5 collective-permute-start
  12.2 1.5 %collective-permute-start.1 = (bf16[256,256]{1,0:T(8,128)(2,1)S(1)}, bf16[256,256]{1,0:T(8,128)(2,1)S(1)}, u32[]{:S(2)}, u32[]{:S(2)}) collective-permute-start(bf16[256,256]{1,0:T(8,128)(2,1)S(1)} %get-tuple-element.23.gate0_ref), channel_id=1, source_target_pairs={{0,2},{1,3},{2,0},{3,1},{4,6},{5,7},{6,4},{7,5},{8,10},{9,11},{10,... | collective-permute-start | bytes 393224 | tf_op jit(solution)/shard_map/ppermute | solution.py:392
  13.7 2.3 %collective-permute-done.gate1_ref = bf16[256,256]{1,0:T(8,128)(2,1)S(1)} collective-permute-done((bf16[256,256]{1,0:T(8,128)(2,1)S(1)}, bf16[256,256]{1,0:T(8,128)(2,1)S(1)}, u32[]{:S(2)}, u32[]{:S(2)}) %collective-permute-start) | collective-permute-done | bytes 131104 | tf_op jit(solution)/shard_map/ppermute | solution.py:392
  16.0 1.2 %collective-permute-start.2 = (bf16[256,256]{1,0:T(8,128)(2,1)S(1)}, bf16[256,256]{1,0:T(8,128)(2,1)S(1)}, u32[]{:S(2)}, u32[]{:S(2)}) collective-permute-start(bf16[256,256]{1,0:T(8,128)(2,1)S(1)} %get-tuple-element.35), channel_id=1, source_target_pairs={{0,3},{1,2},{2,1},{3,0},{4,7},{5,6},{6,5},{7,4},{8,11},{9,10},{10,... | collective-permute-start | bytes 393224 | tf_op jit(solution)/shard_map/ppermute | solution.py:392
  17.2 0.0 copy-done
  17.2 0.1 dynamic-slice_bitcast_fusion
  17.3 0.1 copy.17.skip_ref
  17.4 0.3 collective-permute-done.1.gate2_ref
  17.7 3.8 %collective-permute-done.2.gate3_ref = bf16[256,256]{1,0:T(8,128)(2,1)S(1)} collective-permute-done((bf16[256,256]{1,0:T(8,128)(2,1)S(1)}, bf16[256,256]{1,0:T(8,128)(2,1)S(1)}, u32[]{:S(2)}, u32[]{:S(2)}) %collective-permute-start.2) | collective-permute-done | bytes 131104 | tf_op jit(solution)/shard_map/ppermute | solution.py:392
  21.5 3.1 %all-to-all-done.both_ref = bf16[8,2,32,512]{3,2,1,0:T(8,128)(2,1)S(1)} async-done(((bf16[8,2,32,512]{3,2,1,0:T(8,128)(2,1)}), bf16[8,2,32,512]{3,2,1,0:T(8,128)(2,1)S(1)}, u32[]{:S(2)}, u32[]{:S(2)}) %all-to-all-start) | async-done | bytes 524320 | tf_op jit(solution)/shard_map/all_to_all | solution.py:420
  24.6 4.0 %convolve.1 = bf16[8,2,32,256]{3,2,1,0:T(8,128)(2,1)S(1)} custom-call(bf16[8,2,32,512]{3,2,1,0:T(8,128)(2,1)S(1)} %all-to-all-done.both_ref, bf16[256,512]{1,0:T(8,128)(2,1)} %constant.30.clone.fh_hbm, bf16[256,512]{1,0:T(8,128)(2,1)} %constant.31.clone.fl_hbm, bf16[512,256]{1,0:T(8,128)(2,1)} %constant.32.clone.gh_hbm, ...), custom_call_target="tpu_custom_call" | custom-call | tf_op jit(solution)/shard_map/convolve/pallas_call | solution.py:436
  28.6 13.6 %all_to_all.10 = bf16[16,32,256]{2,1,0:T(8,128)(2,1)S(1)} all-to-all(bf16[16,32,256]{2,1,0:T(8,128)(2,1)S(1)} %bitcast.10), channel_id=1, replica_groups=mesh['tm'=8,'x'=2,'core'=2] {'tm','core'}, dimensions={0} | all-to-all | bytes 524288 | tf_op jit(solution)/shard_map/all_to_all | solution.py:451
  42.2 1.5 %collective-permute-start.3 = (bf16[16,32,256]{2,1,0:T(8,128)(2,1)S(1)}, bf16[16,32,256]{2,1,0:T(8,128)(2,1)S(1)}, u32[]{:S(2)}, u32[]{:S(2)}) collective-permute-start(bf16[16,32,256]{2,1,0:T(8,128)(2,1)S(1)} %all_to_all.10), channel_id=1, source_target_pairs={{0,2},{1,3},{2,0},{3,1},{4,6},{5,7},{6,4},{7,5},{8,10},{9,11},{10,... | collective-permute-start | bytes 786440 | tf_op jit(solution)/shard_map/ppermute | solution.py:392
  43.7 0.1 pad_add_fusion.place_ref
  43.8 0.0 collective-permute-done.4.wg1_hbm
  43.8 0.0 collective-permute-done.5.wu1_hbm
  43.8 0.0 collective-permute-done.6.wd1_hbm
  43.8 3.5 %feed_first.1 = (bf16[2,256,256]{2,1,0:T(8,128)(2,1)S(1)}, f32[256,1]{1,0:T(8,128)S(1)}, f32[4,1,256]{2,1,0:T(1,128)S(1)}, f32[4,256,512]{2,1,0:T(8,128)S(1)}, b...) custom-call(s32[2]{0:T(128)S(1)} %pad_add_fusion.place_ref, bf16[8,2,32,256]{3,2,1,0:T(8,128)(2,1)S(1)} %bitcast.9, ...), custom_call_target="tpu_custom_call" | custom-call | tf_op jit(solution)/shard_map/feed_first/pallas_call | solution.py:471
  47.3 3.0 %collective-permute-done.3 = bf16[16,32,256]{2,1,0:T(8,128)(2,1)S(1)} collective-permute-done((bf16[16,32,256]{2,1,0:T(8,128)(2,1)S(1)}, bf16[16,32,256]{2,1,0:T(8,128)(2,1)S(1)}, u32[]{:S(2)}, u32[]{:S(2)}) %collective-permute-start.3) | collective-permute-done | bytes 262176 | tf_op jit(solution)/shard_map/ppermute | solution.py:392
  50.3 2.3 %feed_second.1 = (bf16[256,256]{1,0:T(8,128)(2,1)S(1)}, bf16[256,256]{1,0:T(8,128)(2,1)S(1)}, bf16[256,256]{1,0:T(8,128)(2,1)S(1)}, bf16[256,256]{1,0:T(8,128)(2,1)S(1)}) custom-call(s32[2]{0:T(128)S(1)} %pad_add_fusion.place_ref, bf16[8,2,32,256]{3,2,1,0:T(8,128)(2,1)S(1)} %bitcast.11, bf16[256,256]{1,0:T(8,128)(2,1)S(1)} %collective-permute-done.1.gate2_ref, ...), custom_call_target="tpu_custom_call" | custom-call | tf_op jit(solution)/shard_map/feed_second/pallas_call | solution.py:484
  52.6 1.6 %collective-permute-start.7 = (bf16[256,256]{1,0:T(8,128)(2,1)S(1)}, bf16[256,256]{1,0:T(8,128)(2,1)S(1)}, u32[]{:S(2)}, u32[]{:S(2)}) collective-permute-start(bf16[256,256]{1,0:T(8,128)(2,1)S(1)} %get-tuple-element.32), channel_id=1, source_target_pairs={{0,2},{1,3},{2,0},{3,1},{4,6},{5,7},{6,4},{7,5},{8,10},{9,11},{10,... | collective-permute-start | bytes 393224 | tf_op jit(solution)/shard_map/ppermute | solution.py:392
  54.1 0.0 collective-permute-start.8
  54.1 0.6 %collective-permute-start.9 = (bf16[256,256]{1,0:T(8,128)(2,1)S(1)}, bf16[256,256]{1,0:T(8,128)(2,1)S(1)}, u32[]{:S(2)}, u32[]{:S(2)}) collective-permute-start(bf16[256,256]{1,0:T(8,128)(2,1)S(1)} %get-tuple-element.34), channel_id=1, source_target_pairs={{0,3},{1,2},{2,1},{3,0},{4,7},{5,6},{6,5},{7,4},{8,11},{9,10},{10,... | collective-permute-start | bytes 393224 | tf_op jit(solution)/shard_map/ppermute | solution.py:392
  54.8 3.3 %collective-permute-done.7.side_ref = bf16[256,256]{1,0:T(8,128)(2,1)S(1)} collective-permute-done((bf16[256,256]{1,0:T(8,128)(2,1)S(1)}, bf16[256,256]{1,0:T(8,128)(2,1)S(1)}, u32[]{:S(2)}, u32[]{:S(2)}) %collective-permute-start.7) | collective-permute-done | bytes 131104 | tf_op jit(solution)/shard_map/ppermute | solution.py:392
  58.1 0.0 collective-permute-done.8.core1_ref
  58.1 1.8 %collective-permute-done.9.side1_ref = bf16[256,256]{1,0:T(8,128)(2,1)S(1)} collective-permute-done((bf16[256,256]{1,0:T(8,128)(2,1)S(1)}, bf16[256,256]{1,0:T(8,128)(2,1)S(1)}, u32[]{:S(2)}, u32[]{:S(2)}) %collective-permute-start.9) | collective-permute-done | bytes 131104 | tf_op jit(solution)/shard_map/ppermute | solution.py:392
  59.9 1.3 %finish.1 = bf16[512,256]{1,0:T(8,128)(2,1)} custom-call(s32[2]{0:T(128)S(1)} %pad_add_fusion.place_ref, bf16[256,256]{1,0:T(8,128)(2,1)S(1)} %get-tuple-element.31.own_ref, bf16[256,256]{1,0:T(8,128)(2,1)S(1)} %collective-permute-done.7.side_ref, bf16[256,256]{1,0:T(8,128)(2,1)S(1)} %collective-permute-done.8.core1_ref, ...), custom_call_target="tpu_custom_call" | custom-call | tf_op jit(solution)/shard_map/finish/pallas_call | solution.py:493
Async XLA Ops:
  0.0 17.2 %copy-start = (f32[256]{0:T(256)S(1)}, f32[256]{0:T(256)}, u32[]{:S(2)}) copy-start(f32[256]{0:T(256)} %param.23) | copy-start | bytes 3076
  0.0 10.1 %copy-start.1 = (bf16[1024,512]{1,0:T(8,128)(2,1)S(1)}, bf16[1024,512]{1,0:T(8,128)(2,1)}, u32[]{:S(2)}) copy-start(bf16[1024,512]{1,0:T(8,128)(2,1)} %wg0_hbm.1) | copy-start | bytes 3145732
  0.0 10.2 %copy-start.2 = (bf16[1024,512]{1,0:T(8,128)(2,1)S(1)}, bf16[1024,512]{1,0:T(8,128)(2,1)}, u32[]{:S(2)}) copy-start(bf16[1024,512]{1,0:T(8,128)(2,1)} %wu0_hbm.1) | copy-start | bytes 3145732
  2.8 21.8 %all-to-all-start = ((bf16[8,2,32,512]{3,2,1,0:T(8,128)(2,1)}), bf16[8,2,32,512]{3,2,1,0:T(8,128)(2,1)S(1)}, u32[]{:S(2)}, u32[]{:S(2)}) async-start(bf16[8,2,32,512]{3,2,1,0:T(8,128)(2,1)} %prepare.1), calls=%async_computation | async-start | bytes 1048576 | tf_op jit(solution)/shard_map/all_to_all | solution.py:420
  10.1 33.7 %collective-permute-start.4 = (bf16[1024,512]{1,0:T(8,128)(2,1)S(1)}, bf16[1024,512]{1,0:T(8,128)(2,1)}, u32[]{:S(2)}, u32[]{:S(2)}) collective-permute-start(bf16[1024,512]{1,0:T(8,128)(2,1)S(1)} %copy-done.1), channel_id=1, source_target_pairs={{0,1},{1,0},{2,3},{3,2},{4,5},{5,4},{6,7},{7,6},{8,9},{9,8},{10,11... | collective-permute-start | bytes 3145736 | tf_op jit(solution)/shard_map/ppermute | solution.py:392
  10.2 33.6 %collective-permute-start.5 = (bf16[1024,512]{1,0:T(8,128)(2,1)S(1)}, bf16[1024,512]{1,0:T(8,128)(2,1)}, u32[]{:S(2)}, u32[]{:S(2)}) collective-permute-start(bf16[1024,512]{1,0:T(8,128)(2,1)S(1)} %copy-done.2), channel_id=1, source_target_pairs={{0,1},{1,0},{2,3},{3,2},{4,5},{5,4},{6,7},{7,6},{8,9},{9,8},{10,11... | collective-permute-start | bytes 3145736 | tf_op jit(solution)/shard_map/ppermute | solution.py:392
  10.7 33.1 %collective-permute-start.6 = (bf16[512,1024]{1,0:T(8,128)(2,1)}, bf16[512,1024]{1,0:T(8,128)(2,1)}, u32[]{:S(2)}, u32[]{:S(2)}) collective-permute-start(bf16[512,1024]{1,0:T(8,128)(2,1)} %wd0_hbm.1), channel_id=1, source_target_pairs={{0,1},{1,0},{2,3},{3,2},{4,5},{5,4},{6,7},{7,6},{8,9},{9,8},{10,11... | collective-permute-start | bytes 3145736 | tf_op jit(solution)/shard_map/ppermute | solution.py:392
  11.7 4.3 %collective-permute-start = (bf16[256,256]{1,0:T(8,128)(2,1)S(1)}, bf16[256,256]{1,0:T(8,128)(2,1)S(1)}, u32[]{:S(2)}, u32[]{:S(2)}) collective-permute-start(bf16[256,256]{1,0:T(8,128)(2,1)S(1)} %get-tuple-element.35), channel_id=1, source_target_pairs={{0,1},{1,0},{2,3},{3,2},{4,5},{5,4},{6,7},{7,6},{8,9},{9,8},{10,11... | collective-permute-start | bytes 393224 | tf_op jit(solution)/shard_map/ppermute | solution.py:392
  12.2 5.5 %collective-permute-start.1 = (bf16[256,256]{1,0:T(8,128)(2,1)S(1)}, bf16[256,256]{1,0:T(8,128)(2,1)S(1)}, u32[]{:S(2)}, u32[]{:S(2)}) collective-permute-start(bf16[256,256]{1,0:T(8,128)(2,1)S(1)} %get-tuple-element.23.gate0_ref), channel_id=1, source_target_pairs={{0,2},{1,3},{2,0},{3,1},{4,6},{5,7},{6,4},{7,5},{8,10},{9,11},{10,... | collective-permute-start | bytes 393224 | tf_op jit(solution)/shard_map/ppermute | solution.py:392
  16.0 5.5 %collective-permute-start.2 = (bf16[256,256]{1,0:T(8,128)(2,1)S(1)}, bf16[256,256]{1,0:T(8,128)(2,1)S(1)}, u32[]{:S(2)}, u32[]{:S(2)}) collective-permute-start(bf16[256,256]{1,0:T(8,128)(2,1)S(1)} %get-tuple-element.35), channel_id=1, source_target_pairs={{0,3},{1,2},{2,1},{3,0},{4,7},{5,6},{6,5},{7,4},{8,11},{9,10},{10,... | collective-permute-start | bytes 393224 | tf_op jit(solution)/shard_map/ppermute | solution.py:392
  42.2 8.1 %collective-permute-start.3 = (bf16[16,32,256]{2,1,0:T(8,128)(2,1)S(1)}, bf16[16,32,256]{2,1,0:T(8,128)(2,1)S(1)}, u32[]{:S(2)}, u32[]{:S(2)}) collective-permute-start(bf16[16,32,256]{2,1,0:T(8,128)(2,1)S(1)} %all_to_all.10), channel_id=1, source_target_pairs={{0,2},{1,3},{2,0},{3,1},{4,6},{5,7},{6,4},{7,5},{8,10},{9,11},{10,... | collective-permute-start | bytes 786440 | tf_op jit(solution)/shard_map/ppermute | solution.py:392
  52.6 5.5 %collective-permute-start.7 = (bf16[256,256]{1,0:T(8,128)(2,1)S(1)}, bf16[256,256]{1,0:T(8,128)(2,1)S(1)}, u32[]{:S(2)}, u32[]{:S(2)}) collective-permute-start(bf16[256,256]{1,0:T(8,128)(2,1)S(1)} %get-tuple-element.32), channel_id=1, source_target_pairs={{0,2},{1,3},{2,0},{3,1},{4,6},{5,7},{6,4},{7,5},{8,10},{9,11},{10,... | collective-permute-start | bytes 393224 | tf_op jit(solution)/shard_map/ppermute | solution.py:392
  54.1 4.0 %collective-permute-start.8 = (bf16[256,256]{1,0:T(8,128)(2,1)S(1)}, bf16[256,256]{1,0:T(8,128)(2,1)S(1)}, u32[]{:S(2)}, u32[]{:S(2)}) collective-permute-start(bf16[256,256]{1,0:T(8,128)(2,1)S(1)} %get-tuple-element.33), channel_id=1, source_target_pairs={{0,1},{1,0},{2,3},{3,2},{4,5},{5,4},{6,7},{7,6},{8,9},{9,8},{10,11... | collective-permute-start | bytes 393224 | tf_op jit(solution)/shard_map/ppermute | solution.py:392
  54.1 5.8 %collective-permute-start.9 = (bf16[256,256]{1,0:T(8,128)(2,1)S(1)}, bf16[256,256]{1,0:T(8,128)(2,1)S(1)}, u32[]{:S(2)}, u32[]{:S(2)}) collective-permute-start(bf16[256,256]{1,0:T(8,128)(2,1)S(1)} %get-tuple-element.34), channel_id=1, source_target_pairs={{0,3},{1,2},{2,1},{3,0},{4,7},{5,6},{6,5},{7,4},{8,11},{9,10},{10,... | collective-permute-start | bytes 393224 | tf_op jit(solution)/shard_map/ppermute | solution.py:392

commit v3 on v2

--- a/solution.py
+++ b/solution.py
@@ -224,12 +224,11 @@
         store.wait()
 
 
-def mix(conv_ref, gate_refs, place_ref, mixed_ref, ready_ref, gain_ref, square):
-    chip, core = place_ref
+def mix(conv_refs, gate_refs, chip, core, mixed_ref, ready_ref, gain_ref, square):
     rows, width = gate_refs[0].shape
-    for j, gate_ref in enumerate(gate_refs):
+    for j, (conv_ref, gate_ref) in enumerate(zip(conv_refs, gate_refs)):
         at = core ^ j
-        conv = conv_ref[:, at].reshape(width, rows).T.astype(f32)
+        conv = conv_ref[:, core].reshape(width, rows).T.astype(f32)
         mixed = (gate_ref[...].astype(f32) * conv).astype(bf16)
         if mixed_ref is not None:
             mixed_ref[j] = mixed
@@ -241,8 +240,10 @@
 
 
 def feed_first_kernel(
-    place_ref,
-    conv_ref,
+    chip_ref,
+    core_ref,
+    conv0_ref,
+    conv1_ref,
     gate0_ref,
     gate1_ref,
     gain_hbm,
@@ -262,7 +263,7 @@
     now_ref,
     sems,
 ):
-    chip, core = place_ref[0], place_ref[1]
+    chip, core = chip_ref[0], core_ref[0]
     depth = now_ref.shape[1]
     hidden = wd0_hbm.shape[0]
     here = pl.ds(pl.multiple_of(chip * depth, depth), depth)
@@ -281,9 +282,10 @@
     rows = gate0_ref.shape[0]
     loads[0].wait()
     square_ref[...] = mix(
-        conv_ref,
+        (conv0_ref, conv1_ref),
         (gate0_ref, gate1_ref),
-        (chip, core),
+        chip,
+        core,
         mixed_ref,
         ready_ref,
         gain_ref,
@@ -298,8 +300,10 @@
 
 
 def feed_second_kernel(
-    place_ref,
-    conv_ref,
+    chip_ref,
+    core_ref,
+    conv2_ref,
+    conv3_ref,
     gate2_ref,
     gate3_ref,
     mixed_ref,
@@ -314,12 +318,13 @@
     out3_ref,
     ready_ref,
 ):
-    chip, core = place_ref[0], place_ref[1]
+    chip, core = chip_ref[0], core_ref[0]
     rows, width = gate2_ref.shape
     square = mix(
-        conv_ref,
+        (conv2_ref, conv3_ref),
         (gate2_ref, gate3_ref),
-        (1 - chip, core),
+        1 - chip,
+        core,
         None,
         ready_ref,
         gain_ref,
@@ -341,10 +346,10 @@
         out_ref[...] = part.astype(bf16)
 
 
-def finish_kernel(place_ref, own_ref, side_ref, core1_ref, side1_ref, out_ref):
+def finish_kernel(core_ref, own_ref, side_ref, core1_ref, side1_ref, out_ref):
     block = own_ref.shape[0]
-    same = pl.ds(pl.multiple_of(place_ref[1] * block, block), block)
-    other = pl.ds(pl.multiple_of((1 - place_ref[1]) * block, block), block)
+    same = pl.ds(pl.multiple_of(core_ref[0] * block, block), block)
+    other = pl.ds(pl.multiple_of((1 - core_ref[0]) * block, block), block)
     out_ref[same, :] = (own_ref[...].astype(f32) + side_ref[...].astype(f32)).astype(bf16)
     out_ref[other, :] = (core1_ref[...].astype(f32) + side1_ref[...].astype(f32)).astype(bf16)
 
@@ -382,7 +387,7 @@
 ):
     tm = lax.axis_size("tm")
     chip, core = lax.axis_index("x"), lax.axis_index("core")
-    place = jnp.stack([chip, core]).astype(jnp.int32)
+    place = chip.reshape(1).astype(jnp.int32), core.reshape(1).astype(jnp.int32)
     rows, width = series_value.shape
     own = width // tm
     block = rows // 2
@@ -448,13 +453,11 @@
     if not direct:
         conv = conv[:, :, :own]
 
-    conv = lax.all_to_all(
-        conv.reshape(tm * 2, own, block), ("tm", "core"), split_axis=0, concat_axis=0, tiled=True
-    )
-    other = swap(conv, 2)
+    conv = lax.all_to_all(conv, "tm", split_axis=0, concat_axis=0, tiled=True)
+    aside = swap(conv, 2)
+    beside = swap(conv, 1)
 
     def view(values):
-        values = values.reshape(tm, 2, own, block)
         if not direct:
             values = values.transpose(1, 0, 2, 3).reshape(1, 2, width, block)
         return values
@@ -471,7 +474,7 @@
     kept = pl.pallas_call(
         feed_first_kernel,
         out_shape=[jax.ShapeDtypeStruct(*spec) for spec in held],
-        in_specs=[whole(SMEM)] + [whole()] * 3 + [whole(HBM)] * 7,
+        in_specs=[whole(SMEM)] * 2 + [whole()] * 4 + [whole(HBM)] * 7,
         out_specs=[whole()] * 6,
         scratch_shapes=[
             pltpu.VMEM((block, depth), bf16),
@@ -480,16 +483,23 @@
         ],
         compiler_params=params(24),
         name="feed_first",
-    )(place, view(conv), *gates[:2], *map(stay, (gain, w_gate, w_up, wg1, wu1, w_down, wd1)))
+    )(
+        *place,
+        view(conv),
+        view(beside),
+        *gates[:2],
+        *map(stay, (gain, w_gate, w_up, wg1, wu1, w_down, wd1)),
+    )
+    aside, kept = lax.optimization_barrier((aside, kept))
     outs = pl.pallas_call(
         feed_second_kernel,
         out_shape=[jax.ShapeDtypeStruct((block, width), bf16)] * 4,
-        in_specs=[whole(SMEM)] + [whole()] * 9,
+        in_specs=[whole(SMEM)] * 2 + [whole()] * 10,
         out_specs=[whole()] * 4,
         scratch_shapes=[pltpu.VMEM((block, depth), bf16)],
         compiler_params=params(24),
         name="feed_second",
-    )(place, view(other), *gates[2:], *kept)
+    )(*place, view(aside), view(swap(aside, 1)), *gates[2:], *kept)
     return pl.pallas_call(
         finish_kernel,
         out_shape=jax.ShapeDtypeStruct((rows, width), bf16),
@@ -497,7 +507,7 @@
         out_specs=whole(),
         compiler_params=params(8),
         name="finish",
-    )(place, outs[0], swap(outs[2], 2), swap(outs[1], 1), swap(outs[3], 3))
+    )(place[1], outs[0], swap(outs[2], 2), swap(outs[1], 1), swap(outs[3], 3))
 
 
 def solution(mesh):

time: 61.5 us -> 63 us (1.024)
  waiting for transfers between devices: 17.6 us -> 21.9 us
  Pallas kernels: 13.1 us -> 11.4 us
  blocking collectives: 13.6 us -> 12.5 us
    ppermute x10 -> x12, waiting for transfers between devices: 14.5 us -> 18.8 us  [swap(): lax.ppermute(values, ('x', 'core'), [(at, at ^ bits) for at in range(4)])]
    all_to_all x1, blocking collectives: 13.6 us -> 12.5 us  [shards(): conv = lax.all_to_all(conv, 'tm', split_axis=0, concat_axis=0, tiled=True)]
    ppermute x10 -> x12, starting transfers between devices: 7.56 us -> 7.56 us  [swap(): lax.ppermute(values, ('x', 'core'), [(at, at ^ bits) for at in range(4)])]
  transfers between devices with their start and end apart: 11 -> 13, of which waited for: 7 -> 8; matrix products, arithmetic and copies ran while one was open for 2% -> 2% of each run, Pallas kernels for 12% -> 11%
where the time goes in v3:
time: 63 us; the launch traced here: 62.7 us
  waiting for transfers between devices  21.9 us (35%)
  starting transfers between devices  14.9 us (24%)
  blocking collectives  12.5 us (20%)
  Pallas kernels  11.4 us (18%)
  local copies, waits for them, and re-layouts  1.16 us (2%)
  between operations  0.87 us (1%)
    ppermute x12, waiting for transfers between devices, swap(): lax.ppermute(values, ('x', 'core'), [(at, at ^ bits) for at in range(4)])  18.8 us
    all_to_all x1, blocking collectives, shards(): conv = lax.all_to_all(conv, 'tm', split_axis=0, concat_axis=0, tiled=True)  12.5 us
    ppermute x12, starting transfers between devices, swap(): lax.ppermute(values, ('x', 'core'), [(at, at ^ bits) for at in range(4)])  7.56 us
    all_to_all x1, starting transfers between devices, shards(): both = lax.all_to_all(made, 'tm', split_axis=0, concat_axis=0, tiled=True)  7.29 us
    pallas_call x1, Pallas kernels, shards(): pl.pallas_call(convolve_kernel, out_shape=jax.ShapeDtypeStruct((tm, 2, he...  4.03 us
    all_to_all x1, waiting for transfers between devices, shards(): both = lax.all_to_all(made, 'tm', split_axis=0, concat_axis=0, tiled=True)  3.09 us
    pallas_call x1, Pallas kernels, shards(): pl.pallas_call(feed_first_kernel, out_shape=[jax.ShapeDtypeStruct(*spec)...  2.91 us
    pallas_call x1, Pallas kernels, shards(): pl.pallas_call(prepare_kernel, out_shape=jax.ShapeDtypeStruct(shape, bf16...  1.97 us
  transfers between devices with their start and end apart: 13, of which 8 were waited for; matrix products, arithmetic and copies ran while one was open for 2% of the time, Pallas kernels for 11%

profile of v3, /device:TPU:0, one launch (start us, length us, event | category | flops | bytes accessed | tf_op | source)
XLA Modules:
  0.0 62.7 jit_solution(441331784298350962)
XLA Ops:
  0.0 0.0 copy-start
  0.0 0.0 copy-start.1
  0.0 0.0 copy-start.2
  0.8 2.0 %prepare.1 = bf16[8,2,32,512]{3,2,1,0:T(8,128)(2,1)} custom-call(s32[1]{0:T(128)S(6)} %copy.18.step_ref, s32[8]{0:T(128)} %flags_hbm.1, bf16[512,256]{1,0:T(8,128)(2,1)} %value_hbm.1, bf16[512,256]{1,0:T(8,128)(2,1)} %filter_hbm.1, f32[200,256]{1,0:T(8,128)} %table_hbm.1, f32[1,256]{1,0:T(1,128)} %bitcast.7), custom_call_target="tpu_custom_call" | custom-call | tf_op jit(solution)/shard_map/prepare/pallas_call | solution.py:401
  2.8 7.3 %all-to-all-start = ((bf16[8,2,32,512]{3,2,1,0:T(8,128)(2,1)}), bf16[8,2,32,512]{3,2,1,0:T(8,128)(2,1)S(1)}, u32[]{:S(2)}, u32[]{:S(2)}) async-start(bf16[8,2,32,512]{3,2,1,0:T(8,128)(2,1)} %prepare.1), calls=%async_computation | async-start | bytes 1048576 | tf_op jit(solution)/shard_map/all_to_all | solution.py:425
  10.1 0.0 copy-done.1
  10.1 0.1 collective-permute-start.5
  10.2 0.0 copy-done.2
  10.2 0.5 collective-permute-start.6
  10.7 0.1 collective-permute-start.7
  10.7 1.0 %constant_dynamic-slice_fusion = (bf16[256,256]{1,0:T(8,128)(2,1)S(1)}, bf16[256,256]{1,0:T(8,128)(2,1)S(1)}) fusion(bf16[512,256]{1,0:T(8,128)(2,1)} %param.17, s32[]{:T(128)S(6)} %select_n.10, s32[]{:T(128)S(6)} %select_n.9), kind=kLoop, calls=%fused_computation.1 | loop fusion | bytes 524296 | tf_op jit(solution)/shard_map/dynamic_slice | solution.py:428
  11.7 0.5 collective-permute-start
  12.2 1.5 %collective-permute-start.1 = (bf16[256,256]{1,0:T(8,128)(2,1)S(1)}, bf16[256,256]{1,0:T(8,128)(2,1)S(1)}, u32[]{:S(2)}, u32[]{:S(2)}) collective-permute-start(bf16[256,256]{1,0:T(8,128)(2,1)S(1)} %get-tuple-element.28.gate0_ref), channel_id=1, source_target_pairs={{0,2},{1,3},{2,0},{3,1},{4,6},{5,7},{6,4},{7,5},{8,10},{9,11},{10,... | collective-permute-start | bytes 393224 | tf_op jit(solution)/shard_map/ppermute | solution.py:397
  13.7 2.3 %collective-permute-done.gate1_ref = bf16[256,256]{1,0:T(8,128)(2,1)S(1)} collective-permute-done((bf16[256,256]{1,0:T(8,128)(2,1)S(1)}, bf16[256,256]{1,0:T(8,128)(2,1)S(1)}, u32[]{:S(2)}, u32[]{:S(2)}) %collective-permute-start) | collective-permute-done | bytes 131104 | tf_op jit(solution)/shard_map/ppermute | solution.py:397
  16.0 1.2 %collective-permute-start.2 = (bf16[256,256]{1,0:T(8,128)(2,1)S(1)}, bf16[256,256]{1,0:T(8,128)(2,1)S(1)}, u32[]{:S(2)}, u32[]{:S(2)}) collective-permute-start(bf16[256,256]{1,0:T(8,128)(2,1)S(1)} %get-tuple-element.49), channel_id=1, source_target_pairs={{0,3},{1,2},{2,1},{3,0},{4,7},{5,6},{6,5},{7,4},{8,11},{9,10},{10,... | collective-permute-start | bytes 393224 | tf_op jit(solution)/shard_map/ppermute | solution.py:397
  17.2 0.0 copy-done
  17.2 0.1 dynamic-slice_bitcast_fusion
  17.3 0.1 copy.17.skip_ref
  17.4 0.3 collective-permute-done.1.gate2_ref
  17.7 3.8 %collective-permute-done.2.gate3_ref = bf16[256,256]{1,0:T(8,128)(2,1)S(1)} collective-permute-done((bf16[256,256]{1,0:T(8,128)(2,1)S(1)}, bf16[256,256]{1,0:T(8,128)(2,1)S(1)}, u32[]{:S(2)}, u32[]{:S(2)}) %collective-permute-start.2) | collective-permute-done | bytes 131104 | tf_op jit(solution)/shard_map/ppermute | solution.py:397
  21.5 3.1 %all-to-all-done.both_ref = bf16[8,2,32,512]{3,2,1,0:T(8,128)(2,1)S(1)} async-done(((bf16[8,2,32,512]{3,2,1,0:T(8,128)(2,1)}), bf16[8,2,32,512]{3,2,1,0:T(8,128)(2,1)S(1)}, u32[]{:S(2)}, u32[]{:S(2)}) %all-to-all-start) | async-done | bytes 524320 | tf_op jit(solution)/shard_map/all_to_all | solution.py:425
  24.6 4.0 %convolve.1 = bf16[8,2,32,256]{3,2,1,0:T(8,128)(2,1)S(1)} custom-call(bf16[8,2,32,512]{3,2,1,0:T(8,128)(2,1)S(1)} %all-to-all-done.both_ref, bf16[256,512]{1,0:T(8,128)(2,1)} %constant.30.clone.fh_hbm, bf16[256,512]{1,0:T(8,128)(2,1)} %constant.31.clone.fl_hbm, bf16[512,256]{1,0:T(8,128)(2,1)} %constant.32.clone.gh_hbm, ...), custom_call_target="tpu_custom_call" | custom-call | tf_op jit(solution)/shard_map/convolve/pallas_call | solution.py:441
  28.6 12.5 %all_to_all.10.conv0_ref = bf16[8,2,32,256]{3,2,1,0:T(8,128)(2,1)S(1)} all-to-all(bf16[8,2,32,256]{3,2,1,0:T(8,128)(2,1)S(1)} %convolve.1), channel_id=1, replica_groups=mesh['tm'=8,'x'=2,'core'=2] {'tm'}, dimensions={0} | all-to-all | bytes 524288 | tf_op jit(solution)/shard_map/all_to_all | solution.py:456
  41.1 0.0 collective-permute-start.4
  41.1 1.5 %collective-permute-start.3 = (bf16[8,2,32,256]{3,2,1,0:T(8,128)(2,1)S(1)}, bf16[8,2,32,256]{3,2,1,0:T(8,128)(2,1)S(1)}, u32[]{:S(2)}, u32[]{:S(2)}) collective-permute-start(bf16[8,2,32,256]{3,2,1,0:T(8,128)(2,1)S(1)} %all_to_all.10.conv0_ref), channel_id=1, source_target_pairs={{0,2},{1,3},{2,0},{3,1},{4,6},{5,7},{6,4},{7,5},{8,10},{9,11},{10,... | collective-permute-start | bytes 786440 | tf_op jit(solution)/shard_map/ppermute | solution.py:397
  42.6 0.0 collective-permute-done.5.wg1_hbm
  42.6 0.0 collective-permute-done.6.wu1_hbm
  42.6 0.0 collective-permute-done.7.wd1_hbm
  42.6 0.0 collective-permute-done.4.conv1_ref
  42.7 2.9 %feed_first.1 = (bf16[2,256,256]{2,1,0:T(8,128)(2,1)S(1)}, f32[256,1]{1,0:T(8,128)S(1)}, f32[4,1,256]{2,1,0:T(1,128)S(1)}, f32[4,256,512]{2,1,0:T(8,128)S(1)}, b...) custom-call(s32[1]{0:T(128)} %bitcast.1.chip_ref, s32[1]{0:T(128)} %bitcast.core_ref, ...), custom_call_target="tpu_custom_call" | custom-call | tf_op jit(solution)/shard_map/feed_first/pallas_call | solution.py:474
  45.6 4.3 %collective-permute-done.3.conv2_ref = bf16[8,2,32,256]{3,2,1,0:T(8,128)(2,1)S(1)} collective-permute-done((bf16[8,2,32,256]{3,2,1,0:T(8,128)(2,1)S(1)}, bf16[8,2,32,256]{3,2,1,0:T(8,128)(2,1)S(1)}, u32[]{:S(2)}, u32[]{:S(2)}) %collective-permute-start.3) | collective-permute-done | bytes 262176 | tf_op jit(solution)/shard_map/ppermute | solution.py:397
  49.9 0.0 collective-permute-start.8
  49.9 1.5 %collective-permute-done.8.conv3_ref = bf16[8,2,32,256]{3,2,1,0:T(8,128)(2,1)S(1)} collective-permute-done((bf16[8,2,32,256]{3,2,1,0:T(8,128)(2,1)S(1)}, bf16[8,2,32,256]{3,2,1,0:T(8,128)(2,1)S(1)}, u32[]{:S(2)}, u32[]{:S(2)}) %collective-permute-start.8) | collective-permute-done | bytes 262176 | tf_op jit(solution)/shard_map/ppermute | solution.py:397
  51.4 1.8 %feed_second.1 = (bf16[256,256]{1,0:T(8,128)(2,1)S(1)}, bf16[256,256]{1,0:T(8,128)(2,1)S(1)}, bf16[256,256]{1,0:T(8,128)(2,1)S(1)}, bf16[256,256]{1,0:T(8,128)(2,1)S(1)}) custom-call(s32[1]{0:T(128)} %bitcast.1.chip_ref, s32[1]{0:T(128)} %bitcast.core_ref, bf16[8,2,32,256]{3,2,1,0:T(8,128)(2,1)S(1)} %collective-permute-done.3.conv2_ref, ...), custom_call_target="tpu_custom_call" | custom-call | tf_op jit(solution)/shard_map/feed_second/pallas_call | solution.py:494
  53.2 0.2 collective-permute-start.10
  53.4 1.5 %collective-permute-start.11 = (bf16[256,256]{1,0:T(8,128)(2,1)S(1)}, bf16[256,256]{1,0:T(8,128)(2,1)S(1)}, u32[]{:S(2)}, u32[]{:S(2)}) collective-permute-start(bf16[256,256]{1,0:T(8,128)(2,1)S(1)} %get-tuple-element.48), channel_id=1, source_target_pairs={{0,3},{1,2},{2,1},{3,0},{4,7},{5,6},{6,5},{7,4},{8,11},{9,10},{10,... | collective-permute-start | bytes 393224 | tf_op jit(solution)/shard_map/ppermute | solution.py:397
  54.8 0.5 collective-permute-start.9
  55.4 0.0 collective-permute-done.10.core1_ref
  55.4 3.3 %collective-permute-done.11.side1_ref = bf16[256,256]{1,0:T(8,128)(2,1)S(1)} collective-permute-done((bf16[256,256]{1,0:T(8,128)(2,1)S(1)}, bf16[256,256]{1,0:T(8,128)(2,1)S(1)}, u32[]{:S(2)}, u32[]{:S(2)}) %collective-permute-start.11) | collective-permute-done | bytes 131104 | tf_op jit(solution)/shard_map/ppermute | solution.py:397
  58.7 3.3 %collective-permute-done.9.side_ref = bf16[256,256]{1,0:T(8,128)(2,1)S(1)} collective-permute-done((bf16[256,256]{1,0:T(8,128)(2,1)S(1)}, bf16[256,256]{1,0:T(8,128)(2,1)S(1)}, u32[]{:S(2)}, u32[]{:S(2)}) %collective-permute-start.9) | collective-permute-done | bytes 131104 | tf_op jit(solution)/shard_map/ppermute | solution.py:397
  62.0 0.8 %finish.1 = bf16[512,256]{1,0:T(8,128)(2,1)} custom-call(s32[1]{0:T(128)} %bitcast.core_ref, bf16[256,256]{1,0:T(8,128)(2,1)S(1)} %get-tuple-element.45.own_ref, bf16[256,256]{1,0:T(8,128)(2,1)S(1)} %collective-permute-done.9.side_ref, bf16[256,256]{1,0:T(8,128)(2,1)S(1)} %collective-permute-done.10.core1_ref, ...), custom_call_target="tpu_custom_call" | custom-call | tf_op jit(solution)/shard_map/finish/pallas_call | solution.py:503
Async XLA Ops:
  0.0 17.2 %copy-start = (f32[256]{0:T(256)S(1)}, f32[256]{0:T(256)}, u32[]{:S(2)}) copy-start(f32[256]{0:T(256)} %param.23) | copy-start | bytes 3076
  0.0 10.1 %copy-start.1 = (bf16[1024,512]{1,0:T(8,128)(2,1)S(1)}, bf16[1024,512]{1,0:T(8,128)(2,1)}, u32[]{:S(2)}) copy-start(bf16[1024,512]{1,0:T(8,128)(2,1)} %wg0_hbm.1) | copy-start | bytes 3145732
  0.0 10.2 %copy-start.2 = (bf16[1024,512]{1,0:T(8,128)(2,1)S(1)}, bf16[1024,512]{1,0:T(8,128)(2,1)}, u32[]{:S(2)}) copy-start(bf16[1024,512]{1,0:T(8,128)(2,1)} %wu0_hbm.1) | copy-start | bytes 3145732
  2.8 21.8 %all-to-all-start = ((bf16[8,2,32,512]{3,2,1,0:T(8,128)(2,1)}), bf16[8,2,32,512]{3,2,1,0:T(8,128)(2,1)S(1)}, u32[]{:S(2)}, u32[]{:S(2)}) async-start(bf16[8,2,32,512]{3,2,1,0:T(8,128)(2,1)} %prepare.1), calls=%async_computation | async-start | bytes 1048576 | tf_op jit(solution)/shard_map/all_to_all | solution.py:425
  10.1 32.6 %collective-permute-start.5 = (bf16[1024,512]{1,0:T(8,128)(2,1)S(1)}, bf16[1024,512]{1,0:T(8,128)(2,1)}, u32[]{:S(2)}, u32[]{:S(2)}) collective-permute-start(bf16[1024,512]{1,0:T(8,128)(2,1)S(1)} %copy-done.1), channel_id=1, source_target_pairs={{0,1},{1,0},{2,3},{3,2},{4,5},{5,4},{6,7},{7,6},{8,9},{9,8},{10,11... | collective-permute-start | bytes 3145736 | tf_op jit(solution)/shard_map/ppermute | solution.py:397
  10.2 32.5 %collective-permute-start.6 = (bf16[1024,512]{1,0:T(8,128)(2,1)S(1)}, bf16[1024,512]{1,0:T(8,128)(2,1)}, u32[]{:S(2)}, u32[]{:S(2)}) collective-permute-start(bf16[1024,512]{1,0:T(8,128)(2,1)S(1)} %copy-done.2), channel_id=1, source_target_pairs={{0,1},{1,0},{2,3},{3,2},{4,5},{5,4},{6,7},{7,6},{8,9},{9,8},{10,11... | collective-permute-start | bytes 3145736 | tf_op jit(solution)/shard_map/ppermute | solution.py:397
  10.7 32.0 %collective-permute-start.7 = (bf16[512,1024]{1,0:T(8,128)(2,1)}, bf16[512,1024]{1,0:T(8,128)(2,1)}, u32[]{:S(2)}, u32[]{:S(2)}) collective-permute-start(bf16[512,1024]{1,0:T(8,128)(2,1)} %wd0_hbm.1), channel_id=1, source_target_pairs={{0,1},{1,0},{2,3},{3,2},{4,5},{5,4},{6,7},{7,6},{8,9},{9,8},{10,11... | collective-permute-start | bytes 3145736 | tf_op jit(solution)/shard_map/ppermute | solution.py:397
  11.7 4.3 %collective-permute-start = (bf16[256,256]{1,0:T(8,128)(2,1)S(1)}, bf16[256,256]{1,0:T(8,128)(2,1)S(1)}, u32[]{:S(2)}, u32[]{:S(2)}) collective-permute-start(bf16[256,256]{1,0:T(8,128)(2,1)S(1)} %get-tuple-element.49), channel_id=1, source_target_pairs={{0,1},{1,0},{2,3},{3,2},{4,5},{5,4},{6,7},{7,6},{8,9},{9,8},{10,11... | collective-permute-start | bytes 393224 | tf_op jit(solution)/shard_map/ppermute | solution.py:397
  12.2 5.5 %collective-permute-start.1 = (bf16[256,256]{1,0:T(8,128)(2,1)S(1)}, bf16[256,256]{1,0:T(8,128)(2,1)S(1)}, u32[]{:S(2)}, u32[]{:S(2)}) collective-permute-start(bf16[256,256]{1,0:T(8,128)(2,1)S(1)} %get-tuple-element.28.gate0_ref), channel_id=1, source_target_pairs={{0,2},{1,3},{2,0},{3,1},{4,6},{5,7},{6,4},{7,5},{8,10},{9,11},{10,... | collective-permute-start | bytes 393224 | tf_op jit(solution)/shard_map/ppermute | solution.py:397
  16.0 5.5 %collective-permute-start.2 = (bf16[256,256]{1,0:T(8,128)(2,1)S(1)}, bf16[256,256]{1,0:T(8,128)(2,1)S(1)}, u32[]{:S(2)}, u32[]{:S(2)}) collective-permute-start(bf16[256,256]{1,0:T(8,128)(2,1)S(1)} %get-tuple-element.49), channel_id=1, source_target_pairs={{0,3},{1,2},{2,1},{3,0},{4,7},{5,6},{6,5},{7,4},{8,11},{9,10},{10,... | collective-permute-start | bytes 393224 | tf_op jit(solution)/shard_map/ppermute | solution.py:397
  41.1 1.5 %collective-permute-start.4 = (bf16[8,2,32,256]{3,2,1,0:T(8,128)(2,1)S(1)}, bf16[8,2,32,256]{3,2,1,0:T(8,128)(2,1)S(1)}, u32[]{:S(2)}, u32[]{:S(2)}) collective-permute-start(bf16[8,2,32,256]{3,2,1,0:T(8,128)(2,1)S(1)} %all_to_all.10.conv0_ref), channel_id=1, source_target_pairs={{0,1},{1,0},{2,3},{3,2},{4,5},{5,4},{6,7},{7,6},{8,9},{9,8},{10,11... | collective-permute-start | bytes 786440 | tf_op jit(solution)/shard_map/ppermute | solution.py:397
  41.1 8.7 %collective-permute-start.3 = (bf16[8,2,32,256]{3,2,1,0:T(8,128)(2,1)S(1)}, bf16[8,2,32,256]{3,2,1,0:T(8,128)(2,1)S(1)}, u32[]{:S(2)}, u32[]{:S(2)}) collective-permute-start(bf16[8,2,32,256]{3,2,1,0:T(8,128)(2,1)S(1)} %all_to_all.10.conv0_ref), channel_id=1, source_target_pairs={{0,2},{1,3},{2,0},{3,1},{4,6},{5,7},{6,4},{7,5},{8,10},{9,11},{10,... | collective-permute-start | bytes 786440 | tf_op jit(solution)/shard_map/ppermute | solution.py:397
  49.9 1.5 %collective-permute-start.8 = (bf16[8,2,32,256]{3,2,1,0:T(8,128)(2,1)S(1)}, bf16[8,2,32,256]{3,2,1,0:T(8,128)(2,1)S(1)}, u32[]{:S(2)}, u32[]{:S(2)}) collective-permute-start(bf16[8,2,32,256]{3,2,1,0:T(8,128)(2,1)S(1)} %collective-permute-done.3.conv2_ref), channel_id=1, source_target_pairs={{0,1},{1,0},{2,3},{3,2},{4,5},{5,4},{6,7},{7,6},{8,9},{9,8},{10,11... | collective-permute-start | bytes 786440 | tf_op jit(solution)/shard_map/ppermute | solution.py:397
  53.2 2.2 %collective-permute-start.10 = (bf16[256,256]{1,0:T(8,128)(2,1)S(1)}, bf16[256,256]{1,0:T(8,128)(2,1)S(1)}, u32[]{:S(2)}, u32[]{:S(2)}) collective-permute-start(bf16[256,256]{1,0:T(8,128)(2,1)S(1)} %get-tuple-element.47), channel_id=1, source_target_pairs={{0,1},{1,0},{2,3},{3,2},{4,5},{5,4},{6,7},{7,6},{8,9},{9,8},{10,11... | collective-permute-start | bytes 393224 | tf_op jit(solution)/shard_map/ppermute | solution.py:397
  53.4 5.3 %collective-permute-start.11 = (bf16[256,256]{1,0:T(8,128)(2,1)S(1)}, bf16[256,256]{1,0:T(8,128)(2,1)S(1)}, u32[]{:S(2)}, u32[]{:S(2)}) collective-permute-start(bf16[256,256]{1,0:T(8,128)(2,1)S(1)} %get-tuple-element.48), channel_id=1, source_target_pairs={{0,3},{1,2},{2,1},{3,0},{4,7},{5,6},{6,5},{7,4},{8,11},{9,10},{10,... | collective-permute-start | bytes 393224 | tf_op jit(solution)/shard_map/ppermute | solution.py:397
  54.8 7.2 %collective-permute-start.9 = (bf16[256,256]{1,0:T(8,128)(2,1)S(1)}, bf16[256,256]{1,0:T(8,128)(2,1)S(1)}, u32[]{:S(2)}, u32[]{:S(2)}) collective-permute-start(bf16[256,256]{1,0:T(8,128)(2,1)S(1)} %get-tuple-element.46), channel_id=1, source_target_pairs={{0,2},{1,3},{2,0},{3,1},{4,6},{5,7},{6,4},{7,5},{8,10},{9,11},{10,... | collective-permute-start | bytes 393224 | tf_op jit(solution)/shard_map/ppermute | solution.py:397

commit v4 on v3

--- a/solution.py
+++ b/solution.py
@@ -107,9 +107,10 @@
 
 
 def convolve_kernel(
+    core_ref,
     both_ref,
-    fh_hbm,
-    fl_hbm,
+    fh_ref,
+    fl_ref,
     gh_hbm,
     gl_hbm,
     skip_ref,
@@ -117,23 +118,17 @@
     x_ref,
     h_ref,
     z_ref,
-    fh_ref,
-    fl_ref,
     gh_ref,
     gl_ref,
     out_ref,
     sems,
     out_sems,
 ):
-    loads = start_loads(
-        ((fh_hbm, fh_ref), (fl_hbm, fl_ref), (gh_hbm, gh_ref), (gl_hbm, gl_ref)), sems
-    )
+    loads = start_loads(((gh_hbm, gh_ref), (gl_hbm, gl_ref)), sems)
     tm, _, chans, rows = both_ref.shape
     block = rows // 2
     half = block // 2
     nb = 2 * tm
-    loads[0].wait()
-    loads[1].wait()
     for which, dst in ((0, x_ref), (1, h_ref)):
         for part in range(2):
             data = both_ref[:, which, :, part * block : (part + 1) * block]
@@ -204,8 +199,8 @@
         return carry
 
     lax.fori_loop(0, chans // 8, tile, 0)
-    loads[2].wait()
-    loads[3].wait()
+    for load in loads:
+        load.wait()
     skip = skip_ref[...]
     stores = []
     for part in range(2):
@@ -216,7 +211,7 @@
         inputs = both_ref[:, 0, :, part * block : (part + 1) * block].astype(f32)
         out_ref[:, part] = (conv.reshape(tm, chans, block) + skip[None] * inputs).astype(bf16)
         store = pltpu.make_async_copy(
-            out_ref.at[:, part], out_hbm.at[:, part], out_sems.at[part]
+            out_ref.at[:, part], out_hbm.at[:, part ^ core_ref[0]], out_sems.at[part]
         )
         store.start()
         stores.append(store)
@@ -228,7 +223,7 @@
     rows, width = gate_refs[0].shape
     for j, (conv_ref, gate_ref) in enumerate(zip(conv_refs, gate_refs)):
         at = core ^ j
-        conv = conv_ref[:, core].reshape(width, rows).T.astype(f32)
+        conv = conv_ref[...].reshape(width, rows).T.astype(f32)
         mixed = (gate_ref[...].astype(f32) * conv).astype(bf16)
         if mixed_ref is not None:
             mixed_ref[j] = mixed
@@ -437,31 +432,31 @@
         both = jnp.pad(both, ((0, 0), (0, 0), (0, held - own), (0, 0)))
         skip = jnp.pad(skip, ((0, held - own), (0, 0)))
     both, gates = lax.optimization_barrier((both, gates))
-    tables = [stay(jnp.asarray(table)) for table in block_tables(block)]
+    tables = [jnp.asarray(table) for table in block_tables(block)]
+    tables = tables[:2] + [stay(table) for table in tables[2:]]
     conv = pl.pallas_call(
         convolve_kernel,
         out_shape=jax.ShapeDtypeStruct((tm, 2, held, block), bf16),
-        in_specs=[whole()] + [whole(HBM)] * 4 + [whole()],
+        in_specs=[whole(SMEM)] + [whole()] * 3 + [whole(HBM)] * 2 + [whole()],
         out_specs=whole(HBM),
         scratch_shapes=[pltpu.VMEM((tm, 2, held, 2 * block), f32)] * 3
-        + [pltpu.VMEM(table.shape, bf16) for table in tables]
+        + [pltpu.VMEM(table.shape, bf16) for table in tables[2:]]
         + [pltpu.VMEM((tm, 2, held, block), bf16)]
-        + [pltpu.SemaphoreType.DMA((4,)), pltpu.SemaphoreType.DMA((2,))],
+        + [pltpu.SemaphoreType.DMA((2,))] * 2,
         compiler_params=params(24),
         name="convolve",
-    )(both, *tables, skip)
+    )(place[1], both, *tables, skip)
     if not direct:
         conv = conv[:, :, :own]
 
     conv = lax.all_to_all(conv, "tm", split_axis=0, concat_axis=0, tiled=True)
-    aside = swap(conv, 2)
-    beside = swap(conv, 1)
-
-    def view(values):
-        if not direct:
-            values = values.transpose(1, 0, 2, 3).reshape(1, 2, width, block)
-        return values
-
+    mine, theirs = conv[:, 0], conv[:, 1]
+    aside, across, beside = swap(mine, 2), swap(theirs, 3), swap(theirs, 1)
+
+    if not direct:
+        mine, beside, aside, across = (
+            values.reshape(1, width, block) for values in (mine, beside, aside, across)
+        )
     gain = norm_gain.reshape(4, 1, width)
     held = [
         ((2, block, width), bf16),
@@ -485,12 +480,12 @@
         name="feed_first",
     )(
         *place,
-        view(conv),
-        view(beside),
+        mine,
+        beside,
         *gates[:2],
         *map(stay, (gain, w_gate, w_up, wg1, wu1, w_down, wd1)),
     )
-    aside, kept = lax.optimization_barrier((aside, kept))
+    aside, across, kept = lax.optimization_barrier((aside, across, kept))
     outs = pl.pallas_call(
         feed_second_kernel,
         out_shape=[jax.ShapeDtypeStruct((block, width), bf16)] * 4,
@@ -499,7 +494,7 @@
         scratch_shapes=[pltpu.VMEM((block, depth), bf16)],
         compiler_params=params(24),
         name="feed_second",
-    )(*place, view(aside), view(swap(aside, 1)), *gates[2:], *kept)
+    )(*place, aside, across, *gates[2:], *kept)
     return pl.pallas_call(
         finish_kernel,
         out_shape=jax.ShapeDtypeStruct((rows, width), bf16),

time: 63 us -> 60.2 us (0.956)
  waiting for transfers between devices: 21.9 us -> 20.5 us
  Pallas kernels: 11.4 us -> 10.4 us
  local copies, waits for them, and re-layouts: 1.16 us -> 0.23 us
    ppermute x12, waiting for transfers between devices: 18.8 us -> 14.8 us  [swap(): lax.ppermute(values, ('x', 'core'), [(at, at ^ bits) for at in range(4)])]
    all_to_all x1, waiting for transfers between devices: 3.09 us -> 5.77 us  [shards(): both = lax.all_to_all(made, 'tm', split_axis=0, concat_axis=0, tiled=True)]
    pallas_call x1, Pallas kernels: 4.03 us -> 2.99 us  [shards(): pl.pallas_call(convolve_kernel, out_shape=jax.ShapeDtypeStruct((tm, 2, he...]
    dynamic_slice x1, local copies, waits for them, and re-layouts: 0.98 us -> 0.02 us  [shards(): lax.dynamic_slice_in_dim(series_gate, (1 - core) * block, block, 0)]
  transfers between devices with their start and end apart: 13 -> 13, of which waited for: 8 -> 8; matrix products, arithmetic and copies ran while one was open for 2% -> 0% of each run, Pallas kernels for 11% -> 10%
where the time goes in v4:
time: 60.2 us; the launch traced here: 59.9 us
  waiting for transfers between devices  20.5 us (34%)
  starting transfers between devices  15.4 us (26%)
  blocking collectives  12.5 us (21%)
  Pallas kernels  10.4 us (17%)
  between operations  0.89 us (1%)
    ppermute x12, waiting for transfers between devices, swap(): lax.ppermute(values, ('x', 'core'), [(at, at ^ bits) for at in range(4)])  14.8 us
    all_to_all x1, blocking collectives, shards(): conv = lax.all_to_all(conv, 'tm', split_axis=0, concat_axis=0, tiled=True)  12.5 us
    ppermute x12, starting transfers between devices, swap(): lax.ppermute(values, ('x', 'core'), [(at, at ^ bits) for at in range(4)])  8.05 us
    all_to_all x1, starting transfers between devices, shards(): both = lax.all_to_all(made, 'tm', split_axis=0, concat_axis=0, tiled=True)  7.3 us
    all_to_all x1, waiting for transfers between devices, shards(): both = lax.all_to_all(made, 'tm', split_axis=0, concat_axis=0, tiled=True)  5.77 us
    pallas_call x1, Pallas kernels, shards(): pl.pallas_call(convolve_kernel, out_shape=jax.ShapeDtypeStruct((tm, 2, he...  2.99 us
    pallas_call x1, Pallas kernels, shards(): pl.pallas_call(feed_first_kernel, out_shape=[jax.ShapeDtypeStruct(*spec)...  2.93 us
    pallas_call x1, Pallas kernels, shards(): pl.pallas_call(prepare_kernel, out_shape=jax.ShapeDtypeStruct(shape, bf16...  1.98 us
  transfers between devices with their start and end apart: 13, of which 8 were waited for; matrix products, arithmetic and copies ran while one was open for 0% of the time, Pallas kernels for 10%

profile of v4, /device:TPU:0, one launch (start us, length us, event | category | flops | bytes accessed | tf_op | source)
XLA Modules:
  0.0 59.9 jit_solution(1196348739257811686)
XLA Ops:
  0.0 0.0 copy-start
  0.0 0.0 copy-start.1
  0.0 0.0 copy-start.2
  0.0 0.0 copy-start.3
  0.0 0.0 copy-start.4
  0.8 2.0 %prepare.1 = bf16[8,2,32,512]{3,2,1,0:T(8,128)(2,1)} custom-call(s32[1]{0:T(128)S(6)} %copy.24.step_ref, s32[8]{0:T(128)} %flags_hbm.1, bf16[512,256]{1,0:T(8,128)(2,1)} %value_hbm.1, bf16[512,256]{1,0:T(8,128)(2,1)} %filter_hbm.1, f32[200,256]{1,0:T(8,128)} %table_hbm.1, f32[1,256]{1,0:T(1,128)} %bitcast.15), custom_call_target="tpu_custom_call" | custom-call | tf_op jit(solution)/shard_map/prepare/pallas_call | solution.py:396
  2.8 7.3 %all-to-all-start = ((bf16[8,2,32,512]{3,2,1,0:T(8,128)(2,1)}), bf16[8,2,32,512]{3,2,1,0:T(8,128)(2,1)S(1)}, u32[]{:S(2)}, u32[]{:S(2)}) async-start(bf16[8,2,32,512]{3,2,1,0:T(8,128)(2,1)} %prepare.1), calls=%async_computation | async-start | bytes 1048576 | tf_op jit(solution)/shard_map/all_to_all | solution.py:420
  10.1 0.0 copy-done.3
  10.1 0.1 collective-permute-start.6
  10.2 0.0 copy-done.4
  10.2 0.5 collective-permute-start
  10.8 0.1 collective-permute-start.7
  10.8 0.4 collective-permute-start.8
  11.3 1.5 %collective-permute-start.1 = (bf16[256,256]{1,0:T(8,128)(2,1)S(1)}, bf16[256,256]{1,0:T(8,128)(2,1)S(1)}, u32[]{:S(2)}, u32[]{:S(2)}) collective-permute-start(bf16[256,256]{1,0:T(8,128)(2,1)S(1)} %get-tuple-element.29.gate0_ref), channel_id=1, source_target_pairs={{0,2},{1,3},{2,0},{3,1},{4,6},{5,7},{6,4},{7,5},{8,10},{9,11},{10,... | collective-permute-start | bytes 393224 | tf_op jit(solution)/shard_map/ppermute | solution.py:392
  12.8 0.2 collective-permute-done.gate1_ref
  13.0 1.3 %collective-permute-start.2 = (bf16[256,256]{1,0:T(8,128)(2,1)S(1)}, bf16[256,256]{1,0:T(8,128)(2,1)S(1)}, u32[]{:S(2)}, u32[]{:S(2)}) collective-permute-start(bf16[256,256]{1,0:T(8,128)(2,1)S(1)} %get-tuple-element.53), channel_id=1, source_target_pairs={{0,3},{1,2},{2,1},{3,0},{4,7},{5,6},{6,5},{7,4},{8,11},{9,10},{10,... | collective-permute-start | bytes 393224 | tf_op jit(solution)/shard_map/ppermute | solution.py:392
  14.3 0.0 copy-done
  14.3 0.1 dynamic-slice_bitcast_fusion
  14.4 0.1 copy.19.skip_ref
  14.5 3.0 %collective-permute-done.1.gate2_ref = bf16[256,256]{1,0:T(8,128)(2,1)S(1)} collective-permute-done((bf16[256,256]{1,0:T(8,128)(2,1)S(1)}, bf16[256,256]{1,0:T(8,128)(2,1)S(1)}, u32[]{:S(2)}, u32[]{:S(2)}) %collective-permute-start.1) | collective-permute-done | bytes 131104 | tf_op jit(solution)/shard_map/ppermute | solution.py:392
  17.5 1.3 %collective-permute-done.2.gate3_ref = bf16[256,256]{1,0:T(8,128)(2,1)S(1)} collective-permute-done((bf16[256,256]{1,0:T(8,128)(2,1)S(1)}, bf16[256,256]{1,0:T(8,128)(2,1)S(1)}, u32[]{:S(2)}, u32[]{:S(2)}) %collective-permute-start.2) | collective-permute-done | bytes 131104 | tf_op jit(solution)/shard_map/ppermute | solution.py:392
  18.8 5.8 %all-to-all-done.both_ref = bf16[8,2,32,512]{3,2,1,0:T(8,128)(2,1)S(1)} async-done(((bf16[8,2,32,512]{3,2,1,0:T(8,128)(2,1)}), bf16[8,2,32,512]{3,2,1,0:T(8,128)(2,1)S(1)}, u32[]{:S(2)}, u32[]{:S(2)}) %all-to-all-start) | async-done | bytes 524320 | tf_op jit(solution)/shard_map/all_to_all | solution.py:420
  24.6 0.0 copy-done.1
  24.6 0.0 copy-done.2
  24.6 3.0 %convolve.1 = bf16[8,2,32,256]{3,2,1,0:T(8,128)(2,1)S(1)} custom-call(s32[1]{0:T(128)} %bitcast.core_ref, bf16[8,2,32,512]{3,2,1,0:T(8,128)(2,1)S(1)} %all-to-all-done.both_ref, bf16[256,512]{1,0:T(8,128)(2,1)S(1)} %copy-done.1, bf16[256,512]{1,0:T(8,128)(2,1)S(1)} %copy-done.2, bf16[512,256]{1,0:T(8,128)(2,1)} %constant.32.clone.gh_hbm, ...), custom_call_target="tpu_custom_call" | custom-call | tf_op jit(solution)/shard_map/convolve/pallas_call | solution.py:437
  27.6 12.5 %all_to_all.10 = bf16[8,2,32,256]{3,2,1,0:T(8,128)(2,1)S(1)} all-to-all(bf16[8,2,32,256]{3,2,1,0:T(8,128)(2,1)S(1)} %convolve.1), channel_id=1, replica_groups=mesh['tm'=8,'x'=2,'core'=2] {'tm'}, dimensions={0} | all-to-all | bytes 524288 | tf_op jit(solution)/shard_map/all_to_all | solution.py:452
  40.1 0.1 collective-permute-start.5
  40.2 1.6 %collective-permute-start.3 = (bf16[8,32,256]{2,1,0:T(8,128)(2,1)S(1)}, bf16[8,32,256]{2,1,0:T(8,128)(2,1)S(1)}, u32[]{:S(2)}, u32[]{:S(2)}) collective-permute-start(bf16[8,32,256]{2,1,0:T(8,128)(2,1)S(1)} %get-tuple-element.52.conv0_ref), channel_id=1, source_target_pairs={{0,2},{1,3},{2,0},{3,1},{4,6},{5,7},{6,4},{7,5},{8,10},{9,11},{10,... | collective-permute-start | bytes 393224 | tf_op jit(solution)/shard_map/ppermute | solution.py:392
  41.8 0.0 collective-permute-done.6.wg1_hbm
  41.8 0.3 collective-permute-start.4
  42.1 0.0 collective-permute-done.7.wu1_hbm
  42.1 0.0 collective-permute-done.8.wd1_hbm
  42.1 0.0 collective-permute-done.5.conv1_ref
  42.1 2.9 %feed_first.1 = (bf16[2,256,256]{2,1,0:T(8,128)(2,1)S(1)}, f32[256,1]{1,0:T(8,128)S(1)}, f32[4,1,256]{2,1,0:T(1,128)S(1)}, f32[4,256,512]{2,1,0:T(8,128)S(1)}, b...) custom-call(s32[1]{0:T(128)} %bitcast.1.chip_ref, s32[1]{0:T(128)} %bitcast.core_ref, ...), custom_call_target="tpu_custom_call" | custom-call | tf_op jit(solution)/shard_map/feed_first/pallas_call | solution.py:469
  45.0 1.5 %collective-permute-done.3.conv2_ref = bf16[8,32,256]{2,1,0:T(8,128)(2,1)S(1)} collective-permute-done((bf16[8,32,256]{2,1,0:T(8,128)(2,1)S(1)}, bf16[8,32,256]{2,1,0:T(8,128)(2,1)S(1)}, u32[]{:S(2)}, u32[]{:S(2)}) %collective-permute-start.3) | collective-permute-done | bytes 131104 | tf_op jit(solution)/shard_map/ppermute | solution.py:392
  46.6 1.9 %collective-permute-done.4.conv3_ref = bf16[8,32,256]{2,1,0:T(8,128)(2,1)S(1)} collective-permute-done((bf16[8,32,256]{2,1,0:T(8,128)(2,1)S(1)}, bf16[8,32,256]{2,1,0:T(8,128)(2,1)S(1)}, u32[]{:S(2)}, u32[]{:S(2)}) %collective-permute-start.4) | collective-permute-done | bytes 131104 | tf_op jit(solution)/shard_map/ppermute | solution.py:392
  48.5 1.7 %feed_second.1 = (bf16[256,256]{1,0:T(8,128)(2,1)S(1)}, bf16[256,256]{1,0:T(8,128)(2,1)S(1)}, bf16[256,256]{1,0:T(8,128)(2,1)S(1)}, bf16[256,256]{1,0:T(8,128)(2,1)S(1)}) custom-call(s32[1]{0:T(128)} %bitcast.1.chip_ref, s32[1]{0:T(128)} %bitcast.core_ref, bf16[8,32,256]{2,1,0:T(8,128)(2,1)S(1)} %collective-permute-done.3.conv2_ref, ...), custom_call_target="tpu_custom_call" | custom-call | tf_op jit(solution)/shard_map/feed_second/pallas_call | solution.py:489
  50.2 0.3 collective-permute-start.10
  50.5 1.3 %collective-permute-start.11 = (bf16[256,256]{1,0:T(8,128)(2,1)S(1)}, bf16[256,256]{1,0:T(8,128)(2,1)S(1)}, u32[]{:S(2)}, u32[]{:S(2)}) collective-permute-start(bf16[256,256]{1,0:T(8,128)(2,1)S(1)} %get-tuple-element.50), channel_id=1, source_target_pairs={{0,3},{1,2},{2,1},{3,0},{4,7},{5,6},{6,5},{7,4},{8,11},{9,10},{10,... | collective-permute-start | bytes 393224 | tf_op jit(solution)/shard_map/ppermute | solution.py:392
  51.9 0.5 collective-permute-start.9
  52.4 0.0 collective-permute-done.10.core1_ref
  52.4 3.6 %collective-permute-done.11.side1_ref = bf16[256,256]{1,0:T(8,128)(2,1)S(1)} collective-permute-done((bf16[256,256]{1,0:T(8,128)(2,1)S(1)}, bf16[256,256]{1,0:T(8,128)(2,1)S(1)}, u32[]{:S(2)}, u32[]{:S(2)}) %collective-permute-start.11) | collective-permute-done | bytes 131104 | tf_op jit(solution)/shard_map/ppermute | solution.py:392
  56.0 3.2 %collective-permute-done.9.side_ref = bf16[256,256]{1,0:T(8,128)(2,1)S(1)} collective-permute-done((bf16[256,256]{1,0:T(8,128)(2,1)S(1)}, bf16[256,256]{1,0:T(8,128)(2,1)S(1)}, u32[]{:S(2)}, u32[]{:S(2)}) %collective-permute-start.9) | collective-permute-done | bytes 131104 | tf_op jit(solution)/shard_map/ppermute | solution.py:392
  59.2 0.8 %finish.1 = bf16[512,256]{1,0:T(8,128)(2,1)} custom-call(s32[1]{0:T(128)} %bitcast.core_ref, bf16[256,256]{1,0:T(8,128)(2,1)S(1)} %get-tuple-element.47.own_ref, bf16[256,256]{1,0:T(8,128)(2,1)S(1)} %collective-permute-done.9.side_ref, bf16[256,256]{1,0:T(8,128)(2,1)S(1)} %collective-permute-done.10.core1_ref, ...), custom_call_target="tpu_custom_call" | custom-call | tf_op jit(solution)/shard_map/finish/pallas_call | solution.py:498
  (2 shorter events, 0.0 us)
Async XLA Ops:
  0.0 14.3 %copy-start = (f32[256]{0:T(256)S(1)}, f32[256]{0:T(256)}, u32[]{:S(2)}) copy-start(f32[256]{0:T(256)} %param.23) | copy-start | bytes 3076
  0.0 24.6 %copy-start.1 = (bf16[256,512]{1,0:T(8,128)(2,1)S(1)}, bf16[256,512]{1,0:T(8,128)(2,1)}, u32[]{:S(2)}) copy-start(bf16[256,512]{1,0:T(8,128)(2,1)} %constant.30.clone.fh_ref) | copy-start | bytes 786436
  0.0 24.6 %copy-start.2 = (bf16[256,512]{1,0:T(8,128)(2,1)S(1)}, bf16[256,512]{1,0:T(8,128)(2,1)}, u32[]{:S(2)}) copy-start(bf16[256,512]{1,0:T(8,128)(2,1)} %constant.31.clone.fl_ref) | copy-start | bytes 786436
  0.0 10.1 %copy-start.3 = (bf16[1024,512]{1,0:T(8,128)(2,1)S(1)}, bf16[1024,512]{1,0:T(8,128)(2,1)}, u32[]{:S(2)}) copy-start(bf16[1024,512]{1,0:T(8,128)(2,1)} %wg0_hbm.1) | copy-start | bytes 3145732
  0.0 10.2 %copy-start.4 = (bf16[512,256]{1,0:T(8,128)(2,1)S(1)}, bf16[512,256]{1,0:T(8,128)(2,1)}, u32[]{:S(2)}) copy-start(bf16[512,256]{1,0:T(8,128)(2,1)} %param.17) | copy-start | bytes 786436
  2.8 21.8 %all-to-all-start = ((bf16[8,2,32,512]{3,2,1,0:T(8,128)(2,1)}), bf16[8,2,32,512]{3,2,1,0:T(8,128)(2,1)S(1)}, u32[]{:S(2)}, u32[]{:S(2)}) async-start(bf16[8,2,32,512]{3,2,1,0:T(8,128)(2,1)} %prepare.1), calls=%async_computation | async-start | bytes 1048576 | tf_op jit(solution)/shard_map/all_to_all | solution.py:420
  10.1 31.7 %collective-permute-start.6 = (bf16[1024,512]{1,0:T(8,128)(2,1)S(1)}, bf16[1024,512]{1,0:T(8,128)(2,1)}, u32[]{:S(2)}, u32[]{:S(2)}) collective-permute-start(bf16[1024,512]{1,0:T(8,128)(2,1)S(1)} %copy-done.3), channel_id=1, source_target_pairs={{0,1},{1,0},{2,3},{3,2},{4,5},{5,4},{6,7},{7,6},{8,9},{9,8},{10,11... | collective-permute-start | bytes 3145736 | tf_op jit(solution)/shard_map/ppermute | solution.py:392
  10.2 2.8 %collective-permute-start = (bf16[256,256]{1,0:T(8,128)(2,1)S(1)}, bf16[256,256]{1,0:T(8,128)(2,1)S(1)}, u32[]{:S(2)}, u32[]{:S(2)}) collective-permute-start(bf16[256,256]{1,0:T(8,128)(2,1)S(1)} %get-tuple-element.53), channel_id=1, source_target_pairs={{0,1},{1,0},{2,3},{3,2},{4,5},{5,4},{6,7},{7,6},{8,9},{9,8},{10,11... | collective-permute-start | bytes 393224 | tf_op jit(solution)/shard_map/ppermute | solution.py:392
  10.8 31.3 %collective-permute-start.7 = (bf16[1024,512]{1,0:T(8,128)(2,1)}, bf16[1024,512]{1,0:T(8,128)(2,1)}, u32[]{:S(2)}, u32[]{:S(2)}) collective-permute-start(bf16[1024,512]{1,0:T(8,128)(2,1)} %wu0_hbm.1), channel_id=1, source_target_pairs={{0,1},{1,0},{2,3},{3,2},{4,5},{5,4},{6,7},{7,6},{8,9},{9,8},{10,11... | collective-permute-start | bytes 3145736 | tf_op jit(solution)/shard_map/ppermute | solution.py:392
  10.8 31.2 %collective-permute-start.8 = (bf16[512,1024]{1,0:T(8,128)(2,1)}, bf16[512,1024]{1,0:T(8,128)(2,1)}, u32[]{:S(2)}, u32[]{:S(2)}) collective-permute-start(bf16[512,1024]{1,0:T(8,128)(2,1)} %wd0_hbm.1), channel_id=1, source_target_pairs={{0,1},{1,0},{2,3},{3,2},{4,5},{5,4},{6,7},{7,6},{8,9},{9,8},{10,11... | collective-permute-start | bytes 3145736 | tf_op jit(solution)/shard_map/ppermute | solution.py:392
  11.3 6.2 %collective-permute-start.1 = (bf16[256,256]{1,0:T(8,128)(2,1)S(1)}, bf16[256,256]{1,0:T(8,128)(2,1)S(1)}, u32[]{:S(2)}, u32[]{:S(2)}) collective-permute-start(bf16[256,256]{1,0:T(8,128)(2,1)S(1)} %get-tuple-element.29.gate0_ref), channel_id=1, source_target_pairs={{0,2},{1,3},{2,0},{3,1},{4,6},{5,7},{6,4},{7,5},{8,10},{9,11},{10,... | collective-permute-start | bytes 393224 | tf_op jit(solution)/shard_map/ppermute | solution.py:392
  13.0 5.8 %collective-permute-start.2 = (bf16[256,256]{1,0:T(8,128)(2,1)S(1)}, bf16[256,256]{1,0:T(8,128)(2,1)S(1)}, u32[]{:S(2)}, u32[]{:S(2)}) collective-permute-start(bf16[256,256]{1,0:T(8,128)(2,1)S(1)} %get-tuple-element.53), channel_id=1, source_target_pairs={{0,3},{1,2},{2,1},{3,0},{4,7},{5,6},{6,5},{7,4},{8,11},{9,10},{10,... | collective-permute-start | bytes 393224 | tf_op jit(solution)/shard_map/ppermute | solution.py:392
  40.1 2.0 %collective-permute-start.5 = (bf16[8,32,256]{2,1,0:T(8,128)(2,1)S(1)}, bf16[8,32,256]{2,1,0:T(8,128)(2,1)S(1)}, u32[]{:S(2)}, u32[]{:S(2)}) collective-permute-start(bf16[8,32,256]{2,1,0:T(8,128)(2,1)S(1)} %get-tuple-element.51), channel_id=1, source_target_pairs={{0,1},{1,0},{2,3},{3,2},{4,5},{5,4},{6,7},{7,6},{8,9},{9,8},{10,11... | collective-permute-start | bytes 393224 | tf_op jit(solution)/shard_map/ppermute | solution.py:392
  40.2 6.4 %collective-permute-start.3 = (bf16[8,32,256]{2,1,0:T(8,128)(2,1)S(1)}, bf16[8,32,256]{2,1,0:T(8,128)(2,1)S(1)}, u32[]{:S(2)}, u32[]{:S(2)}) collective-permute-start(bf16[8,32,256]{2,1,0:T(8,128)(2,1)S(1)} %get-tuple-element.52.conv0_ref), channel_id=1, source_target_pairs={{0,2},{1,3},{2,0},{3,1},{4,6},{5,7},{6,4},{7,5},{8,10},{9,11},{10,... | collective-permute-start | bytes 393224 | tf_op jit(solution)/shard_map/ppermute | solution.py:392
  41.8 6.7 %collective-permute-start.4 = (bf16[8,32,256]{2,1,0:T(8,128)(2,1)S(1)}, bf16[8,32,256]{2,1,0:T(8,128)(2,1)S(1)}, u32[]{:S(2)}, u32[]{:S(2)}) collective-permute-start(bf16[8,32,256]{2,1,0:T(8,128)(2,1)S(1)} %get-tuple-element.51), channel_id=1, source_target_pairs={{0,3},{1,2},{2,1},{3,0},{4,7},{5,6},{6,5},{7,4},{8,11},{9,10},{10,... | collective-permute-start | bytes 393224 | tf_op jit(solution)/shard_map/ppermute | solution.py:392
  50.2 2.2 %collective-permute-start.10 = (bf16[256,256]{1,0:T(8,128)(2,1)S(1)}, bf16[256,256]{1,0:T(8,128)(2,1)S(1)}, u32[]{:S(2)}, u32[]{:S(2)}) collective-permute-start(bf16[256,256]{1,0:T(8,128)(2,1)S(1)} %get-tuple-element.49), channel_id=1, source_target_pairs={{0,1},{1,0},{2,3},{3,2},{4,5},{5,4},{6,7},{7,6},{8,9},{9,8},{10,11... | collective-permute-start | bytes 393224 | tf_op jit(solution)/shard_map/ppermute | solution.py:392
  50.5 5.4 %collective-permute-start.11 = (bf16[256,256]{1,0:T(8,128)(2,1)S(1)}, bf16[256,256]{1,0:T(8,128)(2,1)S(1)}, u32[]{:S(2)}, u32[]{:S(2)}) collective-permute-start(bf16[256,256]{1,0:T(8,128)(2,1)S(1)} %get-tuple-element.50), channel_id=1, source_target_pairs={{0,3},{1,2},{2,1},{3,0},{4,7},{5,6},{6,5},{7,4},{8,11},{9,10},{10,... | collective-permute-start | bytes 393224 | tf_op jit(solution)/shard_map/ppermute | solution.py:392
  51.9 7.3 %collective-permute-start.9 = (bf16[256,256]{1,0:T(8,128)(2,1)S(1)}, bf16[256,256]{1,0:T(8,128)(2,1)S(1)}, u32[]{:S(2)}, u32[]{:S(2)}) collective-permute-start(bf16[256,256]{1,0:T(8,128)(2,1)S(1)} %get-tuple-element.48), channel_id=1, source_target_pairs={{0,2},{1,3},{2,0},{3,1},{4,6},{5,7},{6,4},{7,5},{8,10},{9,11},{10,... | collective-permute-start | bytes 393224 | tf_op jit(solution)/shard_map/ppermute | solution.py:392

commit v5 on v4

--- a/solution.py
+++ b/solution.py
@@ -301,14 +301,12 @@
     conv3_ref,
     gate2_ref,
     gate3_ref,
-    mixed_ref,
     square_ref,
     gain_ref,
     sums_ref,
     rest_ref,
     down_ref,
-    out0_ref,
-    out1_ref,
+    hidden_ref,
     out2_ref,
     out3_ref,
     ready_ref,
@@ -333,19 +331,29 @@
         up = scale * (sums_ref[2 * at + 1] + dot(ready, rest_ref[2 * at + 1]))
         parts.append((gate / (1.0 + jnp.exp(-gate)) * up).astype(bf16))
     hidden = jnp.concatenate(parts, axis=1)
-    for j, out_ref in ((2, out2_ref), (3, out3_ref), (1, out1_ref), (0, out0_ref)):
-        at = (2 * chip + core) ^ j
-        part = dot(hidden, down_ref[:, pl.ds(pl.multiple_of(at * width, width), width)])
-        if j < 2:
-            part = part + mixed_ref[j].astype(f32)
-        out_ref[...] = part.astype(bf16)
+    hidden_ref[...] = hidden
+    for j, out_ref in ((2, out2_ref), (3, out3_ref)):
+        out_ref[...] = piece(hidden, down_ref, (2 * chip + core) ^ j, width).astype(bf16)
+
+
+def piece(hidden, down_ref, at, width):
+    return dot(hidden, down_ref[:, pl.ds(pl.multiple_of(at * width, width), width)])
+
+
+def feed_third_kernel(chip_ref, core_ref, hidden_ref, down_ref, mixed_ref, out0_ref, out1_ref):
+    here = 2 * chip_ref[0] + core_ref[0]
+    width = out0_ref.shape[1]
+    hidden = hidden_ref[...]
+    for j, out_ref in ((1, out1_ref), (0, out0_ref)):
+        part = piece(hidden, down_ref, here ^ j, width) + mixed_ref[j].astype(f32)
+        out_ref[...] = part.astype(out_ref.dtype)
 
 
 def finish_kernel(core_ref, own_ref, side_ref, core1_ref, side1_ref, out_ref):
     block = own_ref.shape[0]
     same = pl.ds(pl.multiple_of(core_ref[0] * block, block), block)
     other = pl.ds(pl.multiple_of((1 - core_ref[0]) * block, block), block)
-    out_ref[same, :] = (own_ref[...].astype(f32) + side_ref[...].astype(f32)).astype(bf16)
+    out_ref[same, :] = (own_ref[...] + side_ref[...].astype(f32)).astype(bf16)
     out_ref[other, :] = (core1_ref[...].astype(f32) + side1_ref[...].astype(f32)).astype(bf16)
 
 
@@ -486,15 +494,28 @@
         *map(stay, (gain, w_gate, w_up, wg1, wu1, w_down, wd1)),
     )
     aside, across, kept = lax.optimization_barrier((aside, across, kept))
-    outs = pl.pallas_call(
+    mixed, *kept = kept
+    shape = jax.ShapeDtypeStruct((block, width), bf16)
+    hidden, *remote = pl.pallas_call(
         feed_second_kernel,
-        out_shape=[jax.ShapeDtypeStruct((block, width), bf16)] * 4,
-        in_specs=[whole(SMEM)] * 2 + [whole()] * 10,
-        out_specs=[whole()] * 4,
+        out_shape=[jax.ShapeDtypeStruct((block, 2 * w_gate.shape[1]), bf16), shape, shape],
+        in_specs=[whole(SMEM)] * 2 + [whole()] * 9,
+        out_specs=[whole()] * 3,
         scratch_shapes=[pltpu.VMEM((block, depth), bf16)],
         compiler_params=params(24),
         name="feed_second",
     )(*place, aside, across, *gates[2:], *kept)
+    side, side1 = swap(remote[0], 2), swap(remote[1], 3)
+    local = pl.pallas_call(
+        feed_third_kernel,
+        out_shape=[jax.ShapeDtypeStruct((block, width), f32), shape],
+        in_specs=[whole(SMEM)] * 2 + [whole()] * 3,
+        out_specs=[whole()] * 2,
+        compiler_params=params(16),
+        name="feed_third",
+    )(*place, hidden, kept[-1], mixed)
+    owned, lent = local
+    lent, side = lax.optimization_barrier((lent, side))
     return pl.pallas_call(
         finish_kernel,
         out_shape=jax.ShapeDtypeStruct((rows, width), bf16),
@@ -502,7 +523,7 @@
         out_specs=whole(),
         compiler_params=params(8),
         name="finish",
-    )(place[1], outs[0], swap(outs[2], 2), swap(outs[1], 1), swap(outs[3], 3))
+    )(place[1], owned, side, swap(lent, 1), side1)
 
 
 def solution(mesh):

time: 60.2 us -> 58.9 us (0.978)
  waiting for transfers between devices: 20.5 us -> 19.5 us
    ppermute x12, waiting for transfers between devices: 14.8 us -> 13.8 us  [swap(): lax.ppermute(values, ('x', 'core'), [(at, at ^ bits) for at in range(4)])]
  transfers between devices with their start and end apart: 13 -> 13, of which waited for: 8 -> 8; matrix products, arithmetic and copies ran while one was open for 0% -> 0% of each run, Pallas kernels for 10% -> 11%
where the time goes in v5:
time: 58.9 us; the launch traced here: 58.6 us
  waiting for transfers between devices  19.5 us (33%)
  starting transfers between devices  14.8 us (25%)
  blocking collectives  12.5 us (21%)
  Pallas kernels  10.5 us (18%)
  between operations  0.9 us (2%)
    ppermute x12, waiting for transfers between devices, swap(): lax.ppermute(values, ('x', 'core'), [(at, at ^ bits) for at in range(4)])  13.8 us
    all_to_all x1, blocking collectives, shards(): conv = lax.all_to_all(conv, 'tm', split_axis=0, concat_axis=0, tiled=True)  12.5 us
    ppermute x12, starting transfers between devices, swap(): lax.ppermute(values, ('x', 'core'), [(at, at ^ bits) for at in range(4)])  7.54 us
    all_to_all x1, starting transfers between devices, shards(): both = lax.all_to_all(made, 'tm', split_axis=0, concat_axis=0, tiled=True)  7.3 us
    all_to_all x1, waiting for transfers between devices, shards(): both = lax.all_to_all(made, 'tm', split_axis=0, concat_axis=0, tiled=True)  5.77 us
    pallas_call x1, Pallas kernels, shards(): pl.pallas_call(convolve_kernel, out_shape=jax.ShapeDtypeStruct((tm, 2, he...  2.99 us
    pallas_call x1, Pallas kernels, shards(): pl.pallas_call(feed_first_kernel, out_shape=[jax.ShapeDtypeStruct(*spec)...  2.93 us
    pallas_call x1, Pallas kernels, shards(): pl.pallas_call(prepare_kernel, out_shape=jax.ShapeDtypeStruct(shape, bf16...  1.97 us
  transfers between devices with their start and end apart: 13, of which 8 were waited for; matrix products, arithmetic and copies ran while one was open for 0% of the time, Pallas kernels for 11%

profile of v5, /device:TPU:0, one launch (start us, length us, event | category | flops | bytes accessed | tf_op | source)
XLA Modules:
  0.0 58.6 jit_solution(468675492793046567)
XLA Ops:
  0.0 0.0 copy-start
  0.0 0.0 copy-start.1
  0.0 0.0 copy-start.2
  0.0 0.0 copy-start.3
  0.0 0.0 copy-start.4
  0.8 2.0 %prepare.1 = bf16[8,2,32,512]{3,2,1,0:T(8,128)(2,1)} custom-call(s32[1]{0:T(128)S(6)} %copy.24.step_ref, s32[8]{0:T(128)} %flags_hbm.1, bf16[512,256]{1,0:T(8,128)(2,1)} %value_hbm.1, bf16[512,256]{1,0:T(8,128)(2,1)} %filter_hbm.1, f32[200,256]{1,0:T(8,128)} %table_hbm.1, f32[1,256]{1,0:T(1,128)} %bitcast.15), custom_call_target="tpu_custom_call" | custom-call | tf_op jit(solution)/shard_map/prepare/pallas_call | solution.py:404
  2.8 7.3 %all-to-all-start = ((bf16[8,2,32,512]{3,2,1,0:T(8,128)(2,1)}), bf16[8,2,32,512]{3,2,1,0:T(8,128)(2,1)S(1)}, u32[]{:S(2)}, u32[]{:S(2)}) async-start(bf16[8,2,32,512]{3,2,1,0:T(8,128)(2,1)} %prepare.1), calls=%async_computation | async-start | bytes 1048576 | tf_op jit(solution)/shard_map/all_to_all | solution.py:428
  10.1 0.0 copy-done.3
  10.1 0.1 collective-permute-start.6
  10.2 0.0 copy-done.4
  10.2 0.5 collective-permute-start
  10.8 0.1 collective-permute-start.7
  10.8 0.4 collective-permute-start.8
  11.3 1.5 %collective-permute-start.1 = (bf16[256,256]{1,0:T(8,128)(2,1)S(1)}, bf16[256,256]{1,0:T(8,128)(2,1)S(1)}, u32[]{:S(2)}, u32[]{:S(2)}) collective-permute-start(bf16[256,256]{1,0:T(8,128)(2,1)S(1)} %get-tuple-element.32.gate0_ref), channel_id=1, source_target_pairs={{0,2},{1,3},{2,0},{3,1},{4,6},{5,7},{6,4},{7,5},{8,10},{9,11},{10,... | collective-permute-start | bytes 393224 | tf_op jit(solution)/shard_map/ppermute | solution.py:400
  12.8 0.2 collective-permute-done.gate1_ref
  13.0 1.3 %collective-permute-start.2 = (bf16[256,256]{1,0:T(8,128)(2,1)S(1)}, bf16[256,256]{1,0:T(8,128)(2,1)S(1)}, u32[]{:S(2)}, u32[]{:S(2)}) collective-permute-start(bf16[256,256]{1,0:T(8,128)(2,1)S(1)} %get-tuple-element.59), channel_id=1, source_target_pairs={{0,3},{1,2},{2,1},{3,0},{4,7},{5,6},{6,5},{7,4},{8,11},{9,10},{10,... | collective-permute-start | bytes 393224 | tf_op jit(solution)/shard_map/ppermute | solution.py:400
  14.3 0.0 copy-done
  14.3 0.1 dynamic-slice_bitcast_fusion
  14.4 0.1 copy.19.skip_ref
  14.5 3.0 %collective-permute-done.1.gate2_ref = bf16[256,256]{1,0:T(8,128)(2,1)S(1)} collective-permute-done((bf16[256,256]{1,0:T(8,128)(2,1)S(1)}, bf16[256,256]{1,0:T(8,128)(2,1)S(1)}, u32[]{:S(2)}, u32[]{:S(2)}) %collective-permute-start.1) | collective-permute-done | bytes 131104 | tf_op jit(solution)/shard_map/ppermute | solution.py:400
  17.5 1.3 %collective-permute-done.2.gate3_ref = bf16[256,256]{1,0:T(8,128)(2,1)S(1)} collective-permute-done((bf16[256,256]{1,0:T(8,128)(2,1)S(1)}, bf16[256,256]{1,0:T(8,128)(2,1)S(1)}, u32[]{:S(2)}, u32[]{:S(2)}) %collective-permute-start.2) | collective-permute-done | bytes 131104 | tf_op jit(solution)/shard_map/ppermute | solution.py:400
  18.8 5.8 %all-to-all-done.both_ref = bf16[8,2,32,512]{3,2,1,0:T(8,128)(2,1)S(1)} async-done(((bf16[8,2,32,512]{3,2,1,0:T(8,128)(2,1)}), bf16[8,2,32,512]{3,2,1,0:T(8,128)(2,1)S(1)}, u32[]{:S(2)}, u32[]{:S(2)}) %all-to-all-start) | async-done | bytes 524320 | tf_op jit(solution)/shard_map/all_to_all | solution.py:428
  24.6 0.0 copy-done.1
  24.6 0.0 copy-done.2
  24.6 3.0 %convolve.1 = bf16[8,2,32,256]{3,2,1,0:T(8,128)(2,1)S(1)} custom-call(s32[1]{0:T(128)} %bitcast.core_ref, bf16[8,2,32,512]{3,2,1,0:T(8,128)(2,1)S(1)} %all-to-all-done.both_ref, bf16[256,512]{1,0:T(8,128)(2,1)S(1)} %copy-done.1, bf16[256,512]{1,0:T(8,128)(2,1)S(1)} %copy-done.2, bf16[512,256]{1,0:T(8,128)(2,1)} %constant.32.clone.gh_hbm, ...), custom_call_target="tpu_custom_call" | custom-call | tf_op jit(solution)/shard_map/convolve/pallas_call | solution.py:445
  27.6 12.5 %all_to_all.10 = bf16[8,2,32,256]{3,2,1,0:T(8,128)(2,1)S(1)} all-to-all(bf16[8,2,32,256]{3,2,1,0:T(8,128)(2,1)S(1)} %convolve.1), channel_id=1, replica_groups=mesh['tm'=8,'x'=2,'core'=2] {'tm'}, dimensions={0} | all-to-all | bytes 524288 | tf_op jit(solution)/shard_map/all_to_all | solution.py:460
  40.1 0.1 collective-permute-start.5
  40.2 1.6 %collective-permute-start.3 = (bf16[8,32,256]{2,1,0:T(8,128)(2,1)S(1)}, bf16[8,32,256]{2,1,0:T(8,128)(2,1)S(1)}, u32[]{:S(2)}, u32[]{:S(2)}) collective-permute-start(bf16[8,32,256]{2,1,0:T(8,128)(2,1)S(1)} %get-tuple-element.58.conv0_ref), channel_id=1, source_target_pairs={{0,2},{1,3},{2,0},{3,1},{4,6},{5,7},{6,4},{7,5},{8,10},{9,11},{10,... | collective-permute-start | bytes 393224 | tf_op jit(solution)/shard_map/ppermute | solution.py:400
  41.8 0.0 collective-permute-done.6.wg1_hbm
  41.8 0.3 collective-permute-start.4
  42.1 0.0 collective-permute-done.7.wu1_hbm
  42.1 0.0 collective-permute-done.8.wd1_hbm
  42.1 0.0 collective-permute-done.5.conv1_ref
  42.1 2.9 %feed_first.1 = (bf16[2,256,256]{2,1,0:T(8,128)(2,1)S(1)}, f32[256,1]{1,0:T(8,128)S(1)}, f32[4,1,256]{2,1,0:T(1,128)S(1)}, f32[4,256,512]{2,1,0:T(8,128)S(1)}, b...) custom-call(s32[1]{0:T(128)} %bitcast.1.chip_ref, s32[1]{0:T(128)} %bitcast.core_ref, ...), custom_call_target="tpu_custom_call" | custom-call | tf_op jit(solution)/shard_map/feed_first/pallas_call | solution.py:477
  45.0 1.5 %collective-permute-done.3.conv2_ref = bf16[8,32,256]{2,1,0:T(8,128)(2,1)S(1)} collective-permute-done((bf16[8,32,256]{2,1,0:T(8,128)(2,1)S(1)}, bf16[8,32,256]{2,1,0:T(8,128)(2,1)S(1)}, u32[]{:S(2)}, u32[]{:S(2)}) %collective-permute-start.3) | collective-permute-done | bytes 131104 | tf_op jit(solution)/shard_map/ppermute | solution.py:400
  46.6 1.9 %collective-permute-done.4.conv3_ref = bf16[8,32,256]{2,1,0:T(8,128)(2,1)S(1)} collective-permute-done((bf16[8,32,256]{2,1,0:T(8,128)(2,1)S(1)}, bf16[8,32,256]{2,1,0:T(8,128)(2,1)S(1)}, u32[]{:S(2)}, u32[]{:S(2)}) %collective-permute-start.4) | collective-permute-done | bytes 131104 | tf_op jit(solution)/shard_map/ppermute | solution.py:400
  48.5 1.4 %feed_second.1 = (bf16[256,1024]{1,0:T(8,128)(2,1)S(1)}, bf16[256,256]{1,0:T(8,128)(2,1)S(1)}, bf16[256,256]{1,0:T(8,128)(2,1)S(1)}) custom-call(s32[1]{0:T(128)} %bitcast.1.chip_ref, s32[1]{0:T(128)} %bitcast.core_ref, bf16[8,32,256]{2,1,0:T(8,128)(2,1)S(1)} %collective-permute-done.3.conv2_ref, bf16[8,32,256]{2,1,0:T(8,128)(2,1)S(1)} %collective-permute-done.4.conv3_ref, ...), custom_call_target="tpu_custom_call" | custom-call | tf_op jit(solution)/shard_map/feed_second/pallas_call | solution.py:499
  49.9 1.6 %collective-permute-start.9 = (bf16[256,256]{1,0:T(8,128)(2,1)S(1)}, bf16[256,256]{1,0:T(8,128)(2,1)S(1)}, u32[]{:S(2)}, u32[]{:S(2)}) collective-permute-start(bf16[256,256]{1,0:T(8,128)(2,1)S(1)} %get-tuple-element.53), channel_id=1, source_target_pairs={{0,2},{1,3},{2,0},{3,1},{4,6},{5,7},{6,4},{7,5},{8,10},{9,11},{10,... | collective-permute-start | bytes 393224 | tf_op jit(solution)/shard_map/ppermute | solution.py:400
  51.5 0.1 collective-permute-start.11
  51.6 0.5 feed_third.1
  52.1 4.2 %collective-permute-done.9.side_ref = bf16[256,256]{1,0:T(8,128)(2,1)S(1)} collective-permute-done((bf16[256,256]{1,0:T(8,128)(2,1)S(1)}, bf16[256,256]{1,0:T(8,128)(2,1)S(1)}, u32[]{:S(2)}, u32[]{:S(2)}) %collective-permute-start.9) | collective-permute-done | bytes 131104 | tf_op jit(solution)/shard_map/ppermute | solution.py:400
  56.3 0.0 collective-permute-start.10
  56.3 1.5 %collective-permute-done.11.side1_ref = bf16[256,256]{1,0:T(8,128)(2,1)S(1)} collective-permute-done((bf16[256,256]{1,0:T(8,128)(2,1)S(1)}, bf16[256,256]{1,0:T(8,128)(2,1)S(1)}, u32[]{:S(2)}, u32[]{:S(2)}) %collective-permute-start.11) | collective-permute-done | bytes 131104 | tf_op jit(solution)/shard_map/ppermute | solution.py:400
  57.8 0.0 collective-permute-done.10.core1_ref
  57.8 0.8 %finish.1 = bf16[512,256]{1,0:T(8,128)(2,1)} custom-call(s32[1]{0:T(128)} %bitcast.core_ref, f32[256,256]{1,0:T(8,128)S(1)} %get-tuple-element.51.own_ref, bf16[256,256]{1,0:T(8,128)(2,1)S(1)} %collective-permute-done.9.side_ref, bf16[256,256]{1,0:T(8,128)(2,1)S(1)} %collective-permute-done.10.core1_ref, bf16[256,256]{1,0:T(8,128)(2,1)S(1)} %collective-permute-done.11.side1_ref), custom_call_target="tpu_custom_call" | custom-call | tf_op jit(solution)/shard_map/finish/pallas_call | solution.py:519
  (2 shorter events, 0.0 us)
Async XLA Ops:
  0.0 14.3 %copy-start = (f32[256]{0:T(256)S(1)}, f32[256]{0:T(256)}, u32[]{:S(2)}) copy-start(f32[256]{0:T(256)} %param.23) | copy-start | bytes 3076
  0.0 24.6 %copy-start.1 = (bf16[256,512]{1,0:T(8,128)(2,1)S(1)}, bf16[256,512]{1,0:T(8,128)(2,1)}, u32[]{:S(2)}) copy-start(bf16[256,512]{1,0:T(8,128)(2,1)} %constant.30.clone.fh_ref) | copy-start | bytes 786436
  0.0 24.6 %copy-start.2 = (bf16[256,512]{1,0:T(8,128)(2,1)S(1)}, bf16[256,512]{1,0:T(8,128)(2,1)}, u32[]{:S(2)}) copy-start(bf16[256,512]{1,0:T(8,128)(2,1)} %constant.31.clone.fl_ref) | copy-start | bytes 786436
  0.0 10.1 %copy-start.3 = (bf16[1024,512]{1,0:T(8,128)(2,1)S(1)}, bf16[1024,512]{1,0:T(8,128)(2,1)}, u32[]{:S(2)}) copy-start(bf16[1024,512]{1,0:T(8,128)(2,1)} %wg0_hbm.1) | copy-start | bytes 3145732
  0.0 10.2 %copy-start.4 = (bf16[512,256]{1,0:T(8,128)(2,1)S(1)}, bf16[512,256]{1,0:T(8,128)(2,1)}, u32[]{:S(2)}) copy-start(bf16[512,256]{1,0:T(8,128)(2,1)} %param.17) | copy-start | bytes 786436
  2.8 21.8 %all-to-all-start = ((bf16[8,2,32,512]{3,2,1,0:T(8,128)(2,1)}), bf16[8,2,32,512]{3,2,1,0:T(8,128)(2,1)S(1)}, u32[]{:S(2)}, u32[]{:S(2)}) async-start(bf16[8,2,32,512]{3,2,1,0:T(8,128)(2,1)} %prepare.1), calls=%async_computation | async-start | bytes 1048576 | tf_op jit(solution)/shard_map/all_to_all | solution.py:428
  10.1 31.7 %collective-permute-start.6 = (bf16[1024,512]{1,0:T(8,128)(2,1)S(1)}, bf16[1024,512]{1,0:T(8,128)(2,1)}, u32[]{:S(2)}, u32[]{:S(2)}) collective-permute-start(bf16[1024,512]{1,0:T(8,128)(2,1)S(1)} %copy-done.3), channel_id=1, source_target_pairs={{0,1},{1,0},{2,3},{3,2},{4,5},{5,4},{6,7},{7,6},{8,9},{9,8},{10,11... | collective-permute-start | bytes 3145736 | tf_op jit(solution)/shard_map/ppermute | solution.py:400
  10.2 2.8 %collective-permute-start = (bf16[256,256]{1,0:T(8,128)(2,1)S(1)}, bf16[256,256]{1,0:T(8,128)(2,1)S(1)}, u32[]{:S(2)}, u32[]{:S(2)}) collective-permute-start(bf16[256,256]{1,0:T(8,128)(2,1)S(1)} %get-tuple-element.59), channel_id=1, source_target_pairs={{0,1},{1,0},{2,3},{3,2},{4,5},{5,4},{6,7},{7,6},{8,9},{9,8},{10,11... | collective-permute-start | bytes 393224 | tf_op jit(solution)/shard_map/ppermute | solution.py:400
  10.8 31.3 %collective-permute-start.7 = (bf16[1024,512]{1,0:T(8,128)(2,1)}, bf16[1024,512]{1,0:T(8,128)(2,1)}, u32[]{:S(2)}, u32[]{:S(2)}) collective-permute-start(bf16[1024,512]{1,0:T(8,128)(2,1)} %wu0_hbm.1), channel_id=1, source_target_pairs={{0,1},{1,0},{2,3},{3,2},{4,5},{5,4},{6,7},{7,6},{8,9},{9,8},{10,11... | collective-permute-start | bytes 3145736 | tf_op jit(solution)/shard_map/ppermute | solution.py:400
  10.8 31.2 %collective-permute-start.8 = (bf16[512,1024]{1,0:T(8,128)(2,1)}, bf16[512,1024]{1,0:T(8,128)(2,1)}, u32[]{:S(2)}, u32[]{:S(2)}) collective-permute-start(bf16[512,1024]{1,0:T(8,128)(2,1)} %wd0_hbm.1), channel_id=1, source_target_pairs={{0,1},{1,0},{2,3},{3,2},{4,5},{5,4},{6,7},{7,6},{8,9},{9,8},{10,11... | collective-permute-start | bytes 3145736 | tf_op jit(solution)/shard_map/ppermute | solution.py:400
  11.3 6.2 %collective-permute-start.1 = (bf16[256,256]{1,0:T(8,128)(2,1)S(1)}, bf16[256,256]{1,0:T(8,128)(2,1)S(1)}, u32[]{:S(2)}, u32[]{:S(2)}) collective-permute-start(bf16[256,256]{1,0:T(8,128)(2,1)S(1)} %get-tuple-element.32.gate0_ref), channel_id=1, source_target_pairs={{0,2},{1,3},{2,0},{3,1},{4,6},{5,7},{6,4},{7,5},{8,10},{9,11},{10,... | collective-permute-start | bytes 393224 | tf_op jit(solution)/shard_map/ppermute | solution.py:400
  13.0 5.8 %collective-permute-start.2 = (bf16[256,256]{1,0:T(8,128)(2,1)S(1)}, bf16[256,256]{1,0:T(8,128)(2,1)S(1)}, u32[]{:S(2)}, u32[]{:S(2)}) collective-permute-start(bf16[256,256]{1,0:T(8,128)(2,1)S(1)} %get-tuple-element.59), channel_id=1, source_target_pairs={{0,3},{1,2},{2,1},{3,0},{4,7},{5,6},{6,5},{7,4},{8,11},{9,10},{10,... | collective-permute-start | bytes 393224 | tf_op jit(solution)/shard_map/ppermute | solution.py:400
  40.1 2.0 %collective-permute-start.5 = (bf16[8,32,256]{2,1,0:T(8,128)(2,1)S(1)}, bf16[8,32,256]{2,1,0:T(8,128)(2,1)S(1)}, u32[]{:S(2)}, u32[]{:S(2)}) collective-permute-start(bf16[8,32,256]{2,1,0:T(8,128)(2,1)S(1)} %get-tuple-element.57), channel_id=1, source_target_pairs={{0,1},{1,0},{2,3},{3,2},{4,5},{5,4},{6,7},{7,6},{8,9},{9,8},{10,11... | collective-permute-start | bytes 393224 | tf_op jit(solution)/shard_map/ppermute | solution.py:400
  40.2 6.4 %collective-permute-start.3 = (bf16[8,32,256]{2,1,0:T(8,128)(2,1)S(1)}, bf16[8,32,256]{2,1,0:T(8,128)(2,1)S(1)}, u32[]{:S(2)}, u32[]{:S(2)}) collective-permute-start(bf16[8,32,256]{2,1,0:T(8,128)(2,1)S(1)} %get-tuple-element.58.conv0_ref), channel_id=1, source_target_pairs={{0,2},{1,3},{2,0},{3,1},{4,6},{5,7},{6,4},{7,5},{8,10},{9,11},{10,... | collective-permute-start | bytes 393224 | tf_op jit(solution)/shard_map/ppermute | solution.py:400
  41.8 6.7 %collective-permute-start.4 = (bf16[8,32,256]{2,1,0:T(8,128)(2,1)S(1)}, bf16[8,32,256]{2,1,0:T(8,128)(2,1)S(1)}, u32[]{:S(2)}, u32[]{:S(2)}) collective-permute-start(bf16[8,32,256]{2,1,0:T(8,128)(2,1)S(1)} %get-tuple-element.57), channel_id=1, source_target_pairs={{0,3},{1,2},{2,1},{3,0},{4,7},{5,6},{6,5},{7,4},{8,11},{9,10},{10,... | collective-permute-start | bytes 393224 | tf_op jit(solution)/shard_map/ppermute | solution.py:400
  49.9 6.4 %collective-permute-start.9 = (bf16[256,256]{1,0:T(8,128)(2,1)S(1)}, bf16[256,256]{1,0:T(8,128)(2,1)S(1)}, u32[]{:S(2)}, u32[]{:S(2)}) collective-permute-start(bf16[256,256]{1,0:T(8,128)(2,1)S(1)} %get-tuple-element.53), channel_id=1, source_target_pairs={{0,2},{1,3},{2,0},{3,1},{4,6},{5,7},{6,4},{7,5},{8,10},{9,11},{10,... | collective-permute-start | bytes 393224 | tf_op jit(solution)/shard_map/ppermute | solution.py:400
  51.5 6.3 %collective-permute-start.11 = (bf16[256,256]{1,0:T(8,128)(2,1)S(1)}, bf16[256,256]{1,0:T(8,128)(2,1)S(1)}, u32[]{:S(2)}, u32[]{:S(2)}) collective-permute-start(bf16[256,256]{1,0:T(8,128)(2,1)S(1)} %get-tuple-element.56), channel_id=1, source_target_pairs={{0,3},{1,2},{2,1},{3,0},{4,7},{5,6},{6,5},{7,4},{8,11},{9,10},{10,... | collective-permute-start | bytes 393224 | tf_op jit(solution)/shard_map/ppermute | solution.py:400
  56.3 1.5 %collective-permute-start.10 = (bf16[256,256]{1,0:T(8,128)(2,1)S(1)}, bf16[256,256]{1,0:T(8,128)(2,1)S(1)}, u32[]{:S(2)}, u32[]{:S(2)}) collective-permute-start(bf16[256,256]{1,0:T(8,128)(2,1)S(1)} %get-tuple-element.55), channel_id=1, source_target_pairs={{0,1},{1,0},{2,3},{3,2},{4,5},{5,4},{6,7},{7,6},{8,9},{9,8},{10,11... | collective-permute-start | bytes 393224 | tf_op jit(solution)/shard_map/ppermute | solution.py:400

commit v6 on v5

--- a/solution.py
+++ b/solution.py
@@ -219,18 +219,16 @@
         store.wait()
 
 
-def mix(conv_refs, gate_refs, chip, core, mixed_ref, ready_ref, gain_ref, square):
+def mix(conv_refs, gate_refs, ats, mixed_ref, ready_ref, gain_ref, square):
     rows, width = gate_refs[0].shape
-    for j, (conv_ref, gate_ref) in enumerate(zip(conv_refs, gate_refs)):
-        at = core ^ j
+    for j, (conv_ref, gate_ref, at) in enumerate(zip(conv_refs, gate_refs, ats)):
         conv = conv_ref[...].reshape(width, rows).T.astype(f32)
         mixed = (gate_ref[...].astype(f32) * conv).astype(bf16)
-        if mixed_ref is not None:
-            mixed_ref[j] = mixed
+        if j == 0:
+            mixed_ref[...] = mixed
         wide = mixed.astype(f32)
         square = square + jnp.sum(wide * wide, axis=-1, keepdims=True)
-        lanes = pl.ds(pl.multiple_of(at * width, width), width)
-        ready_ref[:, lanes] = (wide * gain_ref[2 * chip + at]).astype(bf16)
+        ready_ref[:, j * width : (j + 1) * width] = (wide * gain_ref[at]).astype(bf16)
     return square
 
 
@@ -238,9 +236,7 @@
     chip_ref,
     core_ref,
     conv0_ref,
-    conv1_ref,
     gate0_ref,
-    gate1_ref,
     gain_hbm,
     wg0_hbm,
     wu0_hbm,
@@ -258,29 +254,33 @@
     now_ref,
     sems,
 ):
-    chip, core = chip_ref[0], core_ref[0]
-    depth = now_ref.shape[1]
+    here = 2 * chip_ref[0] + core_ref[0]
+    rows, width = gate0_ref.shape
     hidden = wd0_hbm.shape[0]
-    here = pl.ds(pl.multiple_of(chip * depth, depth), depth)
-    there = pl.ds(pl.multiple_of((1 - chip) * depth, depth), depth)
     weights = (wg0_hbm, wu0_hbm, wg1_hbm, wu1_hbm)
+
+    def source(weight, j):
+        return weight.at[pl.ds(pl.multiple_of((here ^ j) * width, width), width)]
+
     loads = start_loads(
         [(gain_hbm, gain_ref)]
-        + [(weight.at[here], now_ref.at[at]) for at, weight in enumerate(weights)]
-        + [(weight.at[there], rest_ref.at[at]) for at, weight in enumerate(weights)]
+        + [(source(weight, 0), now_ref.at[at]) for at, weight in enumerate(weights)]
+        + [
+            (source(weight, j), rest_ref.at[at, pl.ds((j - 1) * width, width)])
+            for j in (1, 2, 3)
+            for at, weight in enumerate(weights)
+        ]
         + [
             (weight, down_ref.at[pl.ds(at * hidden, hidden)])
             for at, weight in enumerate((wd0_hbm, wd1_hbm))
         ],
         sems,
     )
-    rows = gate0_ref.shape[0]
     loads[0].wait()
     square_ref[...] = mix(
-        (conv0_ref, conv1_ref),
-        (gate0_ref, gate1_ref),
-        chip,
-        core,
+        (conv0_ref,),
+        (gate0_ref,),
+        (here,),
         mixed_ref,
         ready_ref,
         gain_ref,
@@ -297,8 +297,10 @@
 def feed_second_kernel(
     chip_ref,
     core_ref,
+    conv1_ref,
     conv2_ref,
     conv3_ref,
+    gate1_ref,
     gate2_ref,
     gate3_ref,
     square_ref,
@@ -306,19 +308,19 @@
     sums_ref,
     rest_ref,
     down_ref,
+    mixed_ref,
     hidden_ref,
     out2_ref,
     out3_ref,
     ready_ref,
 ):
-    chip, core = chip_ref[0], core_ref[0]
-    rows, width = gate2_ref.shape
+    here = 2 * chip_ref[0] + core_ref[0]
+    width = gate1_ref.shape[1]
     square = mix(
-        (conv2_ref, conv3_ref),
-        (gate2_ref, gate3_ref),
-        1 - chip,
-        core,
-        None,
+        (conv1_ref, conv2_ref, conv3_ref),
+        (gate1_ref, gate2_ref, gate3_ref),
+        (here ^ 1, here ^ 2, here ^ 3),
+        mixed_ref,
         ready_ref,
         gain_ref,
         square_ref[...],
@@ -333,19 +335,21 @@
     hidden = jnp.concatenate(parts, axis=1)
     hidden_ref[...] = hidden
     for j, out_ref in ((2, out2_ref), (3, out3_ref)):
-        out_ref[...] = piece(hidden, down_ref, (2 * chip + core) ^ j, width).astype(bf16)
+        out_ref[...] = piece(hidden, down_ref, here ^ j, width).astype(bf16)
 
 
 def piece(hidden, down_ref, at, width):
     return dot(hidden, down_ref[:, pl.ds(pl.multiple_of(at * width, width), width)])
 
 
-def feed_third_kernel(chip_ref, core_ref, hidden_ref, down_ref, mixed_ref, out0_ref, out1_ref):
+def feed_third_kernel(
+    chip_ref, core_ref, hidden_ref, down_ref, mixed0_ref, mixed1_ref, out0_ref, out1_ref
+):
     here = 2 * chip_ref[0] + core_ref[0]
     width = out0_ref.shape[1]
     hidden = hidden_ref[...]
-    for j, out_ref in ((1, out1_ref), (0, out0_ref)):
-        part = piece(hidden, down_ref, here ^ j, width) + mixed_ref[j].astype(f32)
+    for j, mixed_ref, out_ref in ((1, mixed1_ref, out1_ref), (0, mixed0_ref, out0_ref)):
+        part = piece(hidden, down_ref, here ^ j, width) + mixed_ref[...].astype(f32)
         out_ref[...] = part.astype(out_ref.dtype)
 
 
@@ -394,7 +398,6 @@
     rows, width = series_value.shape
     own = width // tm
     block = rows // 2
-    depth = 2 * width
 
     def swap(values, bits):
         return lax.ppermute(values, ("x", "core"), [(at, at ^ bits) for at in range(4)])
@@ -459,61 +462,60 @@
 
     conv = lax.all_to_all(conv, "tm", split_axis=0, concat_axis=0, tiled=True)
     mine, theirs = conv[:, 0], conv[:, 1]
-    aside, across, beside = swap(mine, 2), swap(theirs, 3), swap(theirs, 1)
-
-    if not direct:
-        mine, beside, aside, across = (
-            values.reshape(1, width, block) for values in (mine, beside, aside, across)
-        )
+    aside, across = swap(mine, 2), swap(theirs, 3)
+
+    def view(values):
+        return values if direct else values.reshape(1, width, block)
+
     gain = norm_gain.reshape(4, 1, width)
     held = [
-        ((2, block, width), bf16),
+        ((block, width), bf16),
         ((block, 1), f32),
         ((4, 1, width), f32),
         ((4, block, w_gate.shape[1]), f32),
-        ((4, depth, w_gate.shape[1]), bf16),
+        ((4, 3 * width, w_gate.shape[1]), bf16),
         ((2 * w_down.shape[0], w_down.shape[1]), bf16),
     ]
     kept = pl.pallas_call(
         feed_first_kernel,
         out_shape=[jax.ShapeDtypeStruct(*spec) for spec in held],
-        in_specs=[whole(SMEM)] * 2 + [whole()] * 4 + [whole(HBM)] * 7,
+        in_specs=[whole(SMEM)] * 2 + [whole()] * 2 + [whole(HBM)] * 7,
         out_specs=[whole()] * 6,
         scratch_shapes=[
-            pltpu.VMEM((block, depth), bf16),
-            pltpu.VMEM((4, depth, w_gate.shape[1]), bf16),
-            pltpu.SemaphoreType.DMA((11,)),
+            pltpu.VMEM((block, width), bf16),
+            pltpu.VMEM((4, width, w_gate.shape[1]), bf16),
+            pltpu.SemaphoreType.DMA((19,)),
         ],
         compiler_params=params(24),
         name="feed_first",
     )(
         *place,
-        mine,
-        beside,
-        *gates[:2],
+        view(mine),
+        gates[0],
         *map(stay, (gain, w_gate, w_up, wg1, wu1, w_down, wd1)),
     )
-    aside, across, kept = lax.optimization_barrier((aside, across, kept))
-    mixed, *kept = kept
+    theirs, aside, kept = lax.optimization_barrier((theirs, aside, kept))
+    beside = swap(theirs, 1)
+    mixed0, *kept = kept
     shape = jax.ShapeDtypeStruct((block, width), bf16)
-    hidden, *remote = pl.pallas_call(
+    mixed1, hidden, *remote = pl.pallas_call(
         feed_second_kernel,
-        out_shape=[jax.ShapeDtypeStruct((block, 2 * w_gate.shape[1]), bf16), shape, shape],
-        in_specs=[whole(SMEM)] * 2 + [whole()] * 9,
-        out_specs=[whole()] * 3,
-        scratch_shapes=[pltpu.VMEM((block, depth), bf16)],
+        out_shape=[shape, jax.ShapeDtypeStruct((block, 2 * w_gate.shape[1]), bf16), shape, shape],
+        in_specs=[whole(SMEM)] * 2 + [whole()] * 11,
+        out_specs=[whole()] * 4,
+        scratch_shapes=[pltpu.VMEM((block, 3 * width), bf16)],
         compiler_params=params(24),
         name="feed_second",
-    )(*place, aside, across, *gates[2:], *kept)
+    )(*place, *map(view, (beside, aside, across)), *gates[1:], *kept)
     side, side1 = swap(remote[0], 2), swap(remote[1], 3)
     local = pl.pallas_call(
         feed_third_kernel,
         out_shape=[jax.ShapeDtypeStruct((block, width), f32), shape],
-        in_specs=[whole(SMEM)] * 2 + [whole()] * 3,
+        in_specs=[whole(SMEM)] * 2 + [whole()] * 4,
         out_specs=[whole()] * 2,
         compiler_params=params(16),
         name="feed_third",
-    )(*place, hidden, kept[-1], mixed)
+    )(*place, hidden, kept[-1], mixed0, mixed1)
     owned, lent = local
     lent, side = lax.optimization_barrier((lent, side))
     return pl.pallas_call(

time: 58.9 us -> 58.2 us (0.988)
  starting transfers between devices: 14.8 us -> 13.5 us
    ppermute x12, starting transfers between devices: 7.54 us -> 6.17 us  [swap(): lax.ppermute(values, ('x', 'core'), [(at, at ^ bits) for at in range(4)])]
  transfers between devices with their start and end apart: 13 -> 13, of which waited for: 8 -> 7; matrix products, arithmetic and copies ran while one was open for 0% -> 0% of each run, Pallas kernels for 11% -> 11%
where the time goes in v6:
time: 58.2 us; the launch traced here: 57.9 us
  waiting for transfers between devices  19.9 us (34%)
  starting transfers between devices  13.5 us (23%)
  blocking collectives  12.5 us (21%)
  Pallas kernels  10.8 us (19%)
  between operations  0.89 us (2%)
    ppermute x12, waiting for transfers between devices, swap(): lax.ppermute(values, ('x', 'core'), [(at, at ^ bits) for at in range(4)])  14 us
    all_to_all x1, blocking collectives, shards(): conv = lax.all_to_all(conv, 'tm', split_axis=0, concat_axis=0, tiled=True)  12.5 us
    all_to_all x1, starting transfers between devices, shards(): both = lax.all_to_all(made, 'tm', split_axis=0, concat_axis=0, tiled=True)  7.3 us
    ppermute x12, starting transfers between devices, swap(): lax.ppermute(values, ('x', 'core'), [(at, at ^ bits) for at in range(4)])  6.17 us
    all_to_all x1, waiting for transfers between devices, shards(): both = lax.all_to_all(made, 'tm', split_axis=0, concat_axis=0, tiled=True)  5.93 us
    pallas_call x1, Pallas kernels, shards(): pl.pallas_call(feed_first_kernel, out_shape=[jax.ShapeDtypeStruct(*spec)...  3 us
    pallas_call x1, Pallas kernels, shards(): pl.pallas_call(convolve_kernel, out_shape=jax.ShapeDtypeStruct((tm, 2, he...  2.99 us
    pallas_call x1, Pallas kernels, shards(): pl.pallas_call(prepare_kernel, out_shape=jax.ShapeDtypeStruct(shape, bf16...  1.97 us
  transfers between devices with their start and end apart: 13, of which 7 were waited for; matrix products, arithmetic and copies ran while one was open for 0% of the time, Pallas kernels for 11%

profile of v6, /device:TPU:0, one launch (start us, length us, event | category | flops | bytes accessed | tf_op | source)
XLA Modules:
  0.0 57.9 jit_solution(7491326044370616390)
XLA Ops:
  0.0 0.0 copy-start
  0.0 0.0 copy-start.1
  0.0 0.0 copy-start.2
  0.0 0.0 copy-start.4
  0.0 0.0 copy-start.3
  0.8 2.0 %prepare.1 = bf16[8,2,32,512]{3,2,1,0:T(8,128)(2,1)} custom-call(s32[1]{0:T(128)S(6)} %copy.24.step_ref, s32[8]{0:T(128)} %flags_hbm.1, bf16[512,256]{1,0:T(8,128)(2,1)} %value_hbm.1, bf16[512,256]{1,0:T(8,128)(2,1)} %filter_hbm.1, f32[200,256]{1,0:T(8,128)} %table_hbm.1, f32[1,256]{1,0:T(1,128)} %bitcast.15), custom_call_target="tpu_custom_call" | custom-call | tf_op jit(solution)/shard_map/prepare/pallas_call | solution.py:407
  2.8 7.3 %all-to-all-start = ((bf16[8,2,32,512]{3,2,1,0:T(8,128)(2,1)}), bf16[8,2,32,512]{3,2,1,0:T(8,128)(2,1)S(1)}, u32[]{:S(2)}, u32[]{:S(2)}) async-start(bf16[8,2,32,512]{3,2,1,0:T(8,128)(2,1)} %prepare.1), calls=%async_computation | async-start | bytes 1048576 | tf_op jit(solution)/shard_map/all_to_all | solution.py:431
  10.1 0.0 copy-done.4
  10.1 0.1 collective-permute-start
  10.2 0.0 copy-done.3
  10.2 0.5 collective-permute-start.4
  10.7 0.1 collective-permute-start.5
  10.8 0.4 collective-permute-start.6
  11.2 1.5 %collective-permute-start.1 = (bf16[256,256]{1,0:T(8,128)(2,1)S(1)}, bf16[256,256]{1,0:T(8,128)(2,1)S(1)}, u32[]{:S(2)}, u32[]{:S(2)}) collective-permute-start(bf16[256,256]{1,0:T(8,128)(2,1)S(1)} %get-tuple-element.33.gate0_ref), channel_id=1, source_target_pairs={{0,2},{1,3},{2,0},{3,1},{4,6},{5,7},{6,4},{7,5},{8,10},{9,11},{10,... | collective-permute-start | bytes 393224 | tf_op jit(solution)/shard_map/ppermute | solution.py:403
  12.7 0.0 collective-permute-done.gate1_ref
  12.7 0.1 collective-permute-start.2
  12.8 0.0 copy-done
  12.8 0.1 dynamic-slice_bitcast_fusion
  12.9 0.1 copy.19.skip_ref
  12.9 4.6 %collective-permute-done.1.gate2_ref = bf16[256,256]{1,0:T(8,128)(2,1)S(1)} collective-permute-done((bf16[256,256]{1,0:T(8,128)(2,1)S(1)}, bf16[256,256]{1,0:T(8,128)(2,1)S(1)}, u32[]{:S(2)}, u32[]{:S(2)}) %collective-permute-start.1) | collective-permute-done | bytes 131104 | tf_op jit(solution)/shard_map/ppermute | solution.py:403
  17.6 1.1 %collective-permute-done.2.gate3_ref = bf16[256,256]{1,0:T(8,128)(2,1)S(1)} collective-permute-done((bf16[256,256]{1,0:T(8,128)(2,1)S(1)}, bf16[256,256]{1,0:T(8,128)(2,1)S(1)}, u32[]{:S(2)}, u32[]{:S(2)}) %collective-permute-start.2) | collective-permute-done | bytes 131104 | tf_op jit(solution)/shard_map/ppermute | solution.py:403
  18.6 5.9 %all-to-all-done.both_ref = bf16[8,2,32,512]{3,2,1,0:T(8,128)(2,1)S(1)} async-done(((bf16[8,2,32,512]{3,2,1,0:T(8,128)(2,1)}), bf16[8,2,32,512]{3,2,1,0:T(8,128)(2,1)S(1)}, u32[]{:S(2)}, u32[]{:S(2)}) %all-to-all-start) | async-done | bytes 524320 | tf_op jit(solution)/shard_map/all_to_all | solution.py:431
  24.6 0.0 copy-done.1
  24.6 0.0 copy-done.2
  24.6 3.0 %convolve.1 = bf16[8,2,32,256]{3,2,1,0:T(8,128)(2,1)S(1)} custom-call(s32[1]{0:T(128)} %bitcast.core_ref, bf16[8,2,32,512]{3,2,1,0:T(8,128)(2,1)S(1)} %all-to-all-done.both_ref, bf16[256,512]{1,0:T(8,128)(2,1)S(1)} %copy-done.1, bf16[256,512]{1,0:T(8,128)(2,1)S(1)} %copy-done.2, bf16[512,256]{1,0:T(8,128)(2,1)} %constant.32.clone.gh_hbm, ...), custom_call_target="tpu_custom_call" | custom-call | tf_op jit(solution)/shard_map/convolve/pallas_call | solution.py:448
  27.6 12.5 %all_to_all.10 = bf16[8,2,32,256]{3,2,1,0:T(8,128)(2,1)S(1)} all-to-all(bf16[8,2,32,256]{3,2,1,0:T(8,128)(2,1)S(1)} %convolve.1), channel_id=1, replica_groups=mesh['tm'=8,'x'=2,'core'=2] {'tm'}, dimensions={0} | all-to-all | bytes 524288 | tf_op jit(solution)/shard_map/all_to_all | solution.py:463
  40.1 1.6 %collective-permute-start.3 = (bf16[8,32,256]{2,1,0:T(8,128)(2,1)S(1)}, bf16[8,32,256]{2,1,0:T(8,128)(2,1)S(1)}, u32[]{:S(2)}, u32[]{:S(2)}) collective-permute-start(bf16[8,32,256]{2,1,0:T(8,128)(2,1)S(1)} %get-tuple-element.59.conv0_ref), channel_id=1, source_target_pairs={{0,2},{1,3},{2,0},{3,1},{4,6},{5,7},{6,4},{7,5},{8,10},{9,11},{10,... | collective-permute-start | bytes 393224 | tf_op jit(solution)/shard_map/ppermute | solution.py:403
  41.7 0.0 collective-permute-start.8
  41.7 0.0 collective-permute-done.4.wg1_hbm
  41.7 0.0 collective-permute-done.5.wu1_hbm
  41.7 0.0 collective-permute-done.6.wd1_hbm
  41.7 3.0 %feed_first.1 = (bf16[256,256]{1,0:T(8,128)(2,1)S(1)}, f32[256,1]{1,0:T(8,128)S(1)}, f32[4,1,256]{2,1,0:T(1,128)S(1)}, f32[4,256,512]{2,1,0:T(8,128)S(1)}, bf16[...) custom-call(s32[1]{0:T(128)} %bitcast.1.chip_ref, s32[1]{0:T(128)} %bitcast.core_ref, ...), custom_call_target="tpu_custom_call" | custom-call | tf_op jit(solution)/shard_map/feed_first/pallas_call | solution.py:479
  44.7 0.9 %collective-permute-done.3.conv2_ref = bf16[8,32,256]{2,1,0:T(8,128)(2,1)S(1)} collective-permute-done((bf16[8,32,256]{2,1,0:T(8,128)(2,1)S(1)}, bf16[8,32,256]{2,1,0:T(8,128)(2,1)S(1)}, u32[]{:S(2)}, u32[]{:S(2)}) %collective-permute-start.3) | collective-permute-done | bytes 131104 | tf_op jit(solution)/shard_map/ppermute | solution.py:403
  45.7 0.0 collective-permute-start.7
  45.7 1.8 %collective-permute-done.8.conv3_ref = bf16[8,32,256]{2,1,0:T(8,128)(2,1)S(1)} collective-permute-done((bf16[8,32,256]{2,1,0:T(8,128)(2,1)S(1)}, bf16[8,32,256]{2,1,0:T(8,128)(2,1)S(1)}, u32[]{:S(2)}, u32[]{:S(2)}) %collective-permute-start.8) | collective-permute-done | bytes 131104 | tf_op jit(solution)/shard_map/ppermute | solution.py:403
  47.5 0.0 collective-permute-done.7.conv1_ref
  47.5 1.7 %feed_second.1 = (bf16[256,256]{1,0:T(8,128)(2,1)S(1)}, bf16[256,1024]{1,0:T(8,128)(2,1)S(1)}, bf16[256,256]{1,0:T(8,128)(2,1)S(1)}, bf16[256,256]{1,0:T(8,128)(2,1)S(1)}) custom-call(s32[1]{0:T(128)} %bitcast.1.chip_ref, s32[1]{0:T(128)} %bitcast.core_ref, bf16[8,32,256]{2,1,0:T(8,128)(2,1)S(1)} %collective-permute-done.7.conv1_ref, ...), custom_call_target="tpu_custom_call" | custom-call | tf_op jit(solution)/shard_map/feed_second/pallas_call | solution.py:501
  49.1 2.0 %collective-permute-start.9 = (bf16[256,256]{1,0:T(8,128)(2,1)S(1)}, bf16[256,256]{1,0:T(8,128)(2,1)S(1)}, u32[]{:S(2)}, u32[]{:S(2)}) collective-permute-start(bf16[256,256]{1,0:T(8,128)(2,1)S(1)} %get-tuple-element.55), channel_id=1, source_target_pairs={{0,2},{1,3},{2,0},{3,1},{4,6},{5,7},{6,4},{7,5},{8,10},{9,11},{10,... | collective-permute-start | bytes 393224 | tf_op jit(solution)/shard_map/ppermute | solution.py:403
  51.1 0.0 collective-permute-start.11
  51.1 0.5 feed_third.1
  51.6 3.9 %collective-permute-done.9.side_ref = bf16[256,256]{1,0:T(8,128)(2,1)S(1)} collective-permute-done((bf16[256,256]{1,0:T(8,128)(2,1)S(1)}, bf16[256,256]{1,0:T(8,128)(2,1)S(1)}, u32[]{:S(2)}, u32[]{:S(2)}) %collective-permute-start.9) | collective-permute-done | bytes 131104 | tf_op jit(solution)/shard_map/ppermute | solution.py:403
  55.5 0.0 collective-permute-start.10
  55.5 1.6 %collective-permute-done.11.side1_ref = bf16[256,256]{1,0:T(8,128)(2,1)S(1)} collective-permute-done((bf16[256,256]{1,0:T(8,128)(2,1)S(1)}, bf16[256,256]{1,0:T(8,128)(2,1)S(1)}, u32[]{:S(2)}, u32[]{:S(2)}) %collective-permute-start.11) | collective-permute-done | bytes 131104 | tf_op jit(solution)/shard_map/ppermute | solution.py:403
  57.1 0.0 collective-permute-done.10.core1_ref
  57.1 0.8 %finish.1 = bf16[512,256]{1,0:T(8,128)(2,1)} custom-call(s32[1]{0:T(128)} %bitcast.core_ref, f32[256,256]{1,0:T(8,128)S(1)} %get-tuple-element.53.own_ref, bf16[256,256]{1,0:T(8,128)(2,1)S(1)} %collective-permute-done.9.side_ref, bf16[256,256]{1,0:T(8,128)(2,1)S(1)} %collective-permute-done.10.core1_ref, bf16[256,256]{1,0:T(8,128)(2,1)S(1)} %collective-permute-done.11.side1_ref), custom_call_target="tpu_custom_call" | custom-call | tf_op jit(solution)/shard_map/finish/pallas_call | solution.py:521
  (2 shorter events, 0.0 us)
Async XLA Ops:
  0.0 12.8 %copy-start = (f32[256]{0:T(256)S(1)}, f32[256]{0:T(256)}, u32[]{:S(2)}) copy-start(f32[256]{0:T(256)} %param.23) | copy-start | bytes 3076
  0.0 24.6 %copy-start.1 = (bf16[256,512]{1,0:T(8,128)(2,1)S(1)}, bf16[256,512]{1,0:T(8,128)(2,1)}, u32[]{:S(2)}) copy-start(bf16[256,512]{1,0:T(8,128)(2,1)} %constant.30.clone.fh_ref) | copy-start | bytes 786436
  0.0 24.6 %copy-start.2 = (bf16[256,512]{1,0:T(8,128)(2,1)S(1)}, bf16[256,512]{1,0:T(8,128)(2,1)}, u32[]{:S(2)}) copy-start(bf16[256,512]{1,0:T(8,128)(2,1)} %constant.31.clone.fl_ref) | copy-start | bytes 786436
  0.0 10.1 %copy-start.4 = (bf16[512,256]{1,0:T(8,128)(2,1)S(1)}, bf16[512,256]{1,0:T(8,128)(2,1)}, u32[]{:S(2)}) copy-start(bf16[512,256]{1,0:T(8,128)(2,1)} %param.17) | copy-start | bytes 786436
  0.0 10.2 %copy-start.3 = (bf16[1024,512]{1,0:T(8,128)(2,1)S(1)}, bf16[1024,512]{1,0:T(8,128)(2,1)}, u32[]{:S(2)}) copy-start(bf16[1024,512]{1,0:T(8,128)(2,1)} %wg0_hbm.1) | copy-start | bytes 3145732
  2.8 21.8 %all-to-all-start = ((bf16[8,2,32,512]{3,2,1,0:T(8,128)(2,1)}), bf16[8,2,32,512]{3,2,1,0:T(8,128)(2,1)S(1)}, u32[]{:S(2)}, u32[]{:S(2)}) async-start(bf16[8,2,32,512]{3,2,1,0:T(8,128)(2,1)} %prepare.1), calls=%async_computation | async-start | bytes 1048576 | tf_op jit(solution)/shard_map/all_to_all | solution.py:431
  10.1 2.6 %collective-permute-start = (bf16[256,256]{1,0:T(8,128)(2,1)S(1)}, bf16[256,256]{1,0:T(8,128)(2,1)S(1)}, u32[]{:S(2)}, u32[]{:S(2)}) collective-permute-start(bf16[256,256]{1,0:T(8,128)(2,1)S(1)} %get-tuple-element.61), channel_id=1, source_target_pairs={{0,1},{1,0},{2,3},{3,2},{4,5},{5,4},{6,7},{7,6},{8,9},{9,8},{10,11... | collective-permute-start | bytes 393224 | tf_op jit(solution)/shard_map/ppermute | solution.py:403
  10.2 31.5 %collective-permute-start.4 = (bf16[1024,512]{1,0:T(8,128)(2,1)S(1)}, bf16[1024,512]{1,0:T(8,128)(2,1)}, u32[]{:S(2)}, u32[]{:S(2)}) collective-permute-start(bf16[1024,512]{1,0:T(8,128)(2,1)S(1)} %copy-done.3), channel_id=1, source_target_pairs={{0,1},{1,0},{2,3},{3,2},{4,5},{5,4},{6,7},{7,6},{8,9},{9,8},{10,11... | collective-permute-start | bytes 3145736 | tf_op jit(solution)/shard_map/ppermute | solution.py:403
  10.7 31.0 %collective-permute-start.5 = (bf16[1024,512]{1,0:T(8,128)(2,1)}, bf16[1024,512]{1,0:T(8,128)(2,1)}, u32[]{:S(2)}, u32[]{:S(2)}) collective-permute-start(bf16[1024,512]{1,0:T(8,128)(2,1)} %wu0_hbm.1), channel_id=1, source_target_pairs={{0,1},{1,0},{2,3},{3,2},{4,5},{5,4},{6,7},{7,6},{8,9},{9,8},{10,11... | collective-permute-start | bytes 3145736 | tf_op jit(solution)/shard_map/ppermute | solution.py:403
  10.8 30.9 %collective-permute-start.6 = (bf16[512,1024]{1,0:T(8,128)(2,1)}, bf16[512,1024]{1,0:T(8,128)(2,1)}, u32[]{:S(2)}, u32[]{:S(2)}) collective-permute-start(bf16[512,1024]{1,0:T(8,128)(2,1)} %wd0_hbm.1), channel_id=1, source_target_pairs={{0,1},{1,0},{2,3},{3,2},{4,5},{5,4},{6,7},{7,6},{8,9},{9,8},{10,11... | collective-permute-start | bytes 3145736 | tf_op jit(solution)/shard_map/ppermute | solution.py:403
  11.2 6.4 %collective-permute-start.1 = (bf16[256,256]{1,0:T(8,128)(2,1)S(1)}, bf16[256,256]{1,0:T(8,128)(2,1)S(1)}, u32[]{:S(2)}, u32[]{:S(2)}) collective-permute-start(bf16[256,256]{1,0:T(8,128)(2,1)S(1)} %get-tuple-element.33.gate0_ref), channel_id=1, source_target_pairs={{0,2},{1,3},{2,0},{3,1},{4,6},{5,7},{6,4},{7,5},{8,10},{9,11},{10,... | collective-permute-start | bytes 393224 | tf_op jit(solution)/shard_map/ppermute | solution.py:403
  12.7 5.9 %collective-permute-start.2 = (bf16[256,256]{1,0:T(8,128)(2,1)S(1)}, bf16[256,256]{1,0:T(8,128)(2,1)S(1)}, u32[]{:S(2)}, u32[]{:S(2)}) collective-permute-start(bf16[256,256]{1,0:T(8,128)(2,1)S(1)} %get-tuple-element.61), channel_id=1, source_target_pairs={{0,3},{1,2},{2,1},{3,0},{4,7},{5,6},{6,5},{7,4},{8,11},{9,10},{10,... | collective-permute-start | bytes 393224 | tf_op jit(solution)/shard_map/ppermute | solution.py:403
  40.1 5.5 %collective-permute-start.3 = (bf16[8,32,256]{2,1,0:T(8,128)(2,1)S(1)}, bf16[8,32,256]{2,1,0:T(8,128)(2,1)S(1)}, u32[]{:S(2)}, u32[]{:S(2)}) collective-permute-start(bf16[8,32,256]{2,1,0:T(8,128)(2,1)S(1)} %get-tuple-element.59.conv0_ref), channel_id=1, source_target_pairs={{0,2},{1,3},{2,0},{3,1},{4,6},{5,7},{6,4},{7,5},{8,10},{9,11},{10,... | collective-permute-start | bytes 393224 | tf_op jit(solution)/shard_map/ppermute | solution.py:403
  41.7 5.8 %collective-permute-start.8 = (bf16[8,32,256]{2,1,0:T(8,128)(2,1)S(1)}, bf16[8,32,256]{2,1,0:T(8,128)(2,1)S(1)}, u32[]{:S(2)}, u32[]{:S(2)}) collective-permute-start(bf16[8,32,256]{2,1,0:T(8,128)(2,1)S(1)} %get-tuple-element.40), channel_id=1, source_target_pairs={{0,3},{1,2},{2,1},{3,0},{4,7},{5,6},{6,5},{7,4},{8,11},{9,10},{10,... | collective-permute-start | bytes 393224 | tf_op jit(solution)/shard_map/ppermute | solution.py:403
  45.7 1.8 %collective-permute-start.7 = (bf16[8,32,256]{2,1,0:T(8,128)(2,1)S(1)}, bf16[8,32,256]{2,1,0:T(8,128)(2,1)S(1)}, u32[]{:S(2)}, u32[]{:S(2)}) collective-permute-start(bf16[8,32,256]{2,1,0:T(8,128)(2,1)S(1)} %get-tuple-element.40), channel_id=1, source_target_pairs={{0,1},{1,0},{2,3},{3,2},{4,5},{5,4},{6,7},{7,6},{8,9},{9,8},{10,11... | collective-permute-start | bytes 393224 | tf_op jit(solution)/shard_map/ppermute | solution.py:403
  49.1 6.4 %collective-permute-start.9 = (bf16[256,256]{1,0:T(8,128)(2,1)S(1)}, bf16[256,256]{1,0:T(8,128)(2,1)S(1)}, u32[]{:S(2)}, u32[]{:S(2)}) collective-permute-start(bf16[256,256]{1,0:T(8,128)(2,1)S(1)} %get-tuple-element.55), channel_id=1, source_target_pairs={{0,2},{1,3},{2,0},{3,1},{4,6},{5,7},{6,4},{7,5},{8,10},{9,11},{10,... | collective-permute-start | bytes 393224 | tf_op jit(solution)/shard_map/ppermute | solution.py:403
  51.1 6.0 %collective-permute-start.11 = (bf16[256,256]{1,0:T(8,128)(2,1)S(1)}, bf16[256,256]{1,0:T(8,128)(2,1)S(1)}, u32[]{:S(2)}, u32[]{:S(2)}) collective-permute-start(bf16[256,256]{1,0:T(8,128)(2,1)S(1)} %get-tuple-element.58), channel_id=1, source_target_pairs={{0,3},{1,2},{2,1},{3,0},{4,7},{5,6},{6,5},{7,4},{8,11},{9,10},{10,... | collective-permute-start | bytes 393224 | tf_op jit(solution)/shard_map/ppermute | solution.py:403
  55.5 1.6 %collective-permute-start.10 = (bf16[256,256]{1,0:T(8,128)(2,1)S(1)}, bf16[256,256]{1,0:T(8,128)(2,1)S(1)}, u32[]{:S(2)}, u32[]{:S(2)}) collective-permute-start(bf16[256,256]{1,0:T(8,128)(2,1)S(1)} %get-tuple-element.57), channel_id=1, source_target_pairs={{0,1},{1,0},{2,3},{3,2},{4,5},{5,4},{6,7},{7,6},{8,9},{9,8},{10,11... | collective-permute-start | bytes 393224 | tf_op jit(solution)/shard_map/ppermute | solution.py:403

commit v7 on v6

--- a/solution.py
+++ b/solution.py
@@ -114,15 +114,13 @@
     gh_hbm,
     gl_hbm,
     skip_ref,
-    out_hbm,
+    out_ref,
     x_ref,
     h_ref,
     z_ref,
     gh_ref,
     gl_ref,
-    out_ref,
     sems,
-    out_sems,
 ):
     loads = start_loads(((gh_hbm, gh_ref), (gl_hbm, gl_ref)), sems)
     tm, _, chans, rows = both_ref.shape
@@ -202,21 +200,14 @@
     for load in loads:
         load.wait()
     skip = skip_ref[...]
-    stores = []
     for part in range(2):
         spec = z_ref[:, part].reshape(tm * chans, 2 * block)
         high = spec.astype(bf16)
         low = (spec - high.astype(f32)).astype(bf16)
         conv = dot(high, gh_ref[...]) + dot(low, gh_ref[...]) + dot(high, gl_ref[...])
         inputs = both_ref[:, 0, :, part * block : (part + 1) * block].astype(f32)
-        out_ref[:, part] = (conv.reshape(tm, chans, block) + skip[None] * inputs).astype(bf16)
-        store = pltpu.make_async_copy(
-            out_ref.at[:, part], out_hbm.at[:, part ^ core_ref[0]], out_sems.at[part]
-        )
-        store.start()
-        stores.append(store)
-    for store in stores:
-        store.wait()
+        total = conv.reshape(tm, chans, block) + skip[None] * inputs
+        out_ref[:, part ^ core_ref[0]] = total.astype(bf16)
 
 
 def mix(conv_refs, gate_refs, ats, mixed_ref, ready_ref, gain_ref, square):
@@ -449,11 +440,10 @@
         convolve_kernel,
         out_shape=jax.ShapeDtypeStruct((tm, 2, held, block), bf16),
         in_specs=[whole(SMEM)] + [whole()] * 3 + [whole(HBM)] * 2 + [whole()],
-        out_specs=whole(HBM),
+        out_specs=whole(),
         scratch_shapes=[pltpu.VMEM((tm, 2, held, 2 * block), f32)] * 3
         + [pltpu.VMEM(table.shape, bf16) for table in tables[2:]]
-        + [pltpu.VMEM((tm, 2, held, block), bf16)]
-        + [pltpu.SemaphoreType.DMA((2,))] * 2,
+        + [pltpu.SemaphoreType.DMA((2,))],
         compiler_params=params(24),
         name="convolve",
     )(place[1], both, *tables, skip)

time: 58.2 us -> 57.6 us (0.990)
  transfers between devices with their start and end apart: 13 -> 13, of which waited for: 7 -> 7; matrix products, arithmetic and copies ran while one was open for 0% -> 0% of each run, Pallas kernels for 11% -> 10%
where the time goes in v7:
time: 57.6 us; the launch traced here: 57.3 us
  waiting for transfers between devices  19.9 us (35%)
  starting transfers between devices  13.5 us (23%)
  blocking collectives  12.5 us (22%)
  Pallas kernels  10.3 us (18%)
  between operations  0.89 us (2%)
    ppermute x12, waiting for transfers between devices, swap(): lax.ppermute(values, ('x', 'core'), [(at, at ^ bits) for at in range(4)])  14 us
    all_to_all x1, blocking collectives, shards(): conv = lax.all_to_all(conv, 'tm', split_axis=0, concat_axis=0, tiled=True)  12.5 us
    all_to_all x1, starting transfers between devices, shards(): both = lax.all_to_all(made, 'tm', split_axis=0, concat_axis=0, tiled=True)  7.3 us
    ppermute x12, starting transfers between devices, swap(): lax.ppermute(values, ('x', 'core'), [(at, at ^ bits) for at in range(4)])  6.17 us
    all_to_all x1, waiting for transfers between devices, shards(): both = lax.all_to_all(made, 'tm', split_axis=0, concat_axis=0, tiled=True)  5.93 us
    pallas_call x1, Pallas kernels, shards(): pl.pallas_call(feed_first_kernel, out_shape=[jax.ShapeDtypeStruct(*spec)...  3 us
    pallas_call x1, Pallas kernels, shards(): pl.pallas_call(convolve_kernel, out_shape=jax.ShapeDtypeStruct((tm, 2, he...  2.41 us
    pallas_call x1, Pallas kernels, shards(): pl.pallas_call(prepare_kernel, out_shape=jax.ShapeDtypeStruct(shape, bf16...  1.97 us
  transfers between devices with their start and end apart: 13, of which 7 were waited for; matrix products, arithmetic and copies ran while one was open for 0% of the time, Pallas kernels for 10%

profile of v7, /device:TPU:0, one launch (start us, length us, event | category | flops | bytes accessed | tf_op | source)
XLA Modules:
  0.0 57.3 jit_solution(17365721716992755243)
XLA Ops:
  0.0 0.0 copy-start
  0.0 0.0 copy-start.1
  0.0 0.0 copy-start.2
  0.0 0.0 copy-start.4
  0.0 0.0 copy-start.3
  0.8 2.0 %prepare.1 = bf16[8,2,32,512]{3,2,1,0:T(8,128)(2,1)} custom-call(s32[1]{0:T(128)S(6)} %copy.24.step_ref, s32[8]{0:T(128)} %flags_hbm.1, bf16[512,256]{1,0:T(8,128)(2,1)} %value_hbm.1, bf16[512,256]{1,0:T(8,128)(2,1)} %filter_hbm.1, f32[200,256]{1,0:T(8,128)} %table_hbm.1, f32[1,256]{1,0:T(1,128)} %bitcast.15), custom_call_target="tpu_custom_call" | custom-call | tf_op jit(solution)/shard_map/prepare/pallas_call | solution.py:398
  2.8 7.3 %all-to-all-start = ((bf16[8,2,32,512]{3,2,1,0:T(8,128)(2,1)}), bf16[8,2,32,512]{3,2,1,0:T(8,128)(2,1)S(1)}, u32[]{:S(2)}, u32[]{:S(2)}) async-start(bf16[8,2,32,512]{3,2,1,0:T(8,128)(2,1)} %prepare.1), calls=%async_computation | async-start | bytes 1048576 | tf_op jit(solution)/shard_map/all_to_all | solution.py:422
  10.1 0.0 copy-done.4
  10.1 0.1 collective-permute-start
  10.2 0.0 copy-done.3
  10.2 0.5 collective-permute-start.4
  10.7 0.1 collective-permute-start.5
  10.8 0.4 collective-permute-start.6
  11.2 1.5 %collective-permute-start.1 = (bf16[256,256]{1,0:T(8,128)(2,1)S(1)}, bf16[256,256]{1,0:T(8,128)(2,1)S(1)}, u32[]{:S(2)}, u32[]{:S(2)}) collective-permute-start(bf16[256,256]{1,0:T(8,128)(2,1)S(1)} %get-tuple-element.33.gate0_ref), channel_id=1, source_target_pairs={{0,2},{1,3},{2,0},{3,1},{4,6},{5,7},{6,4},{7,5},{8,10},{9,11},{10,... | collective-permute-start | bytes 393224 | tf_op jit(solution)/shard_map/ppermute | solution.py:394
  12.7 0.0 collective-permute-done.gate1_ref
  12.7 0.1 collective-permute-start.2
  12.8 0.0 copy-done
  12.8 0.1 dynamic-slice_bitcast_fusion
  12.9 0.1 copy.19.skip_ref
  12.9 4.6 %collective-permute-done.1.gate2_ref = bf16[256,256]{1,0:T(8,128)(2,1)S(1)} collective-permute-done((bf16[256,256]{1,0:T(8,128)(2,1)S(1)}, bf16[256,256]{1,0:T(8,128)(2,1)S(1)}, u32[]{:S(2)}, u32[]{:S(2)}) %collective-permute-start.1) | collective-permute-done | bytes 131104 | tf_op jit(solution)/shard_map/ppermute | solution.py:394
  17.6 1.1 %collective-permute-done.2.gate3_ref = bf16[256,256]{1,0:T(8,128)(2,1)S(1)} collective-permute-done((bf16[256,256]{1,0:T(8,128)(2,1)S(1)}, bf16[256,256]{1,0:T(8,128)(2,1)S(1)}, u32[]{:S(2)}, u32[]{:S(2)}) %collective-permute-start.2) | collective-permute-done | bytes 131104 | tf_op jit(solution)/shard_map/ppermute | solution.py:394
  18.6 5.9 %all-to-all-done.both_ref = bf16[8,2,32,512]{3,2,1,0:T(8,128)(2,1)S(1)} async-done(((bf16[8,2,32,512]{3,2,1,0:T(8,128)(2,1)}), bf16[8,2,32,512]{3,2,1,0:T(8,128)(2,1)S(1)}, u32[]{:S(2)}, u32[]{:S(2)}) %all-to-all-start) | async-done | bytes 524320 | tf_op jit(solution)/shard_map/all_to_all | solution.py:422
  24.6 0.0 copy-done.1
  24.6 0.0 copy-done.2
  24.6 2.4 %convolve.1 = bf16[8,2,32,256]{3,2,1,0:T(8,128)(2,1)S(1)} custom-call(s32[1]{0:T(128)} %bitcast.core_ref, bf16[8,2,32,512]{3,2,1,0:T(8,128)(2,1)S(1)} %all-to-all-done.both_ref, bf16[256,512]{1,0:T(8,128)(2,1)S(1)} %copy-done.1, bf16[256,512]{1,0:T(8,128)(2,1)S(1)} %copy-done.2, bf16[512,256]{1,0:T(8,128)(2,1)} %constant.32.clone.gh_hbm, ...), custom_call_target="tpu_custom_call" | custom-call | tf_op jit(solution)/shard_map/convolve/pallas_call | solution.py:439
  27.0 12.5 %all_to_all.10 = bf16[8,2,32,256]{3,2,1,0:T(8,128)(2,1)S(1)} all-to-all(bf16[8,2,32,256]{3,2,1,0:T(8,128)(2,1)S(1)} %convolve.1), channel_id=1, replica_groups=mesh['tm'=8,'x'=2,'core'=2] {'tm'}, dimensions={0} | all-to-all | bytes 524288 | tf_op jit(solution)/shard_map/all_to_all | solution.py:453
  39.5 1.6 %collective-permute-start.3 = (bf16[8,32,256]{2,1,0:T(8,128)(2,1)S(1)}, bf16[8,32,256]{2,1,0:T(8,128)(2,1)S(1)}, u32[]{:S(2)}, u32[]{:S(2)}) collective-permute-start(bf16[8,32,256]{2,1,0:T(8,128)(2,1)S(1)} %get-tuple-element.59.conv0_ref), channel_id=1, source_target_pairs={{0,2},{1,3},{2,0},{3,1},{4,6},{5,7},{6,4},{7,5},{8,10},{9,11},{10,... | collective-permute-start | bytes 393224 | tf_op jit(solution)/shard_map/ppermute | solution.py:394
  41.1 0.0 collective-permute-start.8
  41.1 0.0 collective-permute-done.4.wg1_hbm
  41.1 0.0 collective-permute-done.5.wu1_hbm
  41.1 0.0 collective-permute-done.6.wd1_hbm
  41.1 3.0 %feed_first.1 = (bf16[256,256]{1,0:T(8,128)(2,1)S(1)}, f32[256,1]{1,0:T(8,128)S(1)}, f32[4,1,256]{2,1,0:T(1,128)S(1)}, f32[4,256,512]{2,1,0:T(8,128)S(1)}, bf16[...) custom-call(s32[1]{0:T(128)} %bitcast.1.chip_ref, s32[1]{0:T(128)} %bitcast.core_ref, ...), custom_call_target="tpu_custom_call" | custom-call | tf_op jit(solution)/shard_map/feed_first/pallas_call | solution.py:469
  44.1 0.9 %collective-permute-done.3.conv2_ref = bf16[8,32,256]{2,1,0:T(8,128)(2,1)S(1)} collective-permute-done((bf16[8,32,256]{2,1,0:T(8,128)(2,1)S(1)}, bf16[8,32,256]{2,1,0:T(8,128)(2,1)S(1)}, u32[]{:S(2)}, u32[]{:S(2)}) %collective-permute-start.3) | collective-permute-done | bytes 131104 | tf_op jit(solution)/shard_map/ppermute | solution.py:394
  45.1 0.0 collective-permute-start.7
  45.1 1.8 %collective-permute-done.8.conv3_ref = bf16[8,32,256]{2,1,0:T(8,128)(2,1)S(1)} collective-permute-done((bf16[8,32,256]{2,1,0:T(8,128)(2,1)S(1)}, bf16[8,32,256]{2,1,0:T(8,128)(2,1)S(1)}, u32[]{:S(2)}, u32[]{:S(2)}) %collective-permute-start.8) | collective-permute-done | bytes 131104 | tf_op jit(solution)/shard_map/ppermute | solution.py:394
  46.9 0.0 collective-permute-done.7.conv1_ref
  46.9 1.7 %feed_second.1 = (bf16[256,256]{1,0:T(8,128)(2,1)S(1)}, bf16[256,1024]{1,0:T(8,128)(2,1)S(1)}, bf16[256,256]{1,0:T(8,128)(2,1)S(1)}, bf16[256,256]{1,0:T(8,128)(2,1)S(1)}) custom-call(s32[1]{0:T(128)} %bitcast.1.chip_ref, s32[1]{0:T(128)} %bitcast.core_ref, bf16[8,32,256]{2,1,0:T(8,128)(2,1)S(1)} %collective-permute-done.7.conv1_ref, ...), custom_call_target="tpu_custom_call" | custom-call | tf_op jit(solution)/shard_map/feed_second/pallas_call | solution.py:491
  48.6 2.0 %collective-permute-start.9 = (bf16[256,256]{1,0:T(8,128)(2,1)S(1)}, bf16[256,256]{1,0:T(8,128)(2,1)S(1)}, u32[]{:S(2)}, u32[]{:S(2)}) collective-permute-start(bf16[256,256]{1,0:T(8,128)(2,1)S(1)} %get-tuple-element.55), channel_id=1, source_target_pairs={{0,2},{1,3},{2,0},{3,1},{4,6},{5,7},{6,4},{7,5},{8,10},{9,11},{10,... | collective-permute-start | bytes 393224 | tf_op jit(solution)/shard_map/ppermute | solution.py:394
  50.5 0.0 collective-permute-start.11
  50.5 0.5 feed_third.1
  51.0 3.9 %collective-permute-done.9.side_ref = bf16[256,256]{1,0:T(8,128)(2,1)S(1)} collective-permute-done((bf16[256,256]{1,0:T(8,128)(2,1)S(1)}, bf16[256,256]{1,0:T(8,128)(2,1)S(1)}, u32[]{:S(2)}, u32[]{:S(2)}) %collective-permute-start.9) | collective-permute-done | bytes 131104 | tf_op jit(solution)/shard_map/ppermute | solution.py:394
  54.9 0.0 collective-permute-start.10
  54.9 1.6 %collective-permute-done.11.side1_ref = bf16[256,256]{1,0:T(8,128)(2,1)S(1)} collective-permute-done((bf16[256,256]{1,0:T(8,128)(2,1)S(1)}, bf16[256,256]{1,0:T(8,128)(2,1)S(1)}, u32[]{:S(2)}, u32[]{:S(2)}) %collective-permute-start.11) | collective-permute-done | bytes 131104 | tf_op jit(solution)/shard_map/ppermute | solution.py:394
  56.6 0.0 collective-permute-done.10.core1_ref
  56.6 0.8 %finish.1 = bf16[512,256]{1,0:T(8,128)(2,1)} custom-call(s32[1]{0:T(128)} %bitcast.core_ref, f32[256,256]{1,0:T(8,128)S(1)} %get-tuple-element.53.own_ref, bf16[256,256]{1,0:T(8,128)(2,1)S(1)} %collective-permute-done.9.side_ref, bf16[256,256]{1,0:T(8,128)(2,1)S(1)} %collective-permute-done.10.core1_ref, bf16[256,256]{1,0:T(8,128)(2,1)S(1)} %collective-permute-done.11.side1_ref), custom_call_target="tpu_custom_call" | custom-call | tf_op jit(solution)/shard_map/finish/pallas_call | solution.py:511
  (2 shorter events, 0.0 us)
Async XLA Ops:
  0.0 12.8 %copy-start = (f32[256]{0:T(256)S(1)}, f32[256]{0:T(256)}, u32[]{:S(2)}) copy-start(f32[256]{0:T(256)} %param.23) | copy-start | bytes 3076
  0.0 24.6 %copy-start.1 = (bf16[256,512]{1,0:T(8,128)(2,1)S(1)}, bf16[256,512]{1,0:T(8,128)(2,1)}, u32[]{:S(2)}) copy-start(bf16[256,512]{1,0:T(8,128)(2,1)} %constant.30.clone.fh_ref) | copy-start | bytes 786436
  0.0 24.6 %copy-start.2 = (bf16[256,512]{1,0:T(8,128)(2,1)S(1)}, bf16[256,512]{1,0:T(8,128)(2,1)}, u32[]{:S(2)}) copy-start(bf16[256,512]{1,0:T(8,128)(2,1)} %constant.31.clone.fl_ref) | copy-start | bytes 786436
  0.0 10.1 %copy-start.4 = (bf16[512,256]{1,0:T(8,128)(2,1)S(1)}, bf16[512,256]{1,0:T(8,128)(2,1)}, u32[]{:S(2)}) copy-start(bf16[512,256]{1,0:T(8,128)(2,1)} %param.17) | copy-start | bytes 786436
  0.0 10.2 %copy-start.3 = (bf16[1024,512]{1,0:T(8,128)(2,1)S(1)}, bf16[1024,512]{1,0:T(8,128)(2,1)}, u32[]{:S(2)}) copy-start(bf16[1024,512]{1,0:T(8,128)(2,1)} %wg0_hbm.1) | copy-start | bytes 3145732
  2.8 21.8 %all-to-all-start = ((bf16[8,2,32,512]{3,2,1,0:T(8,128)(2,1)}), bf16[8,2,32,512]{3,2,1,0:T(8,128)(2,1)S(1)}, u32[]{:S(2)}, u32[]{:S(2)}) async-start(bf16[8,2,32,512]{3,2,1,0:T(8,128)(2,1)} %prepare.1), calls=%async_computation | async-start | bytes 1048576 | tf_op jit(solution)/shard_map/all_to_all | solution.py:422
  10.1 2.6 %collective-permute-start = (bf16[256,256]{1,0:T(8,128)(2,1)S(1)}, bf16[256,256]{1,0:T(8,128)(2,1)S(1)}, u32[]{:S(2)}, u32[]{:S(2)}) collective-permute-start(bf16[256,256]{1,0:T(8,128)(2,1)S(1)} %get-tuple-element.61), channel_id=1, source_target_pairs={{0,1},{1,0},{2,3},{3,2},{4,5},{5,4},{6,7},{7,6},{8,9},{9,8},{10,11... | collective-permute-start | bytes 393224 | tf_op jit(solution)/shard_map/ppermute | solution.py:394
  10.2 30.9 %collective-permute-start.4 = (bf16[1024,512]{1,0:T(8,128)(2,1)S(1)}, bf16[1024,512]{1,0:T(8,128)(2,1)}, u32[]{:S(2)}, u32[]{:S(2)}) collective-permute-start(bf16[1024,512]{1,0:T(8,128)(2,1)S(1)} %copy-done.3), channel_id=1, source_target_pairs={{0,1},{1,0},{2,3},{3,2},{4,5},{5,4},{6,7},{7,6},{8,9},{9,8},{10,11... | collective-permute-start | bytes 3145736 | tf_op jit(solution)/shard_map/ppermute | solution.py:394
  10.7 30.4 %collective-permute-start.5 = (bf16[1024,512]{1,0:T(8,128)(2,1)}, bf16[1024,512]{1,0:T(8,128)(2,1)}, u32[]{:S(2)}, u32[]{:S(2)}) collective-permute-start(bf16[1024,512]{1,0:T(8,128)(2,1)} %wu0_hbm.1), channel_id=1, source_target_pairs={{0,1},{1,0},{2,3},{3,2},{4,5},{5,4},{6,7},{7,6},{8,9},{9,8},{10,11... | collective-permute-start | bytes 3145736 | tf_op jit(solution)/shard_map/ppermute | solution.py:394
  10.8 30.3 %collective-permute-start.6 = (bf16[512,1024]{1,0:T(8,128)(2,1)}, bf16[512,1024]{1,0:T(8,128)(2,1)}, u32[]{:S(2)}, u32[]{:S(2)}) collective-permute-start(bf16[512,1024]{1,0:T(8,128)(2,1)} %wd0_hbm.1), channel_id=1, source_target_pairs={{0,1},{1,0},{2,3},{3,2},{4,5},{5,4},{6,7},{7,6},{8,9},{9,8},{10,11... | collective-permute-start | bytes 3145736 | tf_op jit(solution)/shard_map/ppermute | solution.py:394
  11.2 6.4 %collective-permute-start.1 = (bf16[256,256]{1,0:T(8,128)(2,1)S(1)}, bf16[256,256]{1,0:T(8,128)(2,1)S(1)}, u32[]{:S(2)}, u32[]{:S(2)}) collective-permute-start(bf16[256,256]{1,0:T(8,128)(2,1)S(1)} %get-tuple-element.33.gate0_ref), channel_id=1, source_target_pairs={{0,2},{1,3},{2,0},{3,1},{4,6},{5,7},{6,4},{7,5},{8,10},{9,11},{10,... | collective-permute-start | bytes 393224 | tf_op jit(solution)/shard_map/ppermute | solution.py:394
  12.7 5.9 %collective-permute-start.2 = (bf16[256,256]{1,0:T(8,128)(2,1)S(1)}, bf16[256,256]{1,0:T(8,128)(2,1)S(1)}, u32[]{:S(2)}, u32[]{:S(2)}) collective-permute-start(bf16[256,256]{1,0:T(8,128)(2,1)S(1)} %get-tuple-element.61), channel_id=1, source_target_pairs={{0,3},{1,2},{2,1},{3,0},{4,7},{5,6},{6,5},{7,4},{8,11},{9,10},{10,... | collective-permute-start | bytes 393224 | tf_op jit(solution)/shard_map/ppermute | solution.py:394
  39.5 5.5 %collective-permute-start.3 = (bf16[8,32,256]{2,1,0:T(8,128)(2,1)S(1)}, bf16[8,32,256]{2,1,0:T(8,128)(2,1)S(1)}, u32[]{:S(2)}, u32[]{:S(2)}) collective-permute-start(bf16[8,32,256]{2,1,0:T(8,128)(2,1)S(1)} %get-tuple-element.59.conv0_ref), channel_id=1, source_target_pairs={{0,2},{1,3},{2,0},{3,1},{4,6},{5,7},{6,4},{7,5},{8,10},{9,11},{10,... | collective-permute-start | bytes 393224 | tf_op jit(solution)/shard_map/ppermute | solution.py:394
  41.1 5.8 %collective-permute-start.8 = (bf16[8,32,256]{2,1,0:T(8,128)(2,1)S(1)}, bf16[8,32,256]{2,1,0:T(8,128)(2,1)S(1)}, u32[]{:S(2)}, u32[]{:S(2)}) collective-permute-start(bf16[8,32,256]{2,1,0:T(8,128)(2,1)S(1)} %get-tuple-element.40), channel_id=1, source_target_pairs={{0,3},{1,2},{2,1},{3,0},{4,7},{5,6},{6,5},{7,4},{8,11},{9,10},{10,... | collective-permute-start | bytes 393224 | tf_op jit(solution)/shard_map/ppermute | solution.py:394
  45.1 1.8 %collective-permute-start.7 = (bf16[8,32,256]{2,1,0:T(8,128)(2,1)S(1)}, bf16[8,32,256]{2,1,0:T(8,128)(2,1)S(1)}, u32[]{:S(2)}, u32[]{:S(2)}) collective-permute-start(bf16[8,32,256]{2,1,0:T(8,128)(2,1)S(1)} %get-tuple-element.40), channel_id=1, source_target_pairs={{0,1},{1,0},{2,3},{3,2},{4,5},{5,4},{6,7},{7,6},{8,9},{9,8},{10,11... | collective-permute-start | bytes 393224 | tf_op jit(solution)/shard_map/ppermute | solution.py:394
  48.6 6.4 %collective-permute-start.9 = (bf16[256,256]{1,0:T(8,128)(2,1)S(1)}, bf16[256,256]{1,0:T(8,128)(2,1)S(1)}, u32[]{:S(2)}, u32[]{:S(2)}) collective-permute-start(bf16[256,256]{1,0:T(8,128)(2,1)S(1)} %get-tuple-element.55), channel_id=1, source_target_pairs={{0,2},{1,3},{2,0},{3,1},{4,6},{5,7},{6,4},{7,5},{8,10},{9,11},{10,... | collective-permute-start | bytes 393224 | tf_op jit(solution)/shard_map/ppermute | solution.py:394
  50.5 6.0 %collective-permute-start.11 = (bf16[256,256]{1,0:T(8,128)(2,1)S(1)}, bf16[256,256]{1,0:T(8,128)(2,1)S(1)}, u32[]{:S(2)}, u32[]{:S(2)}) collective-permute-start(bf16[256,256]{1,0:T(8,128)(2,1)S(1)} %get-tuple-element.58), channel_id=1, source_target_pairs={{0,3},{1,2},{2,1},{3,0},{4,7},{5,6},{6,5},{7,4},{8,11},{9,10},{10,... | collective-permute-start | bytes 393224 | tf_op jit(solution)/shard_map/ppermute | solution.py:394
  54.9 1.6 %collective-permute-start.10 = (bf16[256,256]{1,0:T(8,128)(2,1)S(1)}, bf16[256,256]{1,0:T(8,128)(2,1)S(1)}, u32[]{:S(2)}, u32[]{:S(2)}) collective-permute-start(bf16[256,256]{1,0:T(8,128)(2,1)S(1)} %get-tuple-element.57), channel_id=1, source_target_pairs={{0,1},{1,0},{2,3},{3,2},{4,5},{5,4},{6,7},{7,6},{8,9},{9,8},{10,11... | collective-permute-start | bytes 393224 | tf_op jit(solution)/shard_map/ppermute | solution.py:394

commit v8 on v7

--- a/solution.py
+++ b/solution.py
@@ -215,7 +215,7 @@
     for j, (conv_ref, gate_ref, at) in enumerate(zip(conv_refs, gate_refs, ats)):
         conv = conv_ref[...].reshape(width, rows).T.astype(f32)
         mixed = (gate_ref[...].astype(f32) * conv).astype(bf16)
-        if j == 0:
+        if j == 0 and mixed_ref is not None:
             mixed_ref[...] = mixed
         wide = mixed.astype(f32)
         square = square + jnp.sum(wide * wide, axis=-1, keepdims=True)
@@ -239,6 +239,7 @@
     square_ref,
     gain_ref,
     sums_ref,
+    straight_ref,
     rest_ref,
     down_ref,
     ready_ref,
@@ -256,9 +257,10 @@
     loads = start_loads(
         [(gain_hbm, gain_ref)]
         + [(source(weight, 0), now_ref.at[at]) for at, weight in enumerate(weights)]
+        + [(source(weight, 2), straight_ref.at[at]) for at, weight in enumerate(weights)]
         + [
-            (source(weight, j), rest_ref.at[at, pl.ds((j - 1) * width, width)])
-            for j in (1, 2, 3)
+            (source(weight, j), rest_ref.at[at, pl.ds(first, width)])
+            for j, first in ((1, 0), (3, width))
             for at, weight in enumerate(weights)
         ]
         + [
@@ -285,14 +287,34 @@
         load.wait()
 
 
+def feed_middle_kernel(
+    chip_ref,
+    core_ref,
+    conv2_ref,
+    gate2_ref,
+    square_ref,
+    gain_ref,
+    sums_ref,
+    straight_ref,
+    square_out_ref,
+    sums_out_ref,
+    ready_ref,
+):
+    here = 2 * chip_ref[0] + core_ref[0]
+    square_out_ref[...] = mix(
+        (conv2_ref,), (gate2_ref,), (here ^ 2,), None, ready_ref, gain_ref, square_ref[...]
+    )
+    ready = ready_ref[...]
+    for at in range(4):
+        sums_out_ref[at] = sums_ref[at] + dot(ready, straight_ref[at])
+
+
 def feed_second_kernel(
     chip_ref,
     core_ref,
     conv1_ref,
-    conv2_ref,
     conv3_ref,
     gate1_ref,
-    gate2_ref,
     gate3_ref,
     square_ref,
     gain_ref,
@@ -308,9 +330,9 @@
     here = 2 * chip_ref[0] + core_ref[0]
     width = gate1_ref.shape[1]
     square = mix(
-        (conv1_ref, conv2_ref, conv3_ref),
-        (gate1_ref, gate2_ref, gate3_ref),
-        (here ^ 1, here ^ 2, here ^ 3),
+        (conv1_ref, conv3_ref),
+        (gate1_ref, gate3_ref),
+        (here ^ 1, here ^ 3),
         mixed_ref,
         ready_ref,
         gain_ref,
@@ -463,14 +485,15 @@
         ((block, 1), f32),
         ((4, 1, width), f32),
         ((4, block, w_gate.shape[1]), f32),
-        ((4, 3 * width, w_gate.shape[1]), bf16),
+        ((4, width, w_gate.shape[1]), bf16),
+        ((4, 2 * width, w_gate.shape[1]), bf16),
         ((2 * w_down.shape[0], w_down.shape[1]), bf16),
     ]
     kept = pl.pallas_call(
         feed_first_kernel,
         out_shape=[jax.ShapeDtypeStruct(*spec) for spec in held],
         in_specs=[whole(SMEM)] * 2 + [whole()] * 2 + [whole(HBM)] * 7,
-        out_specs=[whole()] * 6,
+        out_specs=[whole()] * 7,
         scratch_shapes=[
             pltpu.VMEM((block, width), bf16),
             pltpu.VMEM((4, width, w_gate.shape[1]), bf16),
@@ -486,17 +509,37 @@
     )
     theirs, aside, kept = lax.optimization_barrier((theirs, aside, kept))
     beside = swap(theirs, 1)
-    mixed0, *kept = kept
+    mixed0, square, gain, sums, straight, rest, down = kept
+    square, sums = pl.pallas_call(
+        feed_middle_kernel,
+        out_shape=[jax.ShapeDtypeStruct(*held[1]), jax.ShapeDtypeStruct(*held[3])],
+        in_specs=[whole(SMEM)] * 2 + [whole()] * 6,
+        out_specs=[whole()] * 2,
+        scratch_shapes=[pltpu.VMEM((block, width), bf16)],
+        compiler_params=params(24),
+        name="feed_middle",
+    )(*place, view(aside), gates[2], square, gain, sums, straight)
     shape = jax.ShapeDtypeStruct((block, width), bf16)
     mixed1, hidden, *remote = pl.pallas_call(
         feed_second_kernel,
         out_shape=[shape, jax.ShapeDtypeStruct((block, 2 * w_gate.shape[1]), bf16), shape, shape],
-        in_specs=[whole(SMEM)] * 2 + [whole()] * 11,
+        in_specs=[whole(SMEM)] * 2 + [whole()] * 9,
         out_specs=[whole()] * 4,
-        scratch_shapes=[pltpu.VMEM((block, 3 * width), bf16)],
+        scratch_shapes=[pltpu.VMEM((block, 2 * width), bf16)],
         compiler_params=params(24),
         name="feed_second",
-    )(*place, *map(view, (beside, aside, across)), *gates[1:], *kept)
+    )(
+        *place,
+        view(beside),
+        view(across),
+        gates[1],
+        gates[3],
+        square,
+        gain,
+        sums,
+        rest,
+        down,
+    )
     side, side1 = swap(remote[0], 2), swap(remote[1], 3)
     local = pl.pallas_call(
         feed_third_kernel,
@@ -505,7 +548,7 @@
         out_specs=[whole()] * 2,
         compiler_params=params(16),
         name="feed_third",
-    )(*place, hidden, kept[-1], mixed0, mixed1)
+    )(*place, hidden, down, mixed0, mixed1)
     owned, lent = local
     lent, side = lax.optimization_barrier((lent, side))
     return pl.pallas_call(

time: 57.6 us -> 57.3 us (level)
  transfers between devices with their start and end apart: 13 -> 13, of which waited for: 7 -> 7; matrix products, arithmetic and copies ran while one was open for 0% -> 0% of each run, Pallas kernels for 10% -> 11%
where the time goes in v8:
time: 57.3 us; the launch traced here: 57 us
  waiting for transfers between devices  19.5 us (34%)
  starting transfers between devices  13.5 us (24%)
  blocking collectives  12.5 us (22%)
  Pallas kernels  10.5 us (18%)
  between operations  0.89 us (2%)
    ppermute x12, waiting for transfers between devices, swap(): lax.ppermute(values, ('x', 'core'), [(at, at ^ bits) for at in range(4)])  13.5 us
    all_to_all x1, blocking collectives, shards(): conv = lax.all_to_all(conv, 'tm', split_axis=0, concat_axis=0, tiled=True)  12.5 us
    all_to_all x1, starting transfers between devices, shards(): both = lax.all_to_all(made, 'tm', split_axis=0, concat_axis=0, tiled=True)  7.3 us
    ppermute x12, starting transfers between devices, swap(): lax.ppermute(values, ('x', 'core'), [(at, at ^ bits) for at in range(4)])  6.17 us
    all_to_all x1, waiting for transfers between devices, shards(): both = lax.all_to_all(made, 'tm', split_axis=0, concat_axis=0, tiled=True)  5.93 us
    pallas_call x1, Pallas kernels, shards(): pl.pallas_call(feed_first_kernel, out_shape=[jax.ShapeDtypeStruct(*spec)...  3 us
    pallas_call x1, Pallas kernels, shards(): pl.pallas_call(convolve_kernel, out_shape=jax.ShapeDtypeStruct((tm, 2, he...  2.41 us
    pallas_call x1, Pallas kernels, shards(): pl.pallas_call(prepare_kernel, out_shape=jax.ShapeDtypeStruct(shape, bf16...  2.01 us
  transfers between devices with their start and end apart: 13, of which 7 were waited for; matrix products, arithmetic and copies ran while one was open for 0% of the time, Pallas kernels for 11%

profile of v8, /device:TPU:0, one launch (start us, length us, event | category | flops | bytes accessed | tf_op | source)
XLA Modules:
  0.0 57.0 jit_solution(17801639529674560903)
XLA Ops:
  0.0 0.0 copy-start
  0.0 0.0 copy-start.1
  0.0 0.0 copy-start.2
  0.0 0.0 copy-start.4
  0.0 0.0 copy-start.3
  0.8 2.0 %prepare.1 = bf16[8,2,32,512]{3,2,1,0:T(8,128)(2,1)} custom-call(s32[1]{0:T(128)S(6)} %copy.24.step_ref, s32[8]{0:T(128)} %flags_hbm.1, bf16[512,256]{1,0:T(8,128)(2,1)} %value_hbm.1, bf16[512,256]{1,0:T(8,128)(2,1)} %filter_hbm.1, f32[200,256]{1,0:T(8,128)} %table_hbm.1, f32[1,256]{1,0:T(1,128)} %bitcast.15), custom_call_target="tpu_custom_call" | custom-call | tf_op jit(solution)/shard_map/prepare/pallas_call | solution.py:420
  2.8 7.3 %all-to-all-start = ((bf16[8,2,32,512]{3,2,1,0:T(8,128)(2,1)}), bf16[8,2,32,512]{3,2,1,0:T(8,128)(2,1)S(1)}, u32[]{:S(2)}, u32[]{:S(2)}) async-start(bf16[8,2,32,512]{3,2,1,0:T(8,128)(2,1)} %prepare.1), calls=%async_computation | async-start | bytes 1048576 | tf_op jit(solution)/shard_map/all_to_all | solution.py:444
  10.1 0.0 copy-done.4
  10.2 0.1 collective-permute-start
  10.2 0.0 copy-done.3
  10.2 0.5 collective-permute-start.4
  10.7 0.1 collective-permute-start.5
  10.8 0.4 collective-permute-start.6
  11.2 1.5 %collective-permute-start.1 = (bf16[256,256]{1,0:T(8,128)(2,1)S(1)}, bf16[256,256]{1,0:T(8,128)(2,1)S(1)}, u32[]{:S(2)}, u32[]{:S(2)}) collective-permute-start(bf16[256,256]{1,0:T(8,128)(2,1)S(1)} %get-tuple-element.37.gate0_ref), channel_id=1, source_target_pairs={{0,2},{1,3},{2,0},{3,1},{4,6},{5,7},{6,4},{7,5},{8,10},{9,11},{10,... | collective-permute-start | bytes 393224 | tf_op jit(solution)/shard_map/ppermute | solution.py:416
  12.7 0.0 collective-permute-done.gate1_ref
  12.7 0.1 collective-permute-start.2
  12.8 0.0 copy-done
  12.8 0.1 dynamic-slice_bitcast_fusion
  12.9 0.1 copy.19.skip_ref
  13.0 4.6 %collective-permute-done.1.gate2_ref = bf16[256,256]{1,0:T(8,128)(2,1)S(1)} collective-permute-done((bf16[256,256]{1,0:T(8,128)(2,1)S(1)}, bf16[256,256]{1,0:T(8,128)(2,1)S(1)}, u32[]{:S(2)}, u32[]{:S(2)}) %collective-permute-start.1) | collective-permute-done | bytes 131104 | tf_op jit(solution)/shard_map/ppermute | solution.py:416
  17.6 1.1 %collective-permute-done.2.gate3_ref = bf16[256,256]{1,0:T(8,128)(2,1)S(1)} collective-permute-done((bf16[256,256]{1,0:T(8,128)(2,1)S(1)}, bf16[256,256]{1,0:T(8,128)(2,1)S(1)}, u32[]{:S(2)}, u32[]{:S(2)}) %collective-permute-start.2) | collective-permute-done | bytes 131104 | tf_op jit(solution)/shard_map/ppermute | solution.py:416
  18.7 5.9 %all-to-all-done.both_ref = bf16[8,2,32,512]{3,2,1,0:T(8,128)(2,1)S(1)} async-done(((bf16[8,2,32,512]{3,2,1,0:T(8,128)(2,1)}), bf16[8,2,32,512]{3,2,1,0:T(8,128)(2,1)S(1)}, u32[]{:S(2)}, u32[]{:S(2)}) %all-to-all-start) | async-done | bytes 524320 | tf_op jit(solution)/shard_map/all_to_all | solution.py:444
  24.6 0.0 copy-done.1
  24.6 0.0 copy-done.2
  24.6 2.4 %convolve.1 = bf16[8,2,32,256]{3,2,1,0:T(8,128)(2,1)S(1)} custom-call(s32[1]{0:T(128)} %bitcast.core_ref, bf16[8,2,32,512]{3,2,1,0:T(8,128)(2,1)S(1)} %all-to-all-done.both_ref, bf16[256,512]{1,0:T(8,128)(2,1)S(1)} %copy-done.1, bf16[256,512]{1,0:T(8,128)(2,1)S(1)} %copy-done.2, bf16[512,256]{1,0:T(8,128)(2,1)} %constant.32.clone.gh_hbm, ...), custom_call_target="tpu_custom_call" | custom-call | tf_op jit(solution)/shard_map/convolve/pallas_call | solution.py:461
  27.0 12.5 %all_to_all.10 = bf16[8,2,32,256]{3,2,1,0:T(8,128)(2,1)S(1)} all-to-all(bf16[8,2,32,256]{3,2,1,0:T(8,128)(2,1)S(1)} %convolve.1), channel_id=1, replica_groups=mesh['tm'=8,'x'=2,'core'=2] {'tm'}, dimensions={0} | all-to-all | bytes 524288 | tf_op jit(solution)/shard_map/all_to_all | solution.py:475
  39.6 1.6 %collective-permute-start.3 = (bf16[8,32,256]{2,1,0:T(8,128)(2,1)S(1)}, bf16[8,32,256]{2,1,0:T(8,128)(2,1)S(1)}, u32[]{:S(2)}, u32[]{:S(2)}) collective-permute-start(bf16[8,32,256]{2,1,0:T(8,128)(2,1)S(1)} %get-tuple-element.67.conv0_ref), channel_id=1, source_target_pairs={{0,2},{1,3},{2,0},{3,1},{4,6},{5,7},{6,4},{7,5},{8,10},{9,11},{10,... | collective-permute-start | bytes 393224 | tf_op jit(solution)/shard_map/ppermute | solution.py:416
  41.1 0.0 collective-permute-start.8
  41.1 0.0 collective-permute-done.4.wg1_hbm
  41.2 0.0 collective-permute-done.5.wu1_hbm
  41.2 0.0 collective-permute-done.6.wd1_hbm
  41.2 3.0 %feed_first.1 = (bf16[256,256]{1,0:T(8,128)(2,1)S(1)}, f32[256,1]{1,0:T(8,128)S(1)}, f32[4,1,256]{2,1,0:T(1,128)S(1)}, f32[4,256,512]{2,1,0:T(8,128)S(1)}, bf16[...) custom-call(s32[1]{0:T(128)} %bitcast.1.chip_ref, s32[1]{0:T(128)} %bitcast.core_ref, ...), custom_call_target="tpu_custom_call" | custom-call | tf_op jit(solution)/shard_map/feed_first/pallas_call | solution.py:492
  44.2 0.9 %collective-permute-done.3.conv2_ref = bf16[8,32,256]{2,1,0:T(8,128)(2,1)S(1)} collective-permute-done((bf16[8,32,256]{2,1,0:T(8,128)(2,1)S(1)}, bf16[8,32,256]{2,1,0:T(8,128)(2,1)S(1)}, u32[]{:S(2)}, u32[]{:S(2)}) %collective-permute-start.3) | collective-permute-done | bytes 131104 | tf_op jit(solution)/shard_map/ppermute | solution.py:416
  45.1 0.0 collective-permute-start.7
  45.1 0.5 feed_middle.1
  45.6 1.3 %collective-permute-done.8.conv3_ref = bf16[8,32,256]{2,1,0:T(8,128)(2,1)S(1)} collective-permute-done((bf16[8,32,256]{2,1,0:T(8,128)(2,1)S(1)}, bf16[8,32,256]{2,1,0:T(8,128)(2,1)S(1)}, u32[]{:S(2)}, u32[]{:S(2)}) %collective-permute-start.8) | collective-permute-done | bytes 131104 | tf_op jit(solution)/shard_map/ppermute | solution.py:416
  46.9 0.0 collective-permute-done.7.conv1_ref
  46.9 1.3 %feed_second.1 = (bf16[256,256]{1,0:T(8,128)(2,1)S(1)}, bf16[256,1024]{1,0:T(8,128)(2,1)S(1)}, bf16[256,256]{1,0:T(8,128)(2,1)S(1)}, bf16[256,256]{1,0:T(8,128)(2,1)S(1)}) custom-call(s32[1]{0:T(128)} %bitcast.1.chip_ref, s32[1]{0:T(128)} %bitcast.core_ref, bf16[8,32,256]{2,1,0:T(8,128)(2,1)S(1)} %collective-permute-done.7.conv1_ref, ...), custom_call_target="tpu_custom_call" | custom-call | tf_op jit(solution)/shard_map/feed_second/pallas_call | solution.py:523
  48.3 2.0 %collective-permute-start.9 = (bf16[256,256]{1,0:T(8,128)(2,1)S(1)}, bf16[256,256]{1,0:T(8,128)(2,1)S(1)}, u32[]{:S(2)}, u32[]{:S(2)}) collective-permute-start(bf16[256,256]{1,0:T(8,128)(2,1)S(1)} %get-tuple-element.63), channel_id=1, source_target_pairs={{0,2},{1,3},{2,0},{3,1},{4,6},{5,7},{6,4},{7,5},{8,10},{9,11},{10,... | collective-permute-start | bytes 393224 | tf_op jit(solution)/shard_map/ppermute | solution.py:416
  50.2 0.0 collective-permute-start.11
  50.3 0.5 feed_third.1
  50.7 4.0 %collective-permute-done.9.side_ref = bf16[256,256]{1,0:T(8,128)(2,1)S(1)} collective-permute-done((bf16[256,256]{1,0:T(8,128)(2,1)S(1)}, bf16[256,256]{1,0:T(8,128)(2,1)S(1)}, u32[]{:S(2)}, u32[]{:S(2)}) %collective-permute-start.9) | collective-permute-done | bytes 131104 | tf_op jit(solution)/shard_map/ppermute | solution.py:416
  54.7 0.0 collective-permute-start.10
  54.7 1.6 %collective-permute-done.11.side1_ref = bf16[256,256]{1,0:T(8,128)(2,1)S(1)} collective-permute-done((bf16[256,256]{1,0:T(8,128)(2,1)S(1)}, bf16[256,256]{1,0:T(8,128)(2,1)S(1)}, u32[]{:S(2)}, u32[]{:S(2)}) %collective-permute-start.11) | collective-permute-done | bytes 131104 | tf_op jit(solution)/shard_map/ppermute | solution.py:416
  56.3 0.0 collective-permute-done.10.core1_ref
  56.3 0.8 %finish.1 = bf16[512,256]{1,0:T(8,128)(2,1)} custom-call(s32[1]{0:T(128)} %bitcast.core_ref, f32[256,256]{1,0:T(8,128)S(1)} %get-tuple-element.61.own_ref, bf16[256,256]{1,0:T(8,128)(2,1)S(1)} %collective-permute-done.9.side_ref, bf16[256,256]{1,0:T(8,128)(2,1)S(1)} %collective-permute-done.10.core1_ref, bf16[256,256]{1,0:T(8,128)(2,1)S(1)} %collective-permute-done.11.side1_ref), custom_call_target="tpu_custom_call" | custom-call | tf_op jit(solution)/shard_map/finish/pallas_call | solution.py:554
  (2 shorter events, 0.0 us)
Async XLA Ops:
  0.0 12.8 %copy-start = (f32[256]{0:T(256)S(1)}, f32[256]{0:T(256)}, u32[]{:S(2)}) copy-start(f32[256]{0:T(256)} %param.23) | copy-start | bytes 3076
  0.0 24.6 %copy-start.1 = (bf16[256,512]{1,0:T(8,128)(2,1)S(1)}, bf16[256,512]{1,0:T(8,128)(2,1)}, u32[]{:S(2)}) copy-start(bf16[256,512]{1,0:T(8,128)(2,1)} %constant.30.clone.fh_ref) | copy-start | bytes 786436
  0.0 24.6 %copy-start.2 = (bf16[256,512]{1,0:T(8,128)(2,1)S(1)}, bf16[256,512]{1,0:T(8,128)(2,1)}, u32[]{:S(2)}) copy-start(bf16[256,512]{1,0:T(8,128)(2,1)} %constant.31.clone.fl_ref) | copy-start | bytes 786436
  0.0 10.1 %copy-start.4 = (bf16[512,256]{1,0:T(8,128)(2,1)S(1)}, bf16[512,256]{1,0:T(8,128)(2,1)}, u32[]{:S(2)}) copy-start(bf16[512,256]{1,0:T(8,128)(2,1)} %param.17) | copy-start | bytes 786436
  0.0 10.2 %copy-start.3 = (bf16[1024,512]{1,0:T(8,128)(2,1)S(1)}, bf16[1024,512]{1,0:T(8,128)(2,1)}, u32[]{:S(2)}) copy-start(bf16[1024,512]{1,0:T(8,128)(2,1)} %wg0_hbm.1) | copy-start | bytes 3145732
  2.8 21.8 %all-to-all-start = ((bf16[8,2,32,512]{3,2,1,0:T(8,128)(2,1)}), bf16[8,2,32,512]{3,2,1,0:T(8,128)(2,1)S(1)}, u32[]{:S(2)}, u32[]{:S(2)}) async-start(bf16[8,2,32,512]{3,2,1,0:T(8,128)(2,1)} %prepare.1), calls=%async_computation | async-start | bytes 1048576 | tf_op jit(solution)/shard_map/all_to_all | solution.py:444
  10.2 2.6 %collective-permute-start = (bf16[256,256]{1,0:T(8,128)(2,1)S(1)}, bf16[256,256]{1,0:T(8,128)(2,1)S(1)}, u32[]{:S(2)}, u32[]{:S(2)}) collective-permute-start(bf16[256,256]{1,0:T(8,128)(2,1)S(1)} %get-tuple-element.69), channel_id=1, source_target_pairs={{0,1},{1,0},{2,3},{3,2},{4,5},{5,4},{6,7},{7,6},{8,9},{9,8},{10,11... | collective-permute-start | bytes 393224 | tf_op jit(solution)/shard_map/ppermute | solution.py:416
  10.2 30.9 %collective-permute-start.4 = (bf16[1024,512]{1,0:T(8,128)(2,1)S(1)}, bf16[1024,512]{1,0:T(8,128)(2,1)}, u32[]{:S(2)}, u32[]{:S(2)}) collective-permute-start(bf16[1024,512]{1,0:T(8,128)(2,1)S(1)} %copy-done.3), channel_id=1, source_target_pairs={{0,1},{1,0},{2,3},{3,2},{4,5},{5,4},{6,7},{7,6},{8,9},{9,8},{10,11... | collective-permute-start | bytes 3145736 | tf_op jit(solution)/shard_map/ppermute | solution.py:416
  10.7 30.4 %collective-permute-start.5 = (bf16[1024,512]{1,0:T(8,128)(2,1)}, bf16[1024,512]{1,0:T(8,128)(2,1)}, u32[]{:S(2)}, u32[]{:S(2)}) collective-permute-start(bf16[1024,512]{1,0:T(8,128)(2,1)} %wu0_hbm.1), channel_id=1, source_target_pairs={{0,1},{1,0},{2,3},{3,2},{4,5},{5,4},{6,7},{7,6},{8,9},{9,8},{10,11... | collective-permute-start | bytes 3145736 | tf_op jit(solution)/shard_map/ppermute | solution.py:416
  10.8 30.3 %collective-permute-start.6 = (bf16[512,1024]{1,0:T(8,128)(2,1)}, bf16[512,1024]{1,0:T(8,128)(2,1)}, u32[]{:S(2)}, u32[]{:S(2)}) collective-permute-start(bf16[512,1024]{1,0:T(8,128)(2,1)} %wd0_hbm.1), channel_id=1, source_target_pairs={{0,1},{1,0},{2,3},{3,2},{4,5},{5,4},{6,7},{7,6},{8,9},{9,8},{10,11... | collective-permute-start | bytes 3145736 | tf_op jit(solution)/shard_map/ppermute | solution.py:416
  11.2 6.4 %collective-permute-start.1 = (bf16[256,256]{1,0:T(8,128)(2,1)S(1)}, bf16[256,256]{1,0:T(8,128)(2,1)S(1)}, u32[]{:S(2)}, u32[]{:S(2)}) collective-permute-start(bf16[256,256]{1,0:T(8,128)(2,1)S(1)} %get-tuple-element.37.gate0_ref), channel_id=1, source_target_pairs={{0,2},{1,3},{2,0},{3,1},{4,6},{5,7},{6,4},{7,5},{8,10},{9,11},{10,... | collective-permute-start | bytes 393224 | tf_op jit(solution)/shard_map/ppermute | solution.py:416
  12.7 5.9 %collective-permute-start.2 = (bf16[256,256]{1,0:T(8,128)(2,1)S(1)}, bf16[256,256]{1,0:T(8,128)(2,1)S(1)}, u32[]{:S(2)}, u32[]{:S(2)}) collective-permute-start(bf16[256,256]{1,0:T(8,128)(2,1)S(1)} %get-tuple-element.69), channel_id=1, source_target_pairs={{0,3},{1,2},{2,1},{3,0},{4,7},{5,6},{6,5},{7,4},{8,11},{9,10},{10,... | collective-permute-start | bytes 393224 | tf_op jit(solution)/shard_map/ppermute | solution.py:416
  39.6 5.5 %collective-permute-start.3 = (bf16[8,32,256]{2,1,0:T(8,128)(2,1)S(1)}, bf16[8,32,256]{2,1,0:T(8,128)(2,1)S(1)}, u32[]{:S(2)}, u32[]{:S(2)}) collective-permute-start(bf16[8,32,256]{2,1,0:T(8,128)(2,1)S(1)} %get-tuple-element.67.conv0_ref), channel_id=1, source_target_pairs={{0,2},{1,3},{2,0},{3,1},{4,6},{5,7},{6,4},{7,5},{8,10},{9,11},{10,... | collective-permute-start | bytes 393224 | tf_op jit(solution)/shard_map/ppermute | solution.py:416
  41.1 5.8 %collective-permute-start.8 = (bf16[8,32,256]{2,1,0:T(8,128)(2,1)S(1)}, bf16[8,32,256]{2,1,0:T(8,128)(2,1)S(1)}, u32[]{:S(2)}, u32[]{:S(2)}) collective-permute-start(bf16[8,32,256]{2,1,0:T(8,128)(2,1)S(1)} %get-tuple-element.45), channel_id=1, source_target_pairs={{0,3},{1,2},{2,1},{3,0},{4,7},{5,6},{6,5},{7,4},{8,11},{9,10},{10,... | collective-permute-start | bytes 393224 | tf_op jit(solution)/shard_map/ppermute | solution.py:416
  45.1 1.8 %collective-permute-start.7 = (bf16[8,32,256]{2,1,0:T(8,128)(2,1)S(1)}, bf16[8,32,256]{2,1,0:T(8,128)(2,1)S(1)}, u32[]{:S(2)}, u32[]{:S(2)}) collective-permute-start(bf16[8,32,256]{2,1,0:T(8,128)(2,1)S(1)} %get-tuple-element.45), channel_id=1, source_target_pairs={{0,1},{1,0},{2,3},{3,2},{4,5},{5,4},{6,7},{7,6},{8,9},{9,8},{10,11... | collective-permute-start | bytes 393224 | tf_op jit(solution)/shard_map/ppermute | solution.py:416
  48.3 6.4 %collective-permute-start.9 = (bf16[256,256]{1,0:T(8,128)(2,1)S(1)}, bf16[256,256]{1,0:T(8,128)(2,1)S(1)}, u32[]{:S(2)}, u32[]{:S(2)}) collective-permute-start(bf16[256,256]{1,0:T(8,128)(2,1)S(1)} %get-tuple-element.63), channel_id=1, source_target_pairs={{0,2},{1,3},{2,0},{3,1},{4,6},{5,7},{6,4},{7,5},{8,10},{9,11},{10,... | collective-permute-start | bytes 393224 | tf_op jit(solution)/shard_map/ppermute | solution.py:416
  50.2 6.0 %collective-permute-start.11 = (bf16[256,256]{1,0:T(8,128)(2,1)S(1)}, bf16[256,256]{1,0:T(8,128)(2,1)S(1)}, u32[]{:S(2)}, u32[]{:S(2)}) collective-permute-start(bf16[256,256]{1,0:T(8,128)(2,1)S(1)} %get-tuple-element.66), channel_id=1, source_target_pairs={{0,3},{1,2},{2,1},{3,0},{4,7},{5,6},{6,5},{7,4},{8,11},{9,10},{10,... | collective-permute-start | bytes 393224 | tf_op jit(solution)/shard_map/ppermute | solution.py:416
  54.7 1.6 %collective-permute-start.10 = (bf16[256,256]{1,0:T(8,128)(2,1)S(1)}, bf16[256,256]{1,0:T(8,128)(2,1)S(1)}, u32[]{:S(2)}, u32[]{:S(2)}) collective-permute-start(bf16[256,256]{1,0:T(8,128)(2,1)S(1)} %get-tuple-element.65), channel_id=1, source_target_pairs={{0,1},{1,0},{2,3},{3,2},{4,5},{5,4},{6,7},{7,6},{8,9},{9,8},{10,11... | collective-permute-start | bytes 393224 | tf_op jit(solution)/shard_map/ppermute | solution.py:416

commit v9 on v8

--- a/solution.py
+++ b/solution.py
@@ -366,12 +366,30 @@
         out_ref[...] = part.astype(out_ref.dtype)
 
 
-def finish_kernel(core_ref, own_ref, side_ref, core1_ref, side1_ref, out_ref):
-    block = own_ref.shape[0]
-    same = pl.ds(pl.multiple_of(core_ref[0] * block, block), block)
-    other = pl.ds(pl.multiple_of((1 - core_ref[0]) * block, block), block)
-    out_ref[same, :] = (own_ref[...] + side_ref[...].astype(f32)).astype(bf16)
-    out_ref[other, :] = (core1_ref[...].astype(f32) + side1_ref[...].astype(f32)).astype(bf16)
+def finish_kernel(flip, core_ref, base_ref, add_ref, *rest):
+    out_hbm, sum_ref, sem = rest[-3:]
+    block = base_ref.shape[0]
+    first = (core_ref[0] ^ flip) * block
+    sum_ref[...] = (base_ref[...].astype(f32) + add_ref[...].astype(f32)).astype(bf16)
+    store = pltpu.make_async_copy(
+        sum_ref, out_hbm.at[pl.ds(pl.multiple_of(first, block), block)], sem
+    )
+    store.start()
+    store.wait()
+
+
+def finish(flip, core, base, add, *into):
+    block, width = base.shape
+    return pl.pallas_call(
+        functools.partial(finish_kernel, flip),
+        out_shape=jax.ShapeDtypeStruct((2 * block, width), bf16),
+        in_specs=[whole(SMEM)] + [whole()] * 2 + [whole(HBM)] * len(into),
+        out_specs=whole(HBM),
+        scratch_shapes=[pltpu.VMEM((block, width), bf16), pltpu.SemaphoreType.DMA],
+        input_output_aliases={3: 0} if into else {},
+        compiler_params=params(8),
+        name="finish",
+    )(core, base, add, *into)
 
 
 VMEM = pltpu.MemorySpace.VMEM
@@ -551,14 +569,8 @@
     )(*place, hidden, down, mixed0, mixed1)
     owned, lent = local
     lent, side = lax.optimization_barrier((lent, side))
-    return pl.pallas_call(
-        finish_kernel,
-        out_shape=jax.ShapeDtypeStruct((rows, width), bf16),
-        in_specs=[whole(SMEM)] + [whole()] * 4,
-        out_specs=whole(),
-        compiler_params=params(8),
-        name="finish",
-    )(place[1], owned, side, swap(lent, 1), side1)
+    half = finish(0, place[1], owned, side)
+    return finish(1, place[1], swap(lent, 1), side1, half)
 
 
 def solution(mesh):

time: 57.3 us -> 57.2 us (level)
  waiting for transfers between devices: 19.5 us -> 18.8 us
  Pallas kernels: 10.5 us -> 11.1 us
    ppermute x12, waiting for transfers between devices: 13.5 us -> 12.8 us  [swap(): lax.ppermute(values, ('x', 'core'), [(at, at ^ bits) for at in range(4)])]
    pallas_call x1 -> x2, Pallas kernels: 0.76 us -> 1.38 us  [finish(): pl.pallas_call(functools.partial(finish_kernel, flip), out_shape=jax.Shap...]
  transfers between devices with their start and end apart: 13 -> 13, of which waited for: 7 -> 7; matrix products, arithmetic and copies ran while one was open for 0% -> 0% of each run, Pallas kernels for 11% -> 12%
where the time goes in v9:
time: 57.2 us; the launch traced here: 57 us
  waiting for transfers between devices  18.8 us (33%)
  starting transfers between devices  13.5 us (24%)
  blocking collectives  12.5 us (22%)
  Pallas kernels  11.1 us (19%)
  between operations  0.9 us (2%)
    ppermute x12, waiting for transfers between devices, swap(): lax.ppermute(values, ('x', 'core'), [(at, at ^ bits) for at in range(4)])  12.8 us
    all_to_all x1, blocking collectives, shards(): conv = lax.all_to_all(conv, 'tm', split_axis=0, concat_axis=0, tiled=True)  12.5 us
    all_to_all x1, starting transfers between devices, shards(): both = lax.all_to_all(made, 'tm', split_axis=0, concat_axis=0, tiled=True)  7.3 us
    ppermute x12, starting transfers between devices, swap(): lax.ppermute(values, ('x', 'core'), [(at, at ^ bits) for at in range(4)])  6.17 us
    all_to_all x1, waiting for transfers between devices, shards(): both = lax.all_to_all(made, 'tm', split_axis=0, concat_axis=0, tiled=True)  5.93 us
    pallas_call x1, Pallas kernels, shards(): pl.pallas_call(feed_first_kernel, out_shape=[jax.ShapeDtypeStruct(*spec)...  3 us
    pallas_call x1, Pallas kernels, shards(): pl.pallas_call(convolve_kernel, out_shape=jax.ShapeDtypeStruct((tm, 2, he...  2.41 us
    pallas_call x1, Pallas kernels, shards(): pl.pallas_call(prepare_kernel, out_shape=jax.ShapeDtypeStruct(shape, bf16...  2.01 us
  transfers between devices with their start and end apart: 13, of which 7 were waited for; matrix products, arithmetic and copies ran while one was open for 0% of the time, Pallas kernels for 12%

profile of v9, /device:TPU:0, one launch (start us, length us, event | category | flops | bytes accessed | tf_op | source)
XLA Modules:
  0.0 57.0 jit_solution(13296525388989901965)
XLA Ops:
  0.0 0.0 copy-start
  0.0 0.0 copy-start.1
  0.0 0.0 copy-start.2
  0.0 0.0 copy-start.4
  0.0 0.0 copy-start.3
  0.8 2.0 %prepare.1 = bf16[8,2,32,512]{3,2,1,0:T(8,128)(2,1)} custom-call(s32[1]{0:T(128)S(6)} %copy.26.step_ref, s32[8]{0:T(128)} %flags_hbm.1, bf16[512,256]{1,0:T(8,128)(2,1)} %value_hbm.1, bf16[512,256]{1,0:T(8,128)(2,1)} %filter_hbm.1, f32[200,256]{1,0:T(8,128)} %table_hbm.1, f32[1,256]{1,0:T(1,128)} %bitcast.15), custom_call_target="tpu_custom_call" | custom-call | tf_op jit(solution)/shard_map/prepare/pallas_call | solution.py:438
  2.8 7.3 %all-to-all-start = ((bf16[8,2,32,512]{3,2,1,0:T(8,128)(2,1)}), bf16[8,2,32,512]{3,2,1,0:T(8,128)(2,1)S(1)}, u32[]{:S(2)}, u32[]{:S(2)}) async-start(bf16[8,2,32,512]{3,2,1,0:T(8,128)(2,1)} %prepare.1), calls=%async_computation | async-start | bytes 1048576 | tf_op jit(solution)/shard_map/all_to_all | solution.py:462
  10.1 0.0 copy-done.4
  10.2 0.1 collective-permute-start
  10.2 0.0 copy-done.3
  10.2 0.5 collective-permute-start.4
  10.7 0.1 collective-permute-start.5
  10.8 0.4 collective-permute-start.6
  11.2 1.5 %collective-permute-start.1 = (bf16[256,256]{1,0:T(8,128)(2,1)S(1)}, bf16[256,256]{1,0:T(8,128)(2,1)S(1)}, u32[]{:S(2)}, u32[]{:S(2)}) collective-permute-start(bf16[256,256]{1,0:T(8,128)(2,1)S(1)} %get-tuple-element.37.gate0_ref), channel_id=1, source_target_pairs={{0,2},{1,3},{2,0},{3,1},{4,6},{5,7},{6,4},{7,5},{8,10},{9,11},{10,... | collective-permute-start | bytes 393224 | tf_op jit(solution)/shard_map/ppermute | solution.py:434
  12.7 0.0 collective-permute-done.gate1_ref
  12.7 0.1 collective-permute-start.2
  12.8 0.0 copy-done
  12.8 0.1 dynamic-slice_bitcast_fusion
  12.9 0.1 copy.20.skip_ref
  13.0 4.6 %collective-permute-done.1.gate2_ref = bf16[256,256]{1,0:T(8,128)(2,1)S(1)} collective-permute-done((bf16[256,256]{1,0:T(8,128)(2,1)S(1)}, bf16[256,256]{1,0:T(8,128)(2,1)S(1)}, u32[]{:S(2)}, u32[]{:S(2)}) %collective-permute-start.1) | collective-permute-done | bytes 131104 | tf_op jit(solution)/shard_map/ppermute | solution.py:434
  17.6 1.1 %collective-permute-done.2.gate3_ref = bf16[256,256]{1,0:T(8,128)(2,1)S(1)} collective-permute-done((bf16[256,256]{1,0:T(8,128)(2,1)S(1)}, bf16[256,256]{1,0:T(8,128)(2,1)S(1)}, u32[]{:S(2)}, u32[]{:S(2)}) %collective-permute-start.2) | collective-permute-done | bytes 131104 | tf_op jit(solution)/shard_map/ppermute | solution.py:434
  18.7 5.9 %all-to-all-done.both_ref = bf16[8,2,32,512]{3,2,1,0:T(8,128)(2,1)S(1)} async-done(((bf16[8,2,32,512]{3,2,1,0:T(8,128)(2,1)}), bf16[8,2,32,512]{3,2,1,0:T(8,128)(2,1)S(1)}, u32[]{:S(2)}, u32[]{:S(2)}) %all-to-all-start) | async-done | bytes 524320 | tf_op jit(solution)/shard_map/all_to_all | solution.py:462
  24.6 0.0 copy-done.1
  24.6 0.0 copy-done.2
  24.6 2.4 %convolve.1 = bf16[8,2,32,256]{3,2,1,0:T(8,128)(2,1)S(1)} custom-call(s32[1]{0:T(128)} %bitcast.core_ref, bf16[8,2,32,512]{3,2,1,0:T(8,128)(2,1)S(1)} %all-to-all-done.both_ref, bf16[256,512]{1,0:T(8,128)(2,1)S(1)} %copy-done.1, bf16[256,512]{1,0:T(8,128)(2,1)S(1)} %copy-done.2, bf16[512,256]{1,0:T(8,128)(2,1)} %constant.32.clone.gh_hbm, ...), custom_call_target="tpu_custom_call" | custom-call | tf_op jit(solution)/shard_map/convolve/pallas_call | solution.py:479
  27.0 12.5 %all_to_all.10 = bf16[8,2,32,256]{3,2,1,0:T(8,128)(2,1)S(1)} all-to-all(bf16[8,2,32,256]{3,2,1,0:T(8,128)(2,1)S(1)} %convolve.1), channel_id=1, replica_groups=mesh['tm'=8,'x'=2,'core'=2] {'tm'}, dimensions={0} | all-to-all | bytes 524288 | tf_op jit(solution)/shard_map/all_to_all | solution.py:493
  39.6 1.6 %collective-permute-start.3 = (bf16[8,32,256]{2,1,0:T(8,128)(2,1)S(1)}, bf16[8,32,256]{2,1,0:T(8,128)(2,1)S(1)}, u32[]{:S(2)}, u32[]{:S(2)}) collective-permute-start(bf16[8,32,256]{2,1,0:T(8,128)(2,1)S(1)} %get-tuple-element.67.conv0_ref), channel_id=1, source_target_pairs={{0,2},{1,3},{2,0},{3,1},{4,6},{5,7},{6,4},{7,5},{8,10},{9,11},{10,... | collective-permute-start | bytes 393224 | tf_op jit(solution)/shard_map/ppermute | solution.py:434
  41.1 0.0 collective-permute-start.8
  41.1 0.0 collective-permute-done.4.wg1_hbm
  41.2 0.0 collective-permute-done.5.wu1_hbm
  41.2 0.0 collective-permute-done.6.wd1_hbm
  41.2 3.0 %feed_first.1 = (bf16[256,256]{1,0:T(8,128)(2,1)S(1)}, f32[256,1]{1,0:T(8,128)S(1)}, f32[4,1,256]{2,1,0:T(1,128)S(1)}, f32[4,256,512]{2,1,0:T(8,128)S(1)}, bf16[...) custom-call(s32[1]{0:T(128)} %bitcast.1.chip_ref, s32[1]{0:T(128)} %bitcast.core_ref, ...), custom_call_target="tpu_custom_call" | custom-call | tf_op jit(solution)/shard_map/feed_first/pallas_call | solution.py:510
  44.2 0.9 %collective-permute-done.3.conv2_ref = bf16[8,32,256]{2,1,0:T(8,128)(2,1)S(1)} collective-permute-done((bf16[8,32,256]{2,1,0:T(8,128)(2,1)S(1)}, bf16[8,32,256]{2,1,0:T(8,128)(2,1)S(1)}, u32[]{:S(2)}, u32[]{:S(2)}) %collective-permute-start.3) | collective-permute-done | bytes 131104 | tf_op jit(solution)/shard_map/ppermute | solution.py:434
  45.1 0.0 collective-permute-start.7
  45.1 0.5 feed_middle.1
  45.6 1.3 %collective-permute-done.8.conv3_ref = bf16[8,32,256]{2,1,0:T(8,128)(2,1)S(1)} collective-permute-done((bf16[8,32,256]{2,1,0:T(8,128)(2,1)S(1)}, bf16[8,32,256]{2,1,0:T(8,128)(2,1)S(1)}, u32[]{:S(2)}, u32[]{:S(2)}) %collective-permute-start.8) | collective-permute-done | bytes 131104 | tf_op jit(solution)/shard_map/ppermute | solution.py:434
  46.9 0.0 collective-permute-done.7.conv1_ref
  46.9 1.3 %feed_second.1 = (bf16[256,256]{1,0:T(8,128)(2,1)S(1)}, bf16[256,1024]{1,0:T(8,128)(2,1)S(1)}, bf16[256,256]{1,0:T(8,128)(2,1)S(1)}, bf16[256,256]{1,0:T(8,128)(2,1)S(1)}) custom-call(s32[1]{0:T(128)} %bitcast.1.chip_ref, s32[1]{0:T(128)} %bitcast.core_ref, bf16[8,32,256]{2,1,0:T(8,128)(2,1)S(1)} %collective-permute-done.7.conv1_ref, ...), custom_call_target="tpu_custom_call" | custom-call | tf_op jit(solution)/shard_map/feed_second/pallas_call | solution.py:541
  48.3 2.0 %collective-permute-start.9 = (bf16[256,256]{1,0:T(8,128)(2,1)S(1)}, bf16[256,256]{1,0:T(8,128)(2,1)S(1)}, u32[]{:S(2)}, u32[]{:S(2)}) collective-permute-start(bf16[256,256]{1,0:T(8,128)(2,1)S(1)} %get-tuple-element.62), channel_id=1, source_target_pairs={{0,2},{1,3},{2,0},{3,1},{4,6},{5,7},{6,4},{7,5},{8,10},{9,11},{10,... | collective-permute-start | bytes 393224 | tf_op jit(solution)/shard_map/ppermute | solution.py:434
  50.2 0.0 collective-permute-start.11
  50.3 0.5 feed_third.1
  50.7 4.0 %collective-permute-done.9.add_ref = bf16[256,256]{1,0:T(8,128)(2,1)S(1)} collective-permute-done((bf16[256,256]{1,0:T(8,128)(2,1)S(1)}, bf16[256,256]{1,0:T(8,128)(2,1)S(1)}, u32[]{:S(2)}, u32[]{:S(2)}) %collective-permute-start.9) | collective-permute-done | bytes 131104 | tf_op jit(solution)/shard_map/ppermute | solution.py:434
  54.7 0.0 collective-permute-start.10
  54.7 0.7 %finish.2.rest_0_ = bf16[512,256]{1,0:T(8,128)(2,1)} custom-call(s32[1]{0:T(128)} %bitcast.core_ref, f32[256,256]{1,0:T(8,128)S(1)} %get-tuple-element.65.base_ref, bf16[256,256]{1,0:T(8,128)(2,1)S(1)} %collective-permute-done.9.add_ref), custom_call_target="tpu_custom_call" | custom-call | tf_op jit(solution)/shard_map/finish/pallas_call | solution.py:383
  55.4 0.9 %collective-permute-done.11.add_ref = bf16[256,256]{1,0:T(8,128)(2,1)S(1)} collective-permute-done((bf16[256,256]{1,0:T(8,128)(2,1)S(1)}, bf16[256,256]{1,0:T(8,128)(2,1)S(1)}, u32[]{:S(2)}, u32[]{:S(2)}) %collective-permute-start.11) | collective-permute-done | bytes 131104 | tf_op jit(solution)/shard_map/ppermute | solution.py:434
  56.3 0.0 collective-permute-done.10.base_ref
  56.3 0.7 %finish.3 = bf16[512,256]{1,0:T(8,128)(2,1)} custom-call(s32[1]{0:T(128)} %bitcast.core_ref, bf16[256,256]{1,0:T(8,128)(2,1)S(1)} %collective-permute-done.10.base_ref, bf16[256,256]{1,0:T(8,128)(2,1)S(1)} %collective-permute-done.11.add_ref, bf16[512,256]{1,0:T(8,128)(2,1)} %finish.2.rest_0_), custom_call_target="tpu_custom_call", output_to_operand_aliasing={{}: (3, {})} | custom-call | tf_op jit(solution)/shard_map/finish/pallas_call | solution.py:383
  (2 shorter events, 0.0 us)
Async XLA Ops:
  0.0 12.8 %copy-start = (f32[256]{0:T(256)S(1)}, f32[256]{0:T(256)}, u32[]{:S(2)}) copy-start(f32[256]{0:T(256)} %param.23) | copy-start | bytes 3076
  0.0 24.6 %copy-start.1 = (bf16[256,512]{1,0:T(8,128)(2,1)S(1)}, bf16[256,512]{1,0:T(8,128)(2,1)}, u32[]{:S(2)}) copy-start(bf16[256,512]{1,0:T(8,128)(2,1)} %constant.30.clone.fh_ref) | copy-start | bytes 786436
  0.0 24.6 %copy-start.2 = (bf16[256,512]{1,0:T(8,128)(2,1)S(1)}, bf16[256,512]{1,0:T(8,128)(2,1)}, u32[]{:S(2)}) copy-start(bf16[256,512]{1,0:T(8,128)(2,1)} %constant.31.clone.fl_ref) | copy-start | bytes 786436
  0.0 10.1 %copy-start.4 = (bf16[512,256]{1,0:T(8,128)(2,1)S(1)}, bf16[512,256]{1,0:T(8,128)(2,1)}, u32[]{:S(2)}) copy-start(bf16[512,256]{1,0:T(8,128)(2,1)} %param.17) | copy-start | bytes 786436
  0.0 10.2 %copy-start.3 = (bf16[1024,512]{1,0:T(8,128)(2,1)S(1)}, bf16[1024,512]{1,0:T(8,128)(2,1)}, u32[]{:S(2)}) copy-start(bf16[1024,512]{1,0:T(8,128)(2,1)} %wg0_hbm.1) | copy-start | bytes 3145732
  2.8 21.8 %all-to-all-start = ((bf16[8,2,32,512]{3,2,1,0:T(8,128)(2,1)}), bf16[8,2,32,512]{3,2,1,0:T(8,128)(2,1)S(1)}, u32[]{:S(2)}, u32[]{:S(2)}) async-start(bf16[8,2,32,512]{3,2,1,0:T(8,128)(2,1)} %prepare.1), calls=%async_computation | async-start | bytes 1048576 | tf_op jit(solution)/shard_map/all_to_all | solution.py:462
  10.2 2.6 %collective-permute-start = (bf16[256,256]{1,0:T(8,128)(2,1)S(1)}, bf16[256,256]{1,0:T(8,128)(2,1)S(1)}, u32[]{:S(2)}, u32[]{:S(2)}) collective-permute-start(bf16[256,256]{1,0:T(8,128)(2,1)S(1)} %get-tuple-element.69), channel_id=1, source_target_pairs={{0,1},{1,0},{2,3},{3,2},{4,5},{5,4},{6,7},{7,6},{8,9},{9,8},{10,11... | collective-permute-start | bytes 393224 | tf_op jit(solution)/shard_map/ppermute | solution.py:434
  10.2 30.9 %collective-permute-start.4 = (bf16[1024,512]{1,0:T(8,128)(2,1)S(1)}, bf16[1024,512]{1,0:T(8,128)(2,1)}, u32[]{:S(2)}, u32[]{:S(2)}) collective-permute-start(bf16[1024,512]{1,0:T(8,128)(2,1)S(1)} %copy-done.3), channel_id=1, source_target_pairs={{0,1},{1,0},{2,3},{3,2},{4,5},{5,4},{6,7},{7,6},{8,9},{9,8},{10,11... | collective-permute-start | bytes 3145736 | tf_op jit(solution)/shard_map/ppermute | solution.py:434
  10.7 30.4 %collective-permute-start.5 = (bf16[1024,512]{1,0:T(8,128)(2,1)}, bf16[1024,512]{1,0:T(8,128)(2,1)}, u32[]{:S(2)}, u32[]{:S(2)}) collective-permute-start(bf16[1024,512]{1,0:T(8,128)(2,1)} %wu0_hbm.1), channel_id=1, source_target_pairs={{0,1},{1,0},{2,3},{3,2},{4,5},{5,4},{6,7},{7,6},{8,9},{9,8},{10,11... | collective-permute-start | bytes 3145736 | tf_op jit(solution)/shard_map/ppermute | solution.py:434
  10.8 30.3 %collective-permute-start.6 = (bf16[512,1024]{1,0:T(8,128)(2,1)}, bf16[512,1024]{1,0:T(8,128)(2,1)}, u32[]{:S(2)}, u32[]{:S(2)}) collective-permute-start(bf16[512,1024]{1,0:T(8,128)(2,1)} %wd0_hbm.1), channel_id=1, source_target_pairs={{0,1},{1,0},{2,3},{3,2},{4,5},{5,4},{6,7},{7,6},{8,9},{9,8},{10,11... | collective-permute-start | bytes 3145736 | tf_op jit(solution)/shard_map/ppermute | solution.py:434
  11.2 6.4 %collective-permute-start.1 = (bf16[256,256]{1,0:T(8,128)(2,1)S(1)}, bf16[256,256]{1,0:T(8,128)(2,1)S(1)}, u32[]{:S(2)}, u32[]{:S(2)}) collective-permute-start(bf16[256,256]{1,0:T(8,128)(2,1)S(1)} %get-tuple-element.37.gate0_ref), channel_id=1, source_target_pairs={{0,2},{1,3},{2,0},{3,1},{4,6},{5,7},{6,4},{7,5},{8,10},{9,11},{10,... | collective-permute-start | bytes 393224 | tf_op jit(solution)/shard_map/ppermute | solution.py:434
  12.7 5.9 %collective-permute-start.2 = (bf16[256,256]{1,0:T(8,128)(2,1)S(1)}, bf16[256,256]{1,0:T(8,128)(2,1)S(1)}, u32[]{:S(2)}, u32[]{:S(2)}) collective-permute-start(bf16[256,256]{1,0:T(8,128)(2,1)S(1)} %get-tuple-element.69), channel_id=1, source_target_pairs={{0,3},{1,2},{2,1},{3,0},{4,7},{5,6},{6,5},{7,4},{8,11},{9,10},{10,... | collective-permute-start | bytes 393224 | tf_op jit(solution)/shard_map/ppermute | solution.py:434
  39.6 5.5 %collective-permute-start.3 = (bf16[8,32,256]{2,1,0:T(8,128)(2,1)S(1)}, bf16[8,32,256]{2,1,0:T(8,128)(2,1)S(1)}, u32[]{:S(2)}, u32[]{:S(2)}) collective-permute-start(bf16[8,32,256]{2,1,0:T(8,128)(2,1)S(1)} %get-tuple-element.67.conv0_ref), channel_id=1, source_target_pairs={{0,2},{1,3},{2,0},{3,1},{4,6},{5,7},{6,4},{7,5},{8,10},{9,11},{10,... | collective-permute-start | bytes 393224 | tf_op jit(solution)/shard_map/ppermute | solution.py:434
  41.1 5.8 %collective-permute-start.8 = (bf16[8,32,256]{2,1,0:T(8,128)(2,1)S(1)}, bf16[8,32,256]{2,1,0:T(8,128)(2,1)S(1)}, u32[]{:S(2)}, u32[]{:S(2)}) collective-permute-start(bf16[8,32,256]{2,1,0:T(8,128)(2,1)S(1)} %get-tuple-element.45), channel_id=1, source_target_pairs={{0,3},{1,2},{2,1},{3,0},{4,7},{5,6},{6,5},{7,4},{8,11},{9,10},{10,... | collective-permute-start | bytes 393224 | tf_op jit(solution)/shard_map/ppermute | solution.py:434
  45.1 1.8 %collective-permute-start.7 = (bf16[8,32,256]{2,1,0:T(8,128)(2,1)S(1)}, bf16[8,32,256]{2,1,0:T(8,128)(2,1)S(1)}, u32[]{:S(2)}, u32[]{:S(2)}) collective-permute-start(bf16[8,32,256]{2,1,0:T(8,128)(2,1)S(1)} %get-tuple-element.45), channel_id=1, source_target_pairs={{0,1},{1,0},{2,3},{3,2},{4,5},{5,4},{6,7},{7,6},{8,9},{9,8},{10,11... | collective-permute-start | bytes 393224 | tf_op jit(solution)/shard_map/ppermute | solution.py:434
  48.3 6.4 %collective-permute-start.9 = (bf16[256,256]{1,0:T(8,128)(2,1)S(1)}, bf16[256,256]{1,0:T(8,128)(2,1)S(1)}, u32[]{:S(2)}, u32[]{:S(2)}) collective-permute-start(bf16[256,256]{1,0:T(8,128)(2,1)S(1)} %get-tuple-element.62), channel_id=1, source_target_pairs={{0,2},{1,3},{2,0},{3,1},{4,6},{5,7},{6,4},{7,5},{8,10},{9,11},{10,... | collective-permute-start | bytes 393224 | tf_op jit(solution)/shard_map/ppermute | solution.py:434
  50.2 6.0 %collective-permute-start.11 = (bf16[256,256]{1,0:T(8,128)(2,1)S(1)}, bf16[256,256]{1,0:T(8,128)(2,1)S(1)}, u32[]{:S(2)}, u32[]{:S(2)}) collective-permute-start(bf16[256,256]{1,0:T(8,128)(2,1)S(1)} %get-tuple-element.64), channel_id=1, source_target_pairs={{0,3},{1,2},{2,1},{3,0},{4,7},{5,6},{6,5},{7,4},{8,11},{9,10},{10,... | collective-permute-start | bytes 393224 | tf_op jit(solution)/shard_map/ppermute | solution.py:434
  54.7 1.6 %collective-permute-start.10 = (bf16[256,256]{1,0:T(8,128)(2,1)S(1)}, bf16[256,256]{1,0:T(8,128)(2,1)S(1)}, u32[]{:S(2)}, u32[]{:S(2)}) collective-permute-start(bf16[256,256]{1,0:T(8,128)(2,1)S(1)} %get-tuple-element.63), channel_id=1, source_target_pairs={{0,1},{1,0},{2,3},{3,2},{4,5},{5,4},{6,7},{7,6},{8,9},{9,8},{10,11... | collective-permute-start | bytes 393224 | tf_op jit(solution)/shard_map/ppermute | solution.py:434

commit v10 on v9

--- a/solution.py
+++ b/solution.py
@@ -345,10 +345,15 @@
         gate = scale * (sums_ref[2 * at] + dot(ready, rest_ref[2 * at]))
         up = scale * (sums_ref[2 * at + 1] + dot(ready, rest_ref[2 * at + 1]))
         parts.append((gate / (1.0 + jnp.exp(-gate)) * up).astype(bf16))
-    hidden = jnp.concatenate(parts, axis=1)
-    hidden_ref[...] = hidden
-    for j, out_ref in ((2, out2_ref), (3, out3_ref)):
-        out_ref[...] = piece(hidden, down_ref, here ^ j, width).astype(bf16)
+    size = parts[0].shape[1]
+    for at, values in enumerate(parts):
+        hidden_ref[:, at * size : (at + 1) * size] = values
+    away = pl.ds(pl.multiple_of((1 - chip_ref[0]) * 2 * width, 2 * width), 2 * width)
+    both = dot(parts[0], down_ref[:size, away]) + dot(parts[1], down_ref[size:, away])
+    low, high = both[:, :width].astype(bf16), both[:, width:].astype(bf16)
+    first = core_ref[0] == 0
+    out2_ref[...] = jnp.where(first, low, high)
+    out3_ref[...] = jnp.where(first, high, low)
 
 
 def piece(hidden, down_ref, at, width):

time: 57.2 us -> 57.2 us (level)
  no operation moved by 1% of the time
where the time goes in v10:
time: 57.2 us; the launch traced here: 56.9 us
  waiting for transfers between devices  18.8 us (33%)
  starting transfers between devices  13.5 us (24%)
  blocking collectives  12.5 us (22%)
  Pallas kernels  11 us (19%)
  between operations  0.9 us (2%)
    ppermute x12, waiting for transfers between devices, swap(): lax.ppermute(values, ('x', 'core'), [(at, at ^ bits) for at in range(4)])  12.8 us
    all_to_all x1, blocking collectives, shards(): conv = lax.all_to_all(conv, 'tm', split_axis=0, concat_axis=0, tiled=True)  12.5 us
    all_to_all x1, starting transfers between devices, shards(): both = lax.all_to_all(made, 'tm', split_axis=0, concat_axis=0, tiled=True)  7.3 us
    ppermute x12, starting transfers between devices, swap(): lax.ppermute(values, ('x', 'core'), [(at, at ^ bits) for at in range(4)])  6.15 us
    all_to_all x1, waiting for transfers between devices, shards(): both = lax.all_to_all(made, 'tm', split_axis=0, concat_axis=0, tiled=True)  5.93 us
    pallas_call x1, Pallas kernels, shards(): pl.pallas_call(feed_first_kernel, out_shape=[jax.ShapeDtypeStruct(*spec)...  3 us
    pallas_call x1, Pallas kernels, shards(): pl.pallas_call(convolve_kernel, out_shape=jax.ShapeDtypeStruct((tm, 2, he...  2.41 us
    pallas_call x1, Pallas kernels, shards(): pl.pallas_call(prepare_kernel, out_shape=jax.ShapeDtypeStruct(shape, bf16...  2.01 us
  transfers between devices with their start and end apart: 13, of which 7 were waited for; matrix products, arithmetic and copies ran while one was open for 0% of the time, Pallas kernels for 12%

profile of v10, /device:TPU:0, one launch (start us, length us, event | category | flops | bytes accessed | tf_op | source)
XLA Modules:
  0.0 56.9 jit_solution(6103663456208611042)
XLA Ops:
  0.0 0.0 copy-start
  0.0 0.0 copy-start.1
  0.0 0.0 copy-start.2
  0.0 0.0 copy-start.4
  0.0 0.0 copy-start.3
  0.8 2.0 %prepare.1 = bf16[8,2,32,512]{3,2,1,0:T(8,128)(2,1)} custom-call(s32[1]{0:T(128)S(6)} %copy.26.step_ref, s32[8]{0:T(128)} %flags_hbm.1, bf16[512,256]{1,0:T(8,128)(2,1)} %value_hbm.1, bf16[512,256]{1,0:T(8,128)(2,1)} %filter_hbm.1, f32[200,256]{1,0:T(8,128)} %table_hbm.1, f32[1,256]{1,0:T(1,128)} %bitcast.15), custom_call_target="tpu_custom_call" | custom-call | tf_op jit(solution)/shard_map/prepare/pallas_call | solution.py:443
  2.8 7.3 %all-to-all-start = ((bf16[8,2,32,512]{3,2,1,0:T(8,128)(2,1)}), bf16[8,2,32,512]{3,2,1,0:T(8,128)(2,1)S(1)}, u32[]{:S(2)}, u32[]{:S(2)}) async-start(bf16[8,2,32,512]{3,2,1,0:T(8,128)(2,1)} %prepare.1), calls=%async_computation | async-start | bytes 1048576 | tf_op jit(solution)/shard_map/all_to_all | solution.py:467
  10.1 0.0 copy-done.4
  10.2 0.1 collective-permute-start
  10.2 0.0 copy-done.3
  10.2 0.5 collective-permute-start.4
  10.7 0.1 collective-permute-start.5
  10.8 0.4 collective-permute-start.6
  11.2 1.5 %collective-permute-start.1 = (bf16[256,256]{1,0:T(8,128)(2,1)S(1)}, bf16[256,256]{1,0:T(8,128)(2,1)S(1)}, u32[]{:S(2)}, u32[]{:S(2)}) collective-permute-start(bf16[256,256]{1,0:T(8,128)(2,1)S(1)} %get-tuple-element.37.gate0_ref), channel_id=1, source_target_pairs={{0,2},{1,3},{2,0},{3,1},{4,6},{5,7},{6,4},{7,5},{8,10},{9,11},{10,... | collective-permute-start | bytes 393224 | tf_op jit(solution)/shard_map/ppermute | solution.py:439
  12.7 0.0 collective-permute-done.gate1_ref
  12.7 0.1 collective-permute-start.2
  12.8 0.0 copy-done
  12.8 0.1 dynamic-slice_bitcast_fusion
  12.9 0.1 copy.20.skip_ref
  13.0 4.6 %collective-permute-done.1.gate2_ref = bf16[256,256]{1,0:T(8,128)(2,1)S(1)} collective-permute-done((bf16[256,256]{1,0:T(8,128)(2,1)S(1)}, bf16[256,256]{1,0:T(8,128)(2,1)S(1)}, u32[]{:S(2)}, u32[]{:S(2)}) %collective-permute-start.1) | collective-permute-done | bytes 131104 | tf_op jit(solution)/shard_map/ppermute | solution.py:439
  17.6 1.1 %collective-permute-done.2.gate3_ref = bf16[256,256]{1,0:T(8,128)(2,1)S(1)} collective-permute-done((bf16[256,256]{1,0:T(8,128)(2,1)S(1)}, bf16[256,256]{1,0:T(8,128)(2,1)S(1)}, u32[]{:S(2)}, u32[]{:S(2)}) %collective-permute-start.2) | collective-permute-done | bytes 131104 | tf_op jit(solution)/shard_map/ppermute | solution.py:439
  18.7 5.9 %all-to-all-done.both_ref = bf16[8,2,32,512]{3,2,1,0:T(8,128)(2,1)S(1)} async-done(((bf16[8,2,32,512]{3,2,1,0:T(8,128)(2,1)}), bf16[8,2,32,512]{3,2,1,0:T(8,128)(2,1)S(1)}, u32[]{:S(2)}, u32[]{:S(2)}) %all-to-all-start) | async-done | bytes 524320 | tf_op jit(solution)/shard_map/all_to_all | solution.py:467
  24.6 0.0 copy-done.1
  24.6 0.0 copy-done.2
  24.6 2.4 %convolve.1 = bf16[8,2,32,256]{3,2,1,0:T(8,128)(2,1)S(1)} custom-call(s32[1]{0:T(128)} %bitcast.core_ref, bf16[8,2,32,512]{3,2,1,0:T(8,128)(2,1)S(1)} %all-to-all-done.both_ref, bf16[256,512]{1,0:T(8,128)(2,1)S(1)} %copy-done.1, bf16[256,512]{1,0:T(8,128)(2,1)S(1)} %copy-done.2, bf16[512,256]{1,0:T(8,128)(2,1)} %constant.32.clone.gh_hbm, ...), custom_call_target="tpu_custom_call" | custom-call | tf_op jit(solution)/shard_map/convolve/pallas_call | solution.py:484
  27.0 12.5 %all_to_all.10 = bf16[8,2,32,256]{3,2,1,0:T(8,128)(2,1)S(1)} all-to-all(bf16[8,2,32,256]{3,2,1,0:T(8,128)(2,1)S(1)} %convolve.1), channel_id=1, replica_groups=mesh['tm'=8,'x'=2,'core'=2] {'tm'}, dimensions={0} | all-to-all | bytes 524288 | tf_op jit(solution)/shard_map/all_to_all | solution.py:498
  39.6 1.6 %collective-permute-start.3 = (bf16[8,32,256]{2,1,0:T(8,128)(2,1)S(1)}, bf16[8,32,256]{2,1,0:T(8,128)(2,1)S(1)}, u32[]{:S(2)}, u32[]{:S(2)}) collective-permute-start(bf16[8,32,256]{2,1,0:T(8,128)(2,1)S(1)} %get-tuple-element.67.conv0_ref), channel_id=1, source_target_pairs={{0,2},{1,3},{2,0},{3,1},{4,6},{5,7},{6,4},{7,5},{8,10},{9,11},{10,... | collective-permute-start | bytes 393224 | tf_op jit(solution)/shard_map/ppermute | solution.py:439
  41.1 0.0 collective-permute-start.8
  41.1 0.0 collective-permute-done.4.wg1_hbm
  41.2 0.0 collective-permute-done.5.wu1_hbm
  41.2 0.0 collective-permute-done.6.wd1_hbm
  41.2 3.0 %feed_first.1 = (bf16[256,256]{1,0:T(8,128)(2,1)S(1)}, f32[256,1]{1,0:T(8,128)S(1)}, f32[4,1,256]{2,1,0:T(1,128)S(1)}, f32[4,256,512]{2,1,0:T(8,128)S(1)}, bf16[...) custom-call(s32[1]{0:T(128)} %bitcast.1.chip_ref, s32[1]{0:T(128)} %bitcast.core_ref, ...), custom_call_target="tpu_custom_call" | custom-call | tf_op jit(solution)/shard_map/feed_first/pallas_call | solution.py:515
  44.2 0.9 %collective-permute-done.3.conv2_ref = bf16[8,32,256]{2,1,0:T(8,128)(2,1)S(1)} collective-permute-done((bf16[8,32,256]{2,1,0:T(8,128)(2,1)S(1)}, bf16[8,32,256]{2,1,0:T(8,128)(2,1)S(1)}, u32[]{:S(2)}, u32[]{:S(2)}) %collective-permute-start.3) | collective-permute-done | bytes 131104 | tf_op jit(solution)/shard_map/ppermute | solution.py:439
  45.1 0.0 collective-permute-start.7
  45.1 0.5 feed_middle.1
  45.6 1.3 %collective-permute-done.8.conv3_ref = bf16[8,32,256]{2,1,0:T(8,128)(2,1)S(1)} collective-permute-done((bf16[8,32,256]{2,1,0:T(8,128)(2,1)S(1)}, bf16[8,32,256]{2,1,0:T(8,128)(2,1)S(1)}, u32[]{:S(2)}, u32[]{:S(2)}) %collective-permute-start.8) | collective-permute-done | bytes 131104 | tf_op jit(solution)/shard_map/ppermute | solution.py:439
  46.9 0.0 collective-permute-done.7.conv1_ref
  46.9 1.3 %feed_second.1 = (bf16[256,256]{1,0:T(8,128)(2,1)S(1)}, bf16[256,1024]{1,0:T(8,128)(2,1)S(1)}, bf16[256,256]{1,0:T(8,128)(2,1)S(1)}, bf16[256,256]{1,0:T(8,128)(2,1)S(1)}) custom-call(s32[1]{0:T(128)} %bitcast.1.chip_ref, s32[1]{0:T(128)} %bitcast.core_ref, bf16[8,32,256]{2,1,0:T(8,128)(2,1)S(1)} %collective-permute-done.7.conv1_ref, ...), custom_call_target="tpu_custom_call" | custom-call | tf_op jit(solution)/shard_map/feed_second/pallas_call | solution.py:546
  48.2 1.9 %collective-permute-start.9 = (bf16[256,256]{1,0:T(8,128)(2,1)S(1)}, bf16[256,256]{1,0:T(8,128)(2,1)S(1)}, u32[]{:S(2)}, u32[]{:S(2)}) collective-permute-start(bf16[256,256]{1,0:T(8,128)(2,1)S(1)} %get-tuple-element.62), channel_id=1, source_target_pairs={{0,2},{1,3},{2,0},{3,1},{4,6},{5,7},{6,4},{7,5},{8,10},{9,11},{10,... | collective-permute-start | bytes 393224 | tf_op jit(solution)/shard_map/ppermute | solution.py:439
  50.2 0.0 collective-permute-start.11
  50.2 0.5 feed_third.1
  50.7 4.0 %collective-permute-done.9.add_ref = bf16[256,256]{1,0:T(8,128)(2,1)S(1)} collective-permute-done((bf16[256,256]{1,0:T(8,128)(2,1)S(1)}, bf16[256,256]{1,0:T(8,128)(2,1)S(1)}, u32[]{:S(2)}, u32[]{:S(2)}) %collective-permute-start.9) | collective-permute-done | bytes 131104 | tf_op jit(solution)/shard_map/ppermute | solution.py:439
  54.6 0.0 collective-permute-start.10
  54.6 0.7 %finish.2.rest_0_ = bf16[512,256]{1,0:T(8,128)(2,1)} custom-call(s32[1]{0:T(128)} %bitcast.core_ref, f32[256,256]{1,0:T(8,128)S(1)} %get-tuple-element.65.base_ref, bf16[256,256]{1,0:T(8,128)(2,1)S(1)} %collective-permute-done.9.add_ref), custom_call_target="tpu_custom_call" | custom-call | tf_op jit(solution)/shard_map/finish/pallas_call | solution.py:388
  55.3 0.9 %collective-permute-done.11.add_ref = bf16[256,256]{1,0:T(8,128)(2,1)S(1)} collective-permute-done((bf16[256,256]{1,0:T(8,128)(2,1)S(1)}, bf16[256,256]{1,0:T(8,128)(2,1)S(1)}, u32[]{:S(2)}, u32[]{:S(2)}) %collective-permute-start.11) | collective-permute-done | bytes 131104 | tf_op jit(solution)/shard_map/ppermute | solution.py:439
  56.2 0.0 collective-permute-done.10.base_ref
  56.2 0.7 %finish.3 = bf16[512,256]{1,0:T(8,128)(2,1)} custom-call(s32[1]{0:T(128)} %bitcast.core_ref, bf16[256,256]{1,0:T(8,128)(2,1)S(1)} %collective-permute-done.10.base_ref, bf16[256,256]{1,0:T(8,128)(2,1)S(1)} %collective-permute-done.11.add_ref, bf16[512,256]{1,0:T(8,128)(2,1)} %finish.2.rest_0_), custom_call_target="tpu_custom_call", output_to_operand_aliasing={{}: (3, {})} | custom-call | tf_op jit(solution)/shard_map/finish/pallas_call | solution.py:388
  (2 shorter events, 0.0 us)
Async XLA Ops:
  0.0 12.8 %copy-start = (f32[256]{0:T(256)S(1)}, f32[256]{0:T(256)}, u32[]{:S(2)}) copy-start(f32[256]{0:T(256)} %param.23) | copy-start | bytes 3076
  0.0 24.6 %copy-start.1 = (bf16[256,512]{1,0:T(8,128)(2,1)S(1)}, bf16[256,512]{1,0:T(8,128)(2,1)}, u32[]{:S(2)}) copy-start(bf16[256,512]{1,0:T(8,128)(2,1)} %constant.30.clone.fh_ref) | copy-start | bytes 786436
  0.0 24.6 %copy-start.2 = (bf16[256,512]{1,0:T(8,128)(2,1)S(1)}, bf16[256,512]{1,0:T(8,128)(2,1)}, u32[]{:S(2)}) copy-start(bf16[256,512]{1,0:T(8,128)(2,1)} %constant.31.clone.fl_ref) | copy-start | bytes 786436
  0.0 10.1 %copy-start.4 = (bf16[512,256]{1,0:T(8,128)(2,1)S(1)}, bf16[512,256]{1,0:T(8,128)(2,1)}, u32[]{:S(2)}) copy-start(bf16[512,256]{1,0:T(8,128)(2,1)} %param.17) | copy-start | bytes 786436
  0.0 10.2 %copy-start.3 = (bf16[1024,512]{1,0:T(8,128)(2,1)S(1)}, bf16[1024,512]{1,0:T(8,128)(2,1)}, u32[]{:S(2)}) copy-start(bf16[1024,512]{1,0:T(8,128)(2,1)} %wg0_hbm.1) | copy-start | bytes 3145732
  2.8 21.8 %all-to-all-start = ((bf16[8,2,32,512]{3,2,1,0:T(8,128)(2,1)}), bf16[8,2,32,512]{3,2,1,0:T(8,128)(2,1)S(1)}, u32[]{:S(2)}, u32[]{:S(2)}) async-start(bf16[8,2,32,512]{3,2,1,0:T(8,128)(2,1)} %prepare.1), calls=%async_computation | async-start | bytes 1048576 | tf_op jit(solution)/shard_map/all_to_all | solution.py:467
  10.2 2.6 %collective-permute-start = (bf16[256,256]{1,0:T(8,128)(2,1)S(1)}, bf16[256,256]{1,0:T(8,128)(2,1)S(1)}, u32[]{:S(2)}, u32[]{:S(2)}) collective-permute-start(bf16[256,256]{1,0:T(8,128)(2,1)S(1)} %get-tuple-element.69), channel_id=1, source_target_pairs={{0,1},{1,0},{2,3},{3,2},{4,5},{5,4},{6,7},{7,6},{8,9},{9,8},{10,11... | collective-permute-start | bytes 393224 | tf_op jit(solution)/shard_map/ppermute | solution.py:439
  10.2 30.9 %collective-permute-start.4 = (bf16[1024,512]{1,0:T(8,128)(2,1)S(1)}, bf16[1024,512]{1,0:T(8,128)(2,1)}, u32[]{:S(2)}, u32[]{:S(2)}) collective-permute-start(bf16[1024,512]{1,0:T(8,128)(2,1)S(1)} %copy-done.3), channel_id=1, source_target_pairs={{0,1},{1,0},{2,3},{3,2},{4,5},{5,4},{6,7},{7,6},{8,9},{9,8},{10,11... | collective-permute-start | bytes 3145736 | tf_op jit(solution)/shard_map/ppermute | solution.py:439
  10.7 30.4 %collective-permute-start.5 = (bf16[1024,512]{1,0:T(8,128)(2,1)}, bf16[1024,512]{1,0:T(8,128)(2,1)}, u32[]{:S(2)}, u32[]{:S(2)}) collective-permute-start(bf16[1024,512]{1,0:T(8,128)(2,1)} %wu0_hbm.1), channel_id=1, source_target_pairs={{0,1},{1,0},{2,3},{3,2},{4,5},{5,4},{6,7},{7,6},{8,9},{9,8},{10,11... | collective-permute-start | bytes 3145736 | tf_op jit(solution)/shard_map/ppermute | solution.py:439
  10.8 30.3 %collective-permute-start.6 = (bf16[512,1024]{1,0:T(8,128)(2,1)}, bf16[512,1024]{1,0:T(8,128)(2,1)}, u32[]{:S(2)}, u32[]{:S(2)}) collective-permute-start(bf16[512,1024]{1,0:T(8,128)(2,1)} %wd0_hbm.1), channel_id=1, source_target_pairs={{0,1},{1,0},{2,3},{3,2},{4,5},{5,4},{6,7},{7,6},{8,9},{9,8},{10,11... | collective-permute-start | bytes 3145736 | tf_op jit(solution)/shard_map/ppermute | solution.py:439
  11.2 6.4 %collective-permute-start.1 = (bf16[256,256]{1,0:T(8,128)(2,1)S(1)}, bf16[256,256]{1,0:T(8,128)(2,1)S(1)}, u32[]{:S(2)}, u32[]{:S(2)}) collective-permute-start(bf16[256,256]{1,0:T(8,128)(2,1)S(1)} %get-tuple-element.37.gate0_ref), channel_id=1, source_target_pairs={{0,2},{1,3},{2,0},{3,1},{4,6},{5,7},{6,4},{7,5},{8,10},{9,11},{10,... | collective-permute-start | bytes 393224 | tf_op jit(solution)/shard_map/ppermute | solution.py:439
  12.7 5.9 %collective-permute-start.2 = (bf16[256,256]{1,0:T(8,128)(2,1)S(1)}, bf16[256,256]{1,0:T(8,128)(2,1)S(1)}, u32[]{:S(2)}, u32[]{:S(2)}) collective-permute-start(bf16[256,256]{1,0:T(8,128)(2,1)S(1)} %get-tuple-element.69), channel_id=1, source_target_pairs={{0,3},{1,2},{2,1},{3,0},{4,7},{5,6},{6,5},{7,4},{8,11},{9,10},{10,... | collective-permute-start | bytes 393224 | tf_op jit(solution)/shard_map/ppermute | solution.py:439
  39.6 5.5 %collective-permute-start.3 = (bf16[8,32,256]{2,1,0:T(8,128)(2,1)S(1)}, bf16[8,32,256]{2,1,0:T(8,128)(2,1)S(1)}, u32[]{:S(2)}, u32[]{:S(2)}) collective-permute-start(bf16[8,32,256]{2,1,0:T(8,128)(2,1)S(1)} %get-tuple-element.67.conv0_ref), channel_id=1, source_target_pairs={{0,2},{1,3},{2,0},{3,1},{4,6},{5,7},{6,4},{7,5},{8,10},{9,11},{10,... | collective-permute-start | bytes 393224 | tf_op jit(solution)/shard_map/ppermute | solution.py:439
  41.1 5.8 %collective-permute-start.8 = (bf16[8,32,256]{2,1,0:T(8,128)(2,1)S(1)}, bf16[8,32,256]{2,1,0:T(8,128)(2,1)S(1)}, u32[]{:S(2)}, u32[]{:S(2)}) collective-permute-start(bf16[8,32,256]{2,1,0:T(8,128)(2,1)S(1)} %get-tuple-element.45), channel_id=1, source_target_pairs={{0,3},{1,2},{2,1},{3,0},{4,7},{5,6},{6,5},{7,4},{8,11},{9,10},{10,... | collective-permute-start | bytes 393224 | tf_op jit(solution)/shard_map/ppermute | solution.py:439
  45.1 1.8 %collective-permute-start.7 = (bf16[8,32,256]{2,1,0:T(8,128)(2,1)S(1)}, bf16[8,32,256]{2,1,0:T(8,128)(2,1)S(1)}, u32[]{:S(2)}, u32[]{:S(2)}) collective-permute-start(bf16[8,32,256]{2,1,0:T(8,128)(2,1)S(1)} %get-tuple-element.45), channel_id=1, source_target_pairs={{0,1},{1,0},{2,3},{3,2},{4,5},{5,4},{6,7},{7,6},{8,9},{9,8},{10,11... | collective-permute-start | bytes 393224 | tf_op jit(solution)/shard_map/ppermute | solution.py:439
  48.2 6.4 %collective-permute-start.9 = (bf16[256,256]{1,0:T(8,128)(2,1)S(1)}, bf16[256,256]{1,0:T(8,128)(2,1)S(1)}, u32[]{:S(2)}, u32[]{:S(2)}) collective-permute-start(bf16[256,256]{1,0:T(8,128)(2,1)S(1)} %get-tuple-element.62), channel_id=1, source_target_pairs={{0,2},{1,3},{2,0},{3,1},{4,6},{5,7},{6,4},{7,5},{8,10},{9,11},{10,... | collective-permute-start | bytes 393224 | tf_op jit(solution)/shard_map/ppermute | solution.py:439
  50.2 6.0 %collective-permute-start.11 = (bf16[256,256]{1,0:T(8,128)(2,1)S(1)}, bf16[256,256]{1,0:T(8,128)(2,1)S(1)}, u32[]{:S(2)}, u32[]{:S(2)}) collective-permute-start(bf16[256,256]{1,0:T(8,128)(2,1)S(1)} %get-tuple-element.64), channel_id=1, source_target_pairs={{0,3},{1,2},{2,1},{3,0},{4,7},{5,6},{6,5},{7,4},{8,11},{9,10},{10,... | collective-permute-start | bytes 393224 | tf_op jit(solution)/shard_map/ppermute | solution.py:439
  54.6 1.6 %collective-permute-start.10 = (bf16[256,256]{1,0:T(8,128)(2,1)S(1)}, bf16[256,256]{1,0:T(8,128)(2,1)S(1)}, u32[]{:S(2)}, u32[]{:S(2)}) collective-permute-start(bf16[256,256]{1,0:T(8,128)(2,1)S(1)} %get-tuple-element.63), channel_id=1, source_target_pairs={{0,1},{1,0},{2,3},{3,2},{4,5},{5,4},{6,7},{7,6},{8,9},{9,8},{10,11... | collective-permute-start | bytes 393224 | tf_op jit(solution)/shard_map/ppermute | solution.py:439

commit v11 on v10

--- a/solution.py
+++ b/solution.py
@@ -200,13 +200,14 @@
     for load in loads:
         load.wait()
     skip = skip_ref[...]
+    spec = z_ref[...].reshape(nb * chans, 2 * block)
+    high = spec.astype(bf16)
+    low = (spec - high.astype(f32)).astype(bf16)
+    conv = dot(high, gh_ref[...]) + dot(low, gh_ref[...]) + dot(high, gl_ref[...])
+    conv = conv.reshape(tm, 2, chans, block)
     for part in range(2):
-        spec = z_ref[:, part].reshape(tm * chans, 2 * block)
-        high = spec.astype(bf16)
-        low = (spec - high.astype(f32)).astype(bf16)
-        conv = dot(high, gh_ref[...]) + dot(low, gh_ref[...]) + dot(high, gl_ref[...])
         inputs = both_ref[:, 0, :, part * block : (part + 1) * block].astype(f32)
-        total = conv.reshape(tm, chans, block) + skip[None] * inputs
+        total = conv[:, part] + skip[None] * inputs
         out_ref[:, part ^ core_ref[0]] = total.astype(bf16)
 
 

time: 57.2 us -> 57.2 us (level)
  no operation moved by 1% of the time
where the time goes in v11:
time: 57.2 us; the launch traced here: 56.9 us
  waiting for transfers between devices  18.8 us (33%)
  starting transfers between devices  13.5 us (24%)
  blocking collectives  12.5 us (22%)
  Pallas kernels  11 us (19%)
  between operations  0.9 us (2%)
    ppermute x12, waiting for transfers between devices, swap(): lax.ppermute(values, ('x', 'core'), [(at, at ^ bits) for at in range(4)])  12.8 us
    all_to_all x1, blocking collectives, shards(): conv = lax.all_to_all(conv, 'tm', split_axis=0, concat_axis=0, tiled=True)  12.5 us
    all_to_all x1, starting transfers between devices, shards(): both = lax.all_to_all(made, 'tm', split_axis=0, concat_axis=0, tiled=True)  7.3 us
    ppermute x12, starting transfers between devices, swap(): lax.ppermute(values, ('x', 'core'), [(at, at ^ bits) for at in range(4)])  6.17 us
    all_to_all x1, waiting for transfers between devices, shards(): both = lax.all_to_all(made, 'tm', split_axis=0, concat_axis=0, tiled=True)  5.93 us
    pallas_call x1, Pallas kernels, shards(): pl.pallas_call(feed_first_kernel, out_shape=[jax.ShapeDtypeStruct(*spec)...  3 us
    pallas_call x1, Pallas kernels, shards(): pl.pallas_call(convolve_kernel, out_shape=jax.ShapeDtypeStruct((tm, 2, he...  2.42 us
    pallas_call x1, Pallas kernels, shards(): pl.pallas_call(prepare_kernel, out_shape=jax.ShapeDtypeStruct(shape, bf16...  2.01 us
  transfers between devices with their start and end apart: 13, of which 7 were waited for; matrix products, arithmetic and copies ran while one was open for 0% of the time, Pallas kernels for 12%

profile of v11, /device:TPU:0, one launch (start us, length us, event | category | flops | bytes accessed | tf_op | source)
XLA Modules:
  0.0 56.9 jit_solution(11057259477350562440)
XLA Ops:
  0.0 0.0 copy-start
  0.0 0.0 copy-start.1
  0.0 0.0 copy-start.2
  0.0 0.0 copy-start.4
  0.0 0.0 copy-start.3
  0.8 2.0 %prepare.1 = bf16[8,2,32,512]{3,2,1,0:T(8,128)(2,1)} custom-call(s32[1]{0:T(128)S(6)} %copy.26.step_ref, s32[8]{0:T(128)} %flags_hbm.1, bf16[512,256]{1,0:T(8,128)(2,1)} %value_hbm.1, bf16[512,256]{1,0:T(8,128)(2,1)} %filter_hbm.1, f32[200,256]{1,0:T(8,128)} %table_hbm.1, f32[1,256]{1,0:T(1,128)} %bitcast.15), custom_call_target="tpu_custom_call" | custom-call | tf_op jit(solution)/shard_map/prepare/pallas_call | solution.py:444
  2.8 7.3 %all-to-all-start = ((bf16[8,2,32,512]{3,2,1,0:T(8,128)(2,1)}), bf16[8,2,32,512]{3,2,1,0:T(8,128)(2,1)S(1)}, u32[]{:S(2)}, u32[]{:S(2)}) async-start(bf16[8,2,32,512]{3,2,1,0:T(8,128)(2,1)} %prepare.1), calls=%async_computation | async-start | bytes 1048576 | tf_op jit(solution)/shard_map/all_to_all | solution.py:468
  10.1 0.0 copy-done.4
  10.2 0.1 collective-permute-start
  10.2 0.0 copy-done.3
  10.2 0.5 collective-permute-start.4
  10.7 0.1 collective-permute-start.5
  10.8 0.4 collective-permute-start.6
  11.2 1.5 %collective-permute-start.1 = (bf16[256,256]{1,0:T(8,128)(2,1)S(1)}, bf16[256,256]{1,0:T(8,128)(2,1)S(1)}, u32[]{:S(2)}, u32[]{:S(2)}) collective-permute-start(bf16[256,256]{1,0:T(8,128)(2,1)S(1)} %get-tuple-element.37.gate0_ref), channel_id=1, source_target_pairs={{0,2},{1,3},{2,0},{3,1},{4,6},{5,7},{6,4},{7,5},{8,10},{9,11},{10,... | collective-permute-start | bytes 393224 | tf_op jit(solution)/shard_map/ppermute | solution.py:440
  12.7 0.0 collective-permute-done.gate1_ref
  12.7 0.1 collective-permute-start.2
  12.8 0.0 copy-done
  12.8 0.1 dynamic-slice_bitcast_fusion
  12.9 0.1 copy.20.skip_ref
  13.0 4.6 %collective-permute-done.1.gate2_ref = bf16[256,256]{1,0:T(8,128)(2,1)S(1)} collective-permute-done((bf16[256,256]{1,0:T(8,128)(2,1)S(1)}, bf16[256,256]{1,0:T(8,128)(2,1)S(1)}, u32[]{:S(2)}, u32[]{:S(2)}) %collective-permute-start.1) | collective-permute-done | bytes 131104 | tf_op jit(solution)/shard_map/ppermute | solution.py:440
  17.6 1.1 %collective-permute-done.2.gate3_ref = bf16[256,256]{1,0:T(8,128)(2,1)S(1)} collective-permute-done((bf16[256,256]{1,0:T(8,128)(2,1)S(1)}, bf16[256,256]{1,0:T(8,128)(2,1)S(1)}, u32[]{:S(2)}, u32[]{:S(2)}) %collective-permute-start.2) | collective-permute-done | bytes 131104 | tf_op jit(solution)/shard_map/ppermute | solution.py:440
  18.7 5.9 %all-to-all-done.both_ref = bf16[8,2,32,512]{3,2,1,0:T(8,128)(2,1)S(1)} async-done(((bf16[8,2,32,512]{3,2,1,0:T(8,128)(2,1)}), bf16[8,2,32,512]{3,2,1,0:T(8,128)(2,1)S(1)}, u32[]{:S(2)}, u32[]{:S(2)}) %all-to-all-start) | async-done | bytes 524320 | tf_op jit(solution)/shard_map/all_to_all | solution.py:468
  24.6 0.0 copy-done.1
  24.6 0.0 copy-done.2
  24.6 2.4 %convolve.1 = bf16[8,2,32,256]{3,2,1,0:T(8,128)(2,1)S(1)} custom-call(s32[1]{0:T(128)} %bitcast.core_ref, bf16[8,2,32,512]{3,2,1,0:T(8,128)(2,1)S(1)} %all-to-all-done.both_ref, bf16[256,512]{1,0:T(8,128)(2,1)S(1)} %copy-done.1, bf16[256,512]{1,0:T(8,128)(2,1)S(1)} %copy-done.2, bf16[512,256]{1,0:T(8,128)(2,1)} %constant.32.clone.gh_hbm, ...), custom_call_target="tpu_custom_call" | custom-call | tf_op jit(solution)/shard_map/convolve/pallas_call | solution.py:485
  27.0 12.5 %all_to_all.10 = bf16[8,2,32,256]{3,2,1,0:T(8,128)(2,1)S(1)} all-to-all(bf16[8,2,32,256]{3,2,1,0:T(8,128)(2,1)S(1)} %convolve.1), channel_id=1, replica_groups=mesh['tm'=8,'x'=2,'core'=2] {'tm'}, dimensions={0} | all-to-all | bytes 524288 | tf_op jit(solution)/shard_map/all_to_all | solution.py:499
  39.6 1.6 %collective-permute-start.3 = (bf16[8,32,256]{2,1,0:T(8,128)(2,1)S(1)}, bf16[8,32,256]{2,1,0:T(8,128)(2,1)S(1)}, u32[]{:S(2)}, u32[]{:S(2)}) collective-permute-start(bf16[8,32,256]{2,1,0:T(8,128)(2,1)S(1)} %get-tuple-element.67.conv0_ref), channel_id=1, source_target_pairs={{0,2},{1,3},{2,0},{3,1},{4,6},{5,7},{6,4},{7,5},{8,10},{9,11},{10,... | collective-permute-start | bytes 393224 | tf_op jit(solution)/shard_map/ppermute | solution.py:440
  41.2 0.0 collective-permute-start.8
  41.2 0.0 collective-permute-done.4.wg1_hbm
  41.2 0.0 collective-permute-done.5.wu1_hbm
  41.2 0.0 collective-permute-done.6.wd1_hbm
  41.2 3.0 %feed_first.1 = (bf16[256,256]{1,0:T(8,128)(2,1)S(1)}, f32[256,1]{1,0:T(8,128)S(1)}, f32[4,1,256]{2,1,0:T(1,128)S(1)}, f32[4,256,512]{2,1,0:T(8,128)S(1)}, bf16[...) custom-call(s32[1]{0:T(128)} %bitcast.1.chip_ref, s32[1]{0:T(128)} %bitcast.core_ref, ...), custom_call_target="tpu_custom_call" | custom-call | tf_op jit(solution)/shard_map/feed_first/pallas_call | solution.py:516
  44.2 0.9 %collective-permute-done.3.conv2_ref = bf16[8,32,256]{2,1,0:T(8,128)(2,1)S(1)} collective-permute-done((bf16[8,32,256]{2,1,0:T(8,128)(2,1)S(1)}, bf16[8,32,256]{2,1,0:T(8,128)(2,1)S(1)}, u32[]{:S(2)}, u32[]{:S(2)}) %collective-permute-start.3) | collective-permute-done | bytes 131104 | tf_op jit(solution)/shard_map/ppermute | solution.py:440
  45.1 0.0 collective-permute-start.7
  45.1 0.5 feed_middle.1
  45.6 1.3 %collective-permute-done.8.conv3_ref = bf16[8,32,256]{2,1,0:T(8,128)(2,1)S(1)} collective-permute-done((bf16[8,32,256]{2,1,0:T(8,128)(2,1)S(1)}, bf16[8,32,256]{2,1,0:T(8,128)(2,1)S(1)}, u32[]{:S(2)}, u32[]{:S(2)}) %collective-permute-start.8) | collective-permute-done | bytes 131104 | tf_op jit(solution)/shard_map/ppermute | solution.py:440
  46.9 0.0 collective-permute-done.7.conv1_ref
  46.9 1.3 %feed_second.1 = (bf16[256,256]{1,0:T(8,128)(2,1)S(1)}, bf16[256,1024]{1,0:T(8,128)(2,1)S(1)}, bf16[256,256]{1,0:T(8,128)(2,1)S(1)}, bf16[256,256]{1,0:T(8,128)(2,1)S(1)}) custom-call(s32[1]{0:T(128)} %bitcast.1.chip_ref, s32[1]{0:T(128)} %bitcast.core_ref, bf16[8,32,256]{2,1,0:T(8,128)(2,1)S(1)} %collective-permute-done.7.conv1_ref, ...), custom_call_target="tpu_custom_call" | custom-call | tf_op jit(solution)/shard_map/feed_second/pallas_call | solution.py:547
  48.2 2.0 %collective-permute-start.9 = (bf16[256,256]{1,0:T(8,128)(2,1)S(1)}, bf16[256,256]{1,0:T(8,128)(2,1)S(1)}, u32[]{:S(2)}, u32[]{:S(2)}) collective-permute-start(bf16[256,256]{1,0:T(8,128)(2,1)S(1)} %get-tuple-element.62), channel_id=1, source_target_pairs={{0,2},{1,3},{2,0},{3,1},{4,6},{5,7},{6,4},{7,5},{8,10},{9,11},{10,... | collective-permute-start | bytes 393224 | tf_op jit(solution)/shard_map/ppermute | solution.py:440
  50.2 0.0 collective-permute-start.11
  50.2 0.5 feed_third.1
  50.7 3.9 %collective-permute-done.9.add_ref = bf16[256,256]{1,0:T(8,128)(2,1)S(1)} collective-permute-done((bf16[256,256]{1,0:T(8,128)(2,1)S(1)}, bf16[256,256]{1,0:T(8,128)(2,1)S(1)}, u32[]{:S(2)}, u32[]{:S(2)}) %collective-permute-start.9) | collective-permute-done | bytes 131104 | tf_op jit(solution)/shard_map/ppermute | solution.py:440
  54.6 0.0 collective-permute-start.10
  54.6 0.7 %finish.2.rest_0_ = bf16[512,256]{1,0:T(8,128)(2,1)} custom-call(s32[1]{0:T(128)} %bitcast.core_ref, f32[256,256]{1,0:T(8,128)S(1)} %get-tuple-element.65.base_ref, bf16[256,256]{1,0:T(8,128)(2,1)S(1)} %collective-permute-done.9.add_ref), custom_call_target="tpu_custom_call" | custom-call | tf_op jit(solution)/shard_map/finish/pallas_call | solution.py:389
  55.3 0.9 %collective-permute-done.11.add_ref = bf16[256,256]{1,0:T(8,128)(2,1)S(1)} collective-permute-done((bf16[256,256]{1,0:T(8,128)(2,1)S(1)}, bf16[256,256]{1,0:T(8,128)(2,1)S(1)}, u32[]{:S(2)}, u32[]{:S(2)}) %collective-permute-start.11) | collective-permute-done | bytes 131104 | tf_op jit(solution)/shard_map/ppermute | solution.py:440
  56.2 0.0 collective-permute-done.10.base_ref
  56.2 0.7 %finish.3 = bf16[512,256]{1,0:T(8,128)(2,1)} custom-call(s32[1]{0:T(128)} %bitcast.core_ref, bf16[256,256]{1,0:T(8,128)(2,1)S(1)} %collective-permute-done.10.base_ref, bf16[256,256]{1,0:T(8,128)(2,1)S(1)} %collective-permute-done.11.add_ref, bf16[512,256]{1,0:T(8,128)(2,1)} %finish.2.rest_0_), custom_call_target="tpu_custom_call", output_to_operand_aliasing={{}: (3, {})} | custom-call | tf_op jit(solution)/shard_map/finish/pallas_call | solution.py:389
  (2 shorter events, 0.0 us)
Async XLA Ops:
  0.0 12.8 %copy-start = (f32[256]{0:T(256)S(1)}, f32[256]{0:T(256)}, u32[]{:S(2)}) copy-start(f32[256]{0:T(256)} %param.23) | copy-start | bytes 3076
  0.0 24.6 %copy-start.1 = (bf16[256,512]{1,0:T(8,128)(2,1)S(1)}, bf16[256,512]{1,0:T(8,128)(2,1)}, u32[]{:S(2)}) copy-start(bf16[256,512]{1,0:T(8,128)(2,1)} %constant.30.clone.fh_ref) | copy-start | bytes 786436
  0.0 24.6 %copy-start.2 = (bf16[256,512]{1,0:T(8,128)(2,1)S(1)}, bf16[256,512]{1,0:T(8,128)(2,1)}, u32[]{:S(2)}) copy-start(bf16[256,512]{1,0:T(8,128)(2,1)} %constant.31.clone.fl_ref) | copy-start | bytes 786436
  0.0 10.1 %copy-start.4 = (bf16[512,256]{1,0:T(8,128)(2,1)S(1)}, bf16[512,256]{1,0:T(8,128)(2,1)}, u32[]{:S(2)}) copy-start(bf16[512,256]{1,0:T(8,128)(2,1)} %param.17) | copy-start | bytes 786436
  0.0 10.2 %copy-start.3 = (bf16[1024,512]{1,0:T(8,128)(2,1)S(1)}, bf16[1024,512]{1,0:T(8,128)(2,1)}, u32[]{:S(2)}) copy-start(bf16[1024,512]{1,0:T(8,128)(2,1)} %wg0_hbm.1) | copy-start | bytes 3145732
  2.8 21.8 %all-to-all-start = ((bf16[8,2,32,512]{3,2,1,0:T(8,128)(2,1)}), bf16[8,2,32,512]{3,2,1,0:T(8,128)(2,1)S(1)}, u32[]{:S(2)}, u32[]{:S(2)}) async-start(bf16[8,2,32,512]{3,2,1,0:T(8,128)(2,1)} %prepare.1), calls=%async_computation | async-start | bytes 1048576 | tf_op jit(solution)/shard_map/all_to_all | solution.py:468
  10.2 2.6 %collective-permute-start = (bf16[256,256]{1,0:T(8,128)(2,1)S(1)}, bf16[256,256]{1,0:T(8,128)(2,1)S(1)}, u32[]{:S(2)}, u32[]{:S(2)}) collective-permute-start(bf16[256,256]{1,0:T(8,128)(2,1)S(1)} %get-tuple-element.69), channel_id=1, source_target_pairs={{0,1},{1,0},{2,3},{3,2},{4,5},{5,4},{6,7},{7,6},{8,9},{9,8},{10,11... | collective-permute-start | bytes 393224 | tf_op jit(solution)/shard_map/ppermute | solution.py:440
  10.2 30.9 %collective-permute-start.4 = (bf16[1024,512]{1,0:T(8,128)(2,1)S(1)}, bf16[1024,512]{1,0:T(8,128)(2,1)}, u32[]{:S(2)}, u32[]{:S(2)}) collective-permute-start(bf16[1024,512]{1,0:T(8,128)(2,1)S(1)} %copy-done.3), channel_id=1, source_target_pairs={{0,1},{1,0},{2,3},{3,2},{4,5},{5,4},{6,7},{7,6},{8,9},{9,8},{10,11... | collective-permute-start | bytes 3145736 | tf_op jit(solution)/shard_map/ppermute | solution.py:440
  10.7 30.4 %collective-permute-start.5 = (bf16[1024,512]{1,0:T(8,128)(2,1)}, bf16[1024,512]{1,0:T(8,128)(2,1)}, u32[]{:S(2)}, u32[]{:S(2)}) collective-permute-start(bf16[1024,512]{1,0:T(8,128)(2,1)} %wu0_hbm.1), channel_id=1, source_target_pairs={{0,1},{1,0},{2,3},{3,2},{4,5},{5,4},{6,7},{7,6},{8,9},{9,8},{10,11... | collective-permute-start | bytes 3145736 | tf_op jit(solution)/shard_map/ppermute | solution.py:440
  10.8 30.3 %collective-permute-start.6 = (bf16[512,1024]{1,0:T(8,128)(2,1)}, bf16[512,1024]{1,0:T(8,128)(2,1)}, u32[]{:S(2)}, u32[]{:S(2)}) collective-permute-start(bf16[512,1024]{1,0:T(8,128)(2,1)} %wd0_hbm.1), channel_id=1, source_target_pairs={{0,1},{1,0},{2,3},{3,2},{4,5},{5,4},{6,7},{7,6},{8,9},{9,8},{10,11... | collective-permute-start | bytes 3145736 | tf_op jit(solution)/shard_map/ppermute | solution.py:440
  11.2 6.4 %collective-permute-start.1 = (bf16[256,256]{1,0:T(8,128)(2,1)S(1)}, bf16[256,256]{1,0:T(8,128)(2,1)S(1)}, u32[]{:S(2)}, u32[]{:S(2)}) collective-permute-start(bf16[256,256]{1,0:T(8,128)(2,1)S(1)} %get-tuple-element.37.gate0_ref), channel_id=1, source_target_pairs={{0,2},{1,3},{2,0},{3,1},{4,6},{5,7},{6,4},{7,5},{8,10},{9,11},{10,... | collective-permute-start | bytes 393224 | tf_op jit(solution)/shard_map/ppermute | solution.py:440
  12.7 5.9 %collective-permute-start.2 = (bf16[256,256]{1,0:T(8,128)(2,1)S(1)}, bf16[256,256]{1,0:T(8,128)(2,1)S(1)}, u32[]{:S(2)}, u32[]{:S(2)}) collective-permute-start(bf16[256,256]{1,0:T(8,128)(2,1)S(1)} %get-tuple-element.69), channel_id=1, source_target_pairs={{0,3},{1,2},{2,1},{3,0},{4,7},{5,6},{6,5},{7,4},{8,11},{9,10},{10,... | collective-permute-start | bytes 393224 | tf_op jit(solution)/shard_map/ppermute | solution.py:440
  39.6 5.5 %collective-permute-start.3 = (bf16[8,32,256]{2,1,0:T(8,128)(2,1)S(1)}, bf16[8,32,256]{2,1,0:T(8,128)(2,1)S(1)}, u32[]{:S(2)}, u32[]{:S(2)}) collective-permute-start(bf16[8,32,256]{2,1,0:T(8,128)(2,1)S(1)} %get-tuple-element.67.conv0_ref), channel_id=1, source_target_pairs={{0,2},{1,3},{2,0},{3,1},{4,6},{5,7},{6,4},{7,5},{8,10},{9,11},{10,... | collective-permute-start | bytes 393224 | tf_op jit(solution)/shard_map/ppermute | solution.py:440
  41.2 5.8 %collective-permute-start.8 = (bf16[8,32,256]{2,1,0:T(8,128)(2,1)S(1)}, bf16[8,32,256]{2,1,0:T(8,128)(2,1)S(1)}, u32[]{:S(2)}, u32[]{:S(2)}) collective-permute-start(bf16[8,32,256]{2,1,0:T(8,128)(2,1)S(1)} %get-tuple-element.45), channel_id=1, source_target_pairs={{0,3},{1,2},{2,1},{3,0},{4,7},{5,6},{6,5},{7,4},{8,11},{9,10},{10,... | collective-permute-start | bytes 393224 | tf_op jit(solution)/shard_map/ppermute | solution.py:440
  45.1 1.8 %collective-permute-start.7 = (bf16[8,32,256]{2,1,0:T(8,128)(2,1)S(1)}, bf16[8,32,256]{2,1,0:T(8,128)(2,1)S(1)}, u32[]{:S(2)}, u32[]{:S(2)}) collective-permute-start(bf16[8,32,256]{2,1,0:T(8,128)(2,1)S(1)} %get-tuple-element.45), channel_id=1, source_target_pairs={{0,1},{1,0},{2,3},{3,2},{4,5},{5,4},{6,7},{7,6},{8,9},{9,8},{10,11... | collective-permute-start | bytes 393224 | tf_op jit(solution)/shard_map/ppermute | solution.py:440
  48.2 6.4 %collective-permute-start.9 = (bf16[256,256]{1,0:T(8,128)(2,1)S(1)}, bf16[256,256]{1,0:T(8,128)(2,1)S(1)}, u32[]{:S(2)}, u32[]{:S(2)}) collective-permute-start(bf16[256,256]{1,0:T(8,128)(2,1)S(1)} %get-tuple-element.62), channel_id=1, source_target_pairs={{0,2},{1,3},{2,0},{3,1},{4,6},{5,7},{6,4},{7,5},{8,10},{9,11},{10,... | collective-permute-start | bytes 393224 | tf_op jit(solution)/shard_map/ppermute | solution.py:440
  50.2 6.0 %collective-permute-start.11 = (bf16[256,256]{1,0:T(8,128)(2,1)S(1)}, bf16[256,256]{1,0:T(8,128)(2,1)S(1)}, u32[]{:S(2)}, u32[]{:S(2)}) collective-permute-start(bf16[256,256]{1,0:T(8,128)(2,1)S(1)} %get-tuple-element.64), channel_id=1, source_target_pairs={{0,3},{1,2},{2,1},{3,0},{4,7},{5,6},{6,5},{7,4},{8,11},{9,10},{10,... | collective-permute-start | bytes 393224 | tf_op jit(solution)/shard_map/ppermute | solution.py:440
  54.6 1.6 %collective-permute-start.10 = (bf16[256,256]{1,0:T(8,128)(2,1)S(1)}, bf16[256,256]{1,0:T(8,128)(2,1)S(1)}, u32[]{:S(2)}, u32[]{:S(2)}) collective-permute-start(bf16[256,256]{1,0:T(8,128)(2,1)S(1)} %get-tuple-element.63), channel_id=1, source_target_pairs={{0,1},{1,0},{2,3},{3,2},{4,5},{5,4},{6,7},{7,6},{8,9},{9,8},{10,11... | collective-permute-start | bytes 393224 | tf_op jit(solution)/shard_map/ppermute | solution.py:440
